TPU v7x, 1024 devices: a whole 4x4x32 slice. The times are simulated.
1024 devices in a mesh: stretch: 8 (over z_hi, y), head: 2 (over core), blk: 64 (over z_lo, x).
Axes of the slice: x: 4, y: 4, z: 32 (z_hi: 2, z_lo: 16; z = z_hi * 16 + z_lo), core: 2. Of those that a mesh axis runs over, the one named last changes fastest.
Arguments:
- queries: bfloat16 [65536, 3072], P(('stretch', 'blk'), 'head'), may hold values from -200 to 200
- keys: bfloat16 [65536, 512], P(('stretch', 'blk'), 'head'), may hold values from -6 to 6
- values: bfloat16 [65536, 512], P(('stretch', 'blk'), 'head'), may hold values from -24 to 24
- key_norm_gain: float32 [512], P('head'), may hold values from 0.5 to 4
- stretch_ids: int32 [8, 64], P('stretch', 'blk'), may hold values from 0 to 15, never falling along the last dimension, each value on 1 to 8 neighbouring positions
- clean_flags: int32 [8, 64], P('stretch', 'blk'), may hold values 0 or 1
- positions: int32 [8, 64], P('stretch', 'blk'), may hold values from 0 to 2047
Outputs:
- attended: bfloat16 [65536, 3072], P(('stretch', 'blk'), 'head')
Inputs may be any that keep to these rules, and one draw needn't show every extreme that they name: `stretch_ids`: stretch numbers start at 0 in each group of 64 blocks and never fall within it; each stretch has 1 to 8 blocks and one stretch of each group has exactly 8.
All inputs are finite; a program needn't handle non-finite values. No bound on the sum of `clean_flags` on one device may be relied on, other than what follows from the above.
Results may differ from a plain program's by a relative error of at most 0.017.
The roundings to bfloat16 on the way count: a program that leaves them out, or rounds other values in their place, can miss the bound.
Values may be sent and summed in bfloat16 or wider, within the bound.
No kernel may reach another device: no remote copies, remote signals or barrier semaphores. Data moves between devices by JAX's collectives and lax.ppermute only.
A program may use at most 32 MiB of HBM per device.

v0:
```python
import math

import jax
import jax.numpy as jnp
from jax import lax
from jax.sharding import PartitionSpec as P

HEAD_WIDTH = 128
WINDOW_BLOCKS = 3


ROPE_BASE = 10000.0
NEG_FILL = -1e30


def passed_along(array, axis, by):
    devices = lax.axis_size(axis)
    pairs = [(i, i + by) for i in range(devices) if 0 <= i + by < devices]
    return lax.ppermute(array, axis, pairs)


def apply_rotary_embedding(values_in, positions_f):
    half_dim = values_in.shape[-1] // 2
    frequency = ROPE_BASE ** (-jnp.arange(half_dim, dtype=jnp.float32) * 2.0 / values_in.shape[-1])
    angles = positions_f[:, None, None] * frequency
    cosine = jnp.cos(angles)
    sine_part = jnp.sin(angles)
    first_half = values_in[..., :half_dim]
    second = values_in[..., half_dim:]
    return jnp.concatenate(
        [first_half * cosine - second * sine_part, second * cosine + first_half * sine_part],
        axis=-1,
    )


def local(queries, keys, values, key_norm_gain, stretch_ids, clean_flags, positions):
    count_of_rows = queries.shape[0]
    kv_heads = keys.shape[1] // HEAD_WIDTH
    q_heads = queries.shape[1] // HEAD_WIDTH
    heads_per_group = q_heads // kv_heads
    score_scale = 1.0 / math.sqrt(HEAD_WIDTH)
    blk_count = lax.axis_size("blk")
    blk_place = lax.axis_index("blk")
    group_index = lax.axis_index("stretch")
    self_index = group_index * blk_count + blk_place
    self_stretch = group_index * blk_count + stretch_ids[0, 0]
    self_clean = clean_flags[0, 0]
    token_positions = (positions[0, 0] + jnp.arange(count_of_rows, dtype=jnp.int32)).astype(
        jnp.float32
    )
    unnormed_keys = keys.astype(jnp.float32).reshape(count_of_rows, kv_heads, HEAD_WIDTH)
    normalized_keys = (
        unnormed_keys
        * lax.rsqrt(jnp.mean(unnormed_keys * unnormed_keys, axis=-1, keepdims=True) + 1e-06)
        * key_norm_gain.reshape(kv_heads, HEAD_WIDTH)
    )
    rotated_rows = (
        apply_rotary_embedding(normalized_keys, token_positions)
        .astype(jnp.bfloat16)
        .reshape(count_of_rows, kv_heads * HEAD_WIDTH)
    )
    rotated_queries = (
        apply_rotary_embedding(
            queries.astype(jnp.float32).reshape(count_of_rows, q_heads, HEAD_WIDTH), token_positions
        )
        .astype(jnp.bfloat16)
        .reshape(count_of_rows, kv_heads, heads_per_group, HEAD_WIDTH)
    )
    block_info = jnp.stack([self_stretch, self_clean, self_index, jnp.ones((), jnp.int32)])

    def blend_block(carry_state, key_rows, value_rows, visible):
        best_prev, weight_total, accumulated = carry_state
        scores = (
            jnp.einsum(
                "qhgd,khd->qhgk",
                rotated_queries,
                key_rows.reshape(-1, kv_heads, HEAD_WIDTH),
                preferred_element_type=jnp.float32,
            )
            * score_scale
        )
        scores = jnp.where(visible, scores, NEG_FILL)
        best_next = jnp.maximum(best_prev, jnp.max(scores, axis=-1))
        rescale = jnp.exp(best_prev - best_next)
        weights = jnp.exp(scores - best_next[..., None])
        weight_total = weight_total * rescale + jnp.sum(weights, axis=-1)
        product = jnp.einsum(
            "qhgk,khd->qhgd",
            weights.astype(jnp.bfloat16),
            value_rows.reshape(-1, kv_heads, HEAD_WIDTH),
            preferred_element_type=jnp.float32,
        )
        accumulated = accumulated * rescale[..., None] + product
        return (best_next, weight_total, accumulated)

    def absorb_block(carry_state, key_rows, value_rows, info_rows, offset):
        visible = (
            (info_rows[3] == 1)
            & (info_rows[2] == self_index + offset)
            & (
                (info_rows[0] < self_stretch) & (info_rows[1] == 1)
                | (info_rows[0] == self_stretch) & (info_rows[1] == self_clean)
            )
        )
        result = blend_block(carry_state, key_rows, value_rows, visible)
        return result

    carry_state = (
        jnp.full((count_of_rows, kv_heads, heads_per_group), NEG_FILL, jnp.float32),
        jnp.zeros((count_of_rows, kv_heads, heads_per_group), jnp.float32),
        jnp.zeros((count_of_rows, kv_heads, heads_per_group, HEAD_WIDTH), jnp.float32),
    )
    carry_state = absorb_block(carry_state, rotated_rows, values, block_info, 0)
    key_back, value_back, info_back = (rotated_rows, values, block_info)
    key_ahead, value_ahead, info_ahead = (rotated_rows, values, block_info)
    for hop_count in range(1, WINDOW_BLOCKS + 1):
        key_back, value_back, info_back = passed_along(
            (key_back, value_back, info_back), ("stretch", "blk"), 1
        )
        carry_state = absorb_block(carry_state, key_back, value_back, info_back, -hop_count)
        key_ahead, value_ahead, info_ahead = passed_along(
            (key_ahead, value_ahead, info_ahead), ("stretch", "blk"), -1
        )
        carry_state = absorb_block(carry_state, key_ahead, value_ahead, info_ahead, hop_count)
    best_last, weight_total, accumulated = carry_state
    attended = accumulated / weight_total[..., None]
    return attended.reshape(count_of_rows, q_heads * HEAD_WIDTH).astype(jnp.bfloat16)


def solution(mesh):
    placed = (
        P(("stretch", "blk"), "head"),
        P(("stretch", "blk"), "head"),
        P(("stretch", "blk"), "head"),
        P("head"),
        P("stretch", "blk"),
        P("stretch", "blk"),
        P("stretch", "blk"),
    )
    return jax.shard_map(
        local, mesh=mesh, in_specs=placed, out_specs=P(("stretch", "blk"), "head"), check_vma=False
    )
```

profile of v0, /device:TPU:24, one launch (start us, length us, event | category | flops | bytes accessed | tf_op | source)
XLA Modules:
  0.0 295.9 jit_solution(15839982983853513830)
XLA Ops:
  1.4 3.4 %collective-permute-start = (s32[4]{0:T(128)S(1)}, s32[4]{0:T(128)S(1)}, u32[]{:S(2)}, u32[]{:S(2)}) collective-permute-start(s32[4]{0:T(128)S(1)} %pad_add_fusion), channel_id=1, source_target_pairs={{0,1},{1,2},{2,3},{3,4},{4,5},{5,6},{6,7},{7,8},{8,9},{9,10},{10,1... | collective-permute-start | bytes 56 | tf_op jit(solution)/shard_map/ppermute | solution.py:19
  4.8 27.3 %collective-permute-start.3 = (s32[4]{0:T(128)S(1)}, s32[4]{0:T(128)S(1)}, u32[]{:S(2)}, u32[]{:S(2)}) collective-permute-start(s32[4]{0:T(128)S(1)} %pad_add_fusion), channel_id=1, source_target_pairs={{1,0},{2,1},{3,2},{4,3},{5,4},{6,5},{7,6},{8,7},{9,8},{10,9},{11,1... | collective-permute-start | bytes 56 | tf_op jit(solution)/shard_map/ppermute | solution.py:19
  35.4 1.9 collective-permute-start.1
  37.4 23.1 %collective-permute-start.4 = (bf16[128,256]{0,1:T(8,128)(2,1)S(1)}, bf16[128,256]{0,1:T(8,128)(2,1)S(1)}, u32[]{:S(2)}, u32[]{:S(2)}) collective-permute-start(bf16[128,256]{0,1:T(8,128)(2,1)S(1)} %bitcast.212), channel_id=1, source_target_pairs={{1,0},{2,1},{3,2},{4,3},{5,4},{6,5},{7,6},{8,7},{9,8},{10,9},{11,1... | collective-permute-start | bytes 196616 | tf_op jit(solution)/shard_map/ppermute | solution.py:19
  60.5 1.9 collective-permute-start.2
  64.6 23.1 %collective-permute-start.5 = (bf16[128,256]{1,0:T(8,128)(2,1)S(1)}, bf16[128,256]{1,0:T(8,128)(2,1)}, u32[]{:S(2)}, u32[]{:S(2)}) collective-permute-start(bf16[128,256]{1,0:T(8,128)(2,1)S(1)} %copy-done.13), channel_id=1, source_target_pairs={{1,0},{2,1},{3,2},{4,3},{5,4},{6,5},{7,6},{8,7},{9,8},{10,9},{11,1... | collective-permute-start | bytes 196616 | tf_op jit(solution)/shard_map/ppermute | solution.py:19
  96.7 1.9 collective-permute-start.9
  98.6 3.5 %collective-permute-done.9 = s32[4]{0:T(128)S(1)} collective-permute-done((s32[4]{0:T(128)S(1)}, s32[4]{0:T(128)S(1)}, u32[]{:S(2)}, u32[]{:S(2)}) %collective-permute-start.9) | collective-permute-done | bytes 48 | tf_op jit(solution)/shard_map/ppermute | solution.py:19
  102.1 1.9 collective-permute-start.6
  105.9 20.9 %collective-permute-done.6 = s32[4]{0:T(128)S(1)} collective-permute-done((s32[4]{0:T(128)S(1)}, s32[4]{0:T(128)S(1)}, u32[]{:S(2)}, u32[]{:S(2)}) %collective-permute-start.6) | collective-permute-done | bytes 48 | tf_op jit(solution)/shard_map/ppermute | solution.py:19
  133.8 1.9 collective-permute-start.12
  135.7 22.7 %collective-permute-done.12 = s32[4]{0:T(128)S(1)} collective-permute-done((s32[4]{0:T(128)S(1)}, s32[4]{0:T(128)S(1)}, u32[]{:S(2)}, u32[]{:S(2)}) %collective-permute-start.12) | collective-permute-done | bytes 48 | tf_op jit(solution)/shard_map/ppermute | solution.py:19
  158.4 1.9 collective-permute-start.15
  171.8 21.1 %collective-permute-start.10 = (bf16[128,256]{0,1:T(8,128)(2,1)S(1)}, bf16[128,256]{0,1:T(8,128)(2,1)}, u32[]{:S(2)}, u32[]{:S(2)}) collective-permute-start(bf16[128,256]{0,1:T(8,128)(2,1)S(1)} %collective-permute-done.4), channel_id=1, source_target_pairs={{1,0},{2,1},{3,2},{4,3},{5,4},{6,5},{7,6},{8,7},{9,8},{10,9},{11,1... | collective-permute-start | bytes 196616 | tf_op jit(solution)/shard_map/ppermute | solution.py:19
  193.0 1.8 fusion.71
  194.7 1.9 collective-permute-start.7
  198.2 1.9 collective-permute-start.8
  201.7 23.1 %collective-permute-start.11 = (bf16[128,256]{1,0:T(8,128)(2,1)}, bf16[128,256]{1,0:T(8,128)(2,1)}, u32[]{:S(2)}, u32[]{:S(2)}) collective-permute-start(bf16[128,256]{1,0:T(8,128)(2,1)} %collective-permute-done.5), channel_id=1, source_target_pairs={{1,0},{2,1},{3,2},{4,3},{5,4},{6,5},{7,6},{8,7},{9,8},{10,9},{11,1... | collective-permute-start | bytes 196616 | tf_op jit(solution)/shard_map/ppermute | solution.py:19
  224.9 1.8 fusion.68
  226.6 1.9 collective-permute-start.13
  228.6 2.7 fusion.69
  231.2 23.1 %collective-permute-start.16 = (bf16[128,256]{0,1:T(8,128)(2,1)}, bf16[128,256]{0,1:T(8,128)(2,1)}, u32[]{:S(2)}, u32[]{:S(2)}) collective-permute-start(bf16[128,256]{0,1:T(8,128)(2,1)} %collective-permute-done.10), channel_id=1, source_target_pairs={{1,0},{2,1},{3,2},{4,3},{5,4},{6,5},{7,6},{8,7},{9,8},{10,9},{11,1... | collective-permute-start | bytes 196616 | tf_op jit(solution)/shard_map/ppermute | solution.py:19
  255.9 1.9 collective-permute-start.14
  259.4 23.1 %collective-permute-start.17 = (bf16[128,256]{1,0:T(8,128)(2,1)}, bf16[128,256]{1,0:T(8,128)(2,1)}, u32[]{:S(2)}, u32[]{:S(2)}) collective-permute-start(bf16[128,256]{1,0:T(8,128)(2,1)} %collective-permute-done.11), channel_id=1, source_target_pairs={{1,0},{2,1},{3,2},{4,3},{5,4},{6,5},{7,6},{8,7},{9,8},{10,9},{11,1... | collective-permute-start | bytes 196616 | tf_op jit(solution)/shard_map/ppermute | solution.py:19
  (108 shorter events, 30.4 us)
Async XLA Ops:
  1.4 88.3 %collective-permute-start = (s32[4]{0:T(128)S(1)}, s32[4]{0:T(128)S(1)}, u32[]{:S(2)}, u32[]{:S(2)}) collective-permute-start(s32[4]{0:T(128)S(1)} %pad_add_fusion), channel_id=1, source_target_pairs={{0,1},{1,2},{2,3},{3,4},{4,5},{5,6},{6,7},{7,8},{8,9},{9,10},{10,1... | collective-permute-start | bytes 56 | tf_op jit(solution)/shard_map/ppermute | solution.py:19
  4.8 59.8 %collective-permute-start.3 = (s32[4]{0:T(128)S(1)}, s32[4]{0:T(128)S(1)}, u32[]{:S(2)}, u32[]{:S(2)}) collective-permute-start(s32[4]{0:T(128)S(1)} %pad_add_fusion), channel_id=1, source_target_pairs={{1,0},{2,1},{3,2},{4,3},{5,4},{6,5},{7,6},{8,7},{9,8},{10,9},{11,1... | collective-permute-start | bytes 56 | tf_op jit(solution)/shard_map/ppermute | solution.py:19
  35.1 28.1 %copy-start.5 = (bf16[128,1536]{1,0:T(8,128)(2,1)S(1)}, bf16[128,1536]{1,0:T(8,128)(2,1)}, u32[]{:S(2)}) copy-start(bf16[128,1536]{1,0:T(8,128)(2,1)} %param.7) | copy-start | bytes 1179652
  35.3 25.2 %copy-start.13 = (bf16[128,256]{1,0:T(8,128)(2,1)S(1)}, bf16[128,256]{1,0:T(8,128)(2,1)}, u32[]{:S(2)}) copy-start(bf16[128,256]{1,0:T(8,128)(2,1)} %param.9) | copy-start | bytes 196612
  35.4 157.5 %collective-permute-start.1 = (bf16[128,256]{0,1:T(8,128)(2,1)S(1)}, bf16[128,256]{0,1:T(8,128)(2,1)}, u32[]{:S(2)}, u32[]{:S(2)}) collective-permute-start(bf16[128,256]{0,1:T(8,128)(2,1)S(1)} %bitcast.211), channel_id=1, source_target_pairs={{0,1},{1,2},{2,3},{3,4},{4,5},{5,6},{6,7},{7,8},{8,9},{9,10},{10,1... | collective-permute-start | bytes 196616 | tf_op jit(solution)/shard_map/ppermute | solution.py:19
  37.4 133.5 %collective-permute-start.4 = (bf16[128,256]{0,1:T(8,128)(2,1)S(1)}, bf16[128,256]{0,1:T(8,128)(2,1)S(1)}, u32[]{:S(2)}, u32[]{:S(2)}) collective-permute-start(bf16[128,256]{0,1:T(8,128)(2,1)S(1)} %bitcast.212), channel_id=1, source_target_pairs={{1,0},{2,1},{3,2},{4,3},{5,4},{6,5},{7,6},{8,7},{9,8},{10,9},{11,1... | collective-permute-start | bytes 196616 | tf_op jit(solution)/shard_map/ppermute | solution.py:19
  60.5 136.1 %collective-permute-start.2 = (bf16[128,256]{1,0:T(8,128)(2,1)S(1)}, bf16[128,256]{1,0:T(8,128)(2,1)}, u32[]{:S(2)}, u32[]{:S(2)}) collective-permute-start(bf16[128,256]{1,0:T(8,128)(2,1)S(1)} %copy-done.13), channel_id=1, source_target_pairs={{0,1},{1,2},{2,3},{3,4},{4,5},{5,6},{6,7},{7,8},{8,9},{9,10},{10,1... | collective-permute-start | bytes 196616 | tf_op jit(solution)/shard_map/ppermute | solution.py:19
  64.6 135.5 %collective-permute-start.5 = (bf16[128,256]{1,0:T(8,128)(2,1)S(1)}, bf16[128,256]{1,0:T(8,128)(2,1)}, u32[]{:S(2)}, u32[]{:S(2)}) collective-permute-start(bf16[128,256]{1,0:T(8,128)(2,1)S(1)} %copy-done.13), channel_id=1, source_target_pairs={{1,0},{2,1},{3,2},{4,3},{5,4},{6,5},{7,6},{8,7},{9,8},{10,9},{11,1... | collective-permute-start | bytes 196616 | tf_op jit(solution)/shard_map/ppermute | solution.py:19
  96.7 5.4 %collective-permute-start.9 = (s32[4]{0:T(128)S(1)}, s32[4]{0:T(128)S(1)}, u32[]{:S(2)}, u32[]{:S(2)}) collective-permute-start(s32[4]{0:T(128)S(1)} %collective-permute-done.3), channel_id=1, source_target_pairs={{1,0},{2,1},{3,2},{4,3},{5,4},{6,5},{7,6},{8,7},{9,8},{10,9},{11,1... | collective-permute-start | bytes 56 | tf_op jit(solution)/shard_map/ppermute | solution.py:19
  102.1 24.6 %collective-permute-start.6 = (s32[4]{0:T(128)S(1)}, s32[4]{0:T(128)S(1)}, u32[]{:S(2)}, u32[]{:S(2)}) collective-permute-start(s32[4]{0:T(128)S(1)} %collective-permute-done), channel_id=1, source_target_pairs={{0,1},{1,2},{2,3},{3,4},{4,5},{5,6},{6,7},{7,8},{8,9},{9,10},{10,1... | collective-permute-start | bytes 56 | tf_op jit(solution)/shard_map/ppermute | solution.py:19
  133.8 24.7 %collective-permute-start.12 = (s32[4]{0:T(128)S(1)}, s32[4]{0:T(128)S(1)}, u32[]{:S(2)}, u32[]{:S(2)}) collective-permute-start(s32[4]{0:T(128)S(1)} %collective-permute-done.6), channel_id=1, source_target_pairs={{0,1},{1,2},{2,3},{3,4},{4,5},{5,6},{6,7},{7,8},{8,9},{9,10},{10,1... | collective-permute-start | bytes 56 | tf_op jit(solution)/shard_map/ppermute | solution.py:19
  158.4 5.4 %collective-permute-start.15 = (s32[4]{0:T(128)S(1)}, s32[4]{0:T(128)S(1)}, u32[]{:S(2)}, u32[]{:S(2)}) collective-permute-start(s32[4]{0:T(128)S(1)} %collective-permute-done.9), channel_id=1, source_target_pairs={{1,0},{2,1},{3,2},{4,3},{5,4},{6,5},{7,6},{8,7},{9,8},{10,9},{11,1... | collective-permute-start | bytes 56 | tf_op jit(solution)/shard_map/ppermute | solution.py:19
  171.8 53.1 %collective-permute-start.10 = (bf16[128,256]{0,1:T(8,128)(2,1)S(1)}, bf16[128,256]{0,1:T(8,128)(2,1)}, u32[]{:S(2)}, u32[]{:S(2)}) collective-permute-start(bf16[128,256]{0,1:T(8,128)(2,1)S(1)} %collective-permute-done.4), channel_id=1, source_target_pairs={{1,0},{2,1},{3,2},{4,3},{5,4},{6,5},{7,6},{8,7},{9,8},{10,9},{11,1... | collective-permute-start | bytes 196616 | tf_op jit(solution)/shard_map/ppermute | solution.py:19
  194.7 31.9 %collective-permute-start.7 = (bf16[128,256]{0,1:T(8,128)(2,1)}, bf16[128,256]{0,1:T(8,128)(2,1)}, u32[]{:S(2)}, u32[]{:S(2)}) collective-permute-start(bf16[128,256]{0,1:T(8,128)(2,1)} %collective-permute-done.1), channel_id=1, source_target_pairs={{0,1},{1,2},{2,3},{3,4},{4,5},{5,6},{6,7},{7,8},{8,9},{9,10},{10,1... | collective-permute-start | bytes 196616 | tf_op jit(solution)/shard_map/ppermute | solution.py:19
  198.2 56.2 %collective-permute-start.8 = (bf16[128,256]{1,0:T(8,128)(2,1)}, bf16[128,256]{1,0:T(8,128)(2,1)}, u32[]{:S(2)}, u32[]{:S(2)}) collective-permute-start(bf16[128,256]{1,0:T(8,128)(2,1)} %collective-permute-done.2), channel_id=1, source_target_pairs={{0,1},{1,2},{2,3},{3,4},{4,5},{5,6},{6,7},{7,8},{8,9},{9,10},{10,1... | collective-permute-start | bytes 196616 | tf_op jit(solution)/shard_map/ppermute | solution.py:19
  201.7 56.2 %collective-permute-start.11 = (bf16[128,256]{1,0:T(8,128)(2,1)}, bf16[128,256]{1,0:T(8,128)(2,1)}, u32[]{:S(2)}, u32[]{:S(2)}) collective-permute-start(bf16[128,256]{1,0:T(8,128)(2,1)} %collective-permute-done.5), channel_id=1, source_target_pairs={{1,0},{2,1},{3,2},{4,3},{5,4},{6,5},{7,6},{8,7},{9,8},{10,9},{11,1... | collective-permute-start | bytes 196616 | tf_op jit(solution)/shard_map/ppermute | solution.py:19
  226.6 55.9 %collective-permute-start.13 = (bf16[128,256]{0,1:T(8,128)(2,1)}, bf16[128,256]{0,1:T(8,128)(2,1)}, u32[]{:S(2)}, u32[]{:S(2)}) collective-permute-start(bf16[128,256]{0,1:T(8,128)(2,1)} %collective-permute-done.7), channel_id=1, source_target_pairs={{0,1},{1,2},{2,3},{3,4},{4,5},{5,6},{6,7},{7,8},{8,9},{9,10},{10,1... | collective-permute-start | bytes 196616 | tf_op jit(solution)/shard_map/ppermute | solution.py:19
  231.2 52.6 %collective-permute-start.16 = (bf16[128,256]{0,1:T(8,128)(2,1)}, bf16[128,256]{0,1:T(8,128)(2,1)}, u32[]{:S(2)}, u32[]{:S(2)}) collective-permute-start(bf16[128,256]{0,1:T(8,128)(2,1)} %collective-permute-done.10), channel_id=1, source_target_pairs={{1,0},{2,1},{3,2},{4,3},{5,4},{6,5},{7,6},{8,7},{9,8},{10,9},{11,1... | collective-permute-start | bytes 196616 | tf_op jit(solution)/shard_map/ppermute | solution.py:19
  255.9 36.4 %collective-permute-start.14 = (bf16[128,256]{1,0:T(8,128)(2,1)}, bf16[128,256]{1,0:T(8,128)(2,1)}, u32[]{:S(2)}, u32[]{:S(2)}) collective-permute-start(bf16[128,256]{1,0:T(8,128)(2,1)} %collective-permute-done.8), channel_id=1, source_target_pairs={{0,1},{1,2},{2,3},{3,4},{4,5},{5,6},{6,7},{7,8},{8,9},{9,10},{10,1... | collective-permute-start | bytes 196616 | tf_op jit(solution)/shard_map/ppermute | solution.py:19
  259.4 34.2 %collective-permute-start.17 = (bf16[128,256]{1,0:T(8,128)(2,1)}, bf16[128,256]{1,0:T(8,128)(2,1)}, u32[]{:S(2)}, u32[]{:S(2)}) collective-permute-start(bf16[128,256]{1,0:T(8,128)(2,1)} %collective-permute-done.11), channel_id=1, source_target_pairs={{1,0},{2,1},{3,2},{4,3},{5,4},{6,5},{7,6},{8,7},{9,8},{10,9},{11,1... | collective-permute-start | bytes 196616 | tf_op jit(solution)/shard_map/ppermute | solution.py:19
  283.8 3.8 %copy-start.1 = (f32[128,2,6,128]{0,3,2,1:T(8,128)}, f32[128,2,6,128]{0,3,2,1:T(8,128)S(1)}, u32[]{:S(2)}) copy-start(f32[128,2,6,128]{0,3,2,1:T(8,128)S(1)} %get-tuple-element.53) | copy-start | bytes 2359300
  283.8 1.5 copy-start.15
  283.8 1.5 copy-start.16
  286.0 1.9 copy-start.11
  (15 other events, 14.7 us)
where the time goes:
time: 298 us; the launch traced here: 296 us
  starting transfers between devices  187 us (63%)
  waiting for transfers between devices  48.7 us (16%)
  between operations  25.5 us (9%)
  local copies, waits for them, and re-layouts  20.5 us (7%)
  matrix products  11.9 us (4%)
    ppermute x18, starting transfers between devices, passed_along(): return lax.ppermute(array, axis, pairs)  187 us
    ppermute x18, waiting for transfers between devices, passed_along(): return lax.ppermute(array, axis, pairs)  48.7 us
    dot_general x7, matrix products, blend_block(): jnp.einsum('qhgd,khd->qhgk', rotated_queries, key_rows.reshape(-1, kv_hea...  9.95 us
    ppermute x6, local copies, waits for them, and re-layouts, passed_along(): return lax.ppermute(array, axis, pairs)  8.17 us
  transfers between devices with their start and end apart: 18, of which 4 were waited for; matrix products, arithmetic and copies ran while one was open for 9% of the time, Pallas kernels for 0%

commit v1 on v0

v1 whole, which is shorter than its diff:
```python
import math

import jax
import jax.numpy as jnp
import numpy as np
from jax import lax
from jax.experimental import pallas as pl
from jax.experimental.pallas import tpu as pltpu
from jax.sharding import PartitionSpec as P

D = 128
WINDOW = 3
ROPE_BASE = 10000.0
NEG = -1e30
LABEL_ROWS = 16
AXES = ("stretch", "blk")
SCALE = math.log2(math.e) / math.sqrt(D)


def rope_tables(rows):
    half = D // 2
    f = ROPE_BASE ** (-2.0 * np.arange(half) / D)
    f = np.concatenate([f, f])[None, :]
    t = np.arange(rows, dtype=np.float64)[:, None] * f
    a = 128.0 * np.arange(16, dtype=np.float64)[:, None] * f
    cos = np.concatenate([np.cos(t), np.cos(a)], 0)
    sin = np.concatenate([np.sin(t), np.sin(a)], 0)
    return np.stack([cos, sin]).astype(np.float32)


def angles(pos, tab, rows):
    high = lax.shift_right_logical(pos, 7)
    low = lax.bitwise_and(pos, 127)
    ch, sh = tab[0, pl.ds(rows + high, 1), :], tab[1, pl.ds(rows + high, 1), :]
    cl, sl = tab[0, pl.ds(low, 1), :], tab[1, pl.ds(low, 1), :]
    cp = ch * cl - sh * sl
    sp = sh * cl + ch * sl
    ct, st = tab[0, 0:rows, :], tab[1, 0:rows, :]
    lane = lax.broadcasted_iota(jnp.int32, (1, D), 1)
    sign = jnp.where(lane < D // 2, -1.0, 1.0)
    return cp * ct - sp * st, (sp * ct + cp * st) * sign


def rotate(x, cos, sin):
    return x * cos + pltpu.roll(x, D // 2, 1) * sin


def pack_kernel(stretch, clean, pos, k, v, gain, tab, out):
    rows = k.shape[0]
    cos, sin = angles(pos[0, 0], tab, rows)
    for g in range(k.shape[1] // D):
        cols = pl.ds(g * D, D)
        x = k[:, cols].astype(jnp.float32)
        x = x * lax.rsqrt(jnp.mean(x * x, axis=-1, keepdims=True) + 1e-6) * gain[:, cols]
        out[0:rows, cols] = rotate(x, cos, sin).astype(jnp.bfloat16)
    out[pl.ds(rows, rows), :] = v[...]
    label = stretch[0, 0] + 16 * lax.axis_index("stretch")
    row = lax.broadcasted_iota(jnp.int32, (LABEL_ROWS, k.shape[1]), 0)
    info = jnp.where(row == 0, label, jnp.where(row == 1, clean[0, 0], 1))
    out[pl.ds(2 * rows, LABEL_ROWS), :] = info.astype(jnp.float32).astype(jnp.bfloat16)


def labels(ref):
    top = ref.shape[0] - LABEL_ROWS
    info = ref[pl.ds(top, LABEL_ROWS), 0:D].astype(jnp.float32)
    return info[0:1], info[1:2], info[2:3]


def seen(own, other):
    (stretch, clean, _), (stretch2, clean2, there) = own, other
    earlier = (stretch2 < stretch) & (clean2 > 0.5)
    same = (stretch2 == stretch) & (clean2 == clean)
    return (there > 0.5) & (earlier | same)


def scores_of(q, kv, g):
    rows = (kv.shape[0] - LABEL_ROWS) // 2
    keys = kv[0:rows, pl.ds(g * D, D)]
    return lax.dot_general(
        q, keys, (((1,), (1,)), ((), ())), preferred_element_type=jnp.float32
    )


def blend(q, blocks, visible, g, best):
    scores = [scores_of(q, kv, g) for kv in blocks]
    for s, vis in zip(scores, visible):
        top = jnp.where(vis, jnp.max(s, axis=-1, keepdims=True), NEG)
        best = top if best is None else jnp.maximum(best, top)
    shift = best * SCALE
    total, mixed = None, None
    for s, vis, kv in zip(scores, visible, blocks):
        rows = (kv.shape[0] - LABEL_ROWS) // 2
        w = jnp.exp2(s * SCALE - jnp.where(vis, shift, -NEG))
        part = jnp.dot(
            w.astype(jnp.bfloat16),
            kv[pl.ds(rows, rows), pl.ds(g * D, D)],
            preferred_element_type=jnp.float32,
        )
        total = w if total is None else total + w
        mixed = part if mixed is None else mixed + part
    total = jnp.broadcast_to(jnp.sum(total, axis=-1, keepdims=True), best.shape)
    return best, total, mixed


def query_kernel(pos, q, own, tab, rq, again):
    rows, heads = q.shape[0], q.shape[1] // D
    cos, sin = angles(pos[0, 0], tab, rows)
    again[...] = own[...]
    for h in range(heads):
        x = q[:, pl.ds(h * D, D)].astype(jnp.float32)
        rq[pl.ds(h * rows, rows), :] = rotate(x, cos, sin).astype(jnp.bfloat16)


def first_kernel(own, a1, a23, rq, best_out, total_out, mixed_out):
    rows = (own.shape[0] - LABEL_ROWS) // 2
    groups = own.shape[1] // D
    per = rq.shape[0] // rows // groups
    mine = labels(own)
    size = own.shape[0]
    blocks = (own, a1, a23.at[pl.ds(0, size)], a23.at[pl.ds(size, size)])
    visible = [seen(mine, labels(kv)) for kv in blocks]
    for g in range(groups):
        at = pl.ds(g * per * rows, per * rows)
        best, total, mixed = blend(rq[at, :], blocks, visible, g, None)
        best_out[at, :] = best
        total_out[at, :] = total
        mixed_out[at, :] = mixed


def last_kernel(own, b1, b2, b3, rq, best_in, total_in, mixed_in, out):
    rows = out.shape[0]
    groups = own.shape[1] // D
    per = rq.shape[0] // rows // groups
    mine = labels(own)
    blocks = (b3, b2, b1)
    visible = [seen(mine, labels(kv)) for kv in blocks]
    for g in range(groups):
        at = pl.ds(g * per * rows, per * rows)
        before = best_in[at, :]
        best, total, mixed = blend(rq[at, :], blocks, visible, g, before)
        kept = jnp.exp2((before - best) * SCALE)
        total = total_in[at, :] * kept + total
        mixed = (mixed_in[at, :] * kept + mixed) / total
        for i in range(per):
            out[:, pl.ds((g * per + i) * D, D)] = mixed[i * rows : (i + 1) * rows].astype(
                jnp.bfloat16
            )


VM = pl.BlockSpec(memory_space=pltpu.VMEM)
SM = pl.BlockSpec(memory_space=pltpu.SMEM)
LIMIT = 40 * 1024 * 1024


def local(queries, keys, values, key_norm_gain, stretch_ids, clean_flags, positions):
    rows, width = keys.shape
    heads = queries.shape[1] // D
    groups, per_group = lax.axis_size("stretch"), lax.axis_size("blk")
    blocks = groups * per_group
    tab = jnp.asarray(rope_tables(rows))
    packed = jax.ShapeDtypeStruct((2 * rows + LABEL_ROWS, width), jnp.bfloat16)
    own = pl.pallas_call(
        pack_kernel,
        out_shape=packed,
        in_specs=[SM, SM, SM, VM, VM, VM, VM],
        out_specs=VM,
        compiler_params=pltpu.CompilerParams(vmem_limit_bytes=LIMIT),
        cost_estimate=pl.CostEstimate(flops=10**6, bytes_accessed=4 * 10**5, transcendentals=0),
        name="pack",
    )(stretch_ids, clean_flags, positions, keys, values, key_norm_gain[None, :], tab)

    turned = jax.ShapeDtypeStruct((heads * rows, D), jnp.bfloat16)
    rq, again = pl.pallas_call(
        query_kernel,
        out_shape=(turned, packed),
        in_specs=[SM] + [VM] * 3,
        out_specs=(VM, VM),
        compiler_params=pltpu.CompilerParams(vmem_limit_bytes=LIMIT),
        cost_estimate=pl.CostEstimate(flops=10**6, bytes_accessed=10**6, transcendentals=0),
        name="turn_queries",
    )(positions, queries, own, tab)

    def back(by):
        return lax.ppermute(own, AXES, [(b, b + by) for b in range(blocks - by)])

    def ahead(by):
        pairs = [(b, b - by) for b in range(blocks) if b % per_group >= by]
        return lax.ppermute(again, AXES, pairs)

    b3, b2, b1 = back(3), back(2), back(1)

    def ahead(array, by):
        pairs = [(b, b - by) for b in range(blocks) if b % per_group >= by]
        return lax.ppermute(array, AXES, pairs)

    state = jax.ShapeDtypeStruct((heads * rows, D), jnp.float32)
    def near(own, again, rq):
        a1 = ahead(again, 1)
        a23 = ahead(jnp.concatenate([again, a1], 0), 2)
        done = pl.pallas_call(
            first_kernel,
            out_shape=(state, state, state),
            in_specs=[VM] * 4,
            out_specs=(VM,) * 3,
            compiler_params=pltpu.CompilerParams(vmem_limit_bytes=LIMIT),
            cost_estimate=pl.CostEstimate(
                flops=4 * heads * rows * 4 * rows * D,
                bytes_accessed=3 * 10**6,
                transcendentals=10**6,
            ),
            name="own_and_ahead",
        )(own, a1, a23, rq)
        return tuple(done)

    def never(own, again, rq):
        return (jnp.zeros(state.shape, state.dtype),) * 3

    best, total, mixed = lax.cond(positions[0, 0] >= 0, near, never, own, again, rq)
    return pl.pallas_call(
        last_kernel,
        out_shape=jax.ShapeDtypeStruct((rows, heads * D), jnp.bfloat16),
        in_specs=[VM] * 8,
        out_specs=VM,
        compiler_params=pltpu.CompilerParams(vmem_limit_bytes=LIMIT),
        cost_estimate=pl.CostEstimate(
            flops=4 * heads * rows * 3 * rows * D, bytes_accessed=3 * 10**6, transcendentals=10**6
        ),
        name="back",
    )(own, b1, b2, b3, rq, best, total, mixed)


def solution(mesh):
    placed = (
        P(("stretch", "blk"), "head"),
        P(("stretch", "blk"), "head"),
        P(("stretch", "blk"), "head"),
        P("head"),
        P("stretch", "blk"),
        P("stretch", "blk"),
        P("stretch", "blk"),
    )
    return jax.shard_map(
        local, mesh=mesh, in_specs=placed, out_specs=P(("stretch", "blk"), "head"), check_vma=False
    )
```

time: 298 us -> 51.9 us (0.17)
  the two profiles are of different devices: /device:TPU:24 before, /device:TPU:974 now
where the time goes in v1:
time: 51.9 us; the launch traced here: 51.5 us
  starting transfers between devices  25.3 us (49%)
  waiting for transfers between devices  14.9 us (29%)
  Pallas kernels  4.89 us (9%)
  local copies, waits for them, and re-layouts  4.25 us (8%)
  between operations  2.04 us (4%)
    ppermute x3, starting transfers between devices, back(): return lax.ppermute(own, AXES, [(b, b + by) for b in range(blocks - by)])  20.3 us
    ppermute x2, waiting for transfers between devices, ahead(): return lax.ppermute(array, AXES, pairs)  14.9 us
    ppermute x2, starting transfers between devices, ahead(): return lax.ppermute(array, AXES, pairs)  4.97 us
    unnamed x12, local copies, waits for them, and re-layouts  4.25 us
    pallas_call x1, Pallas kernels, local(): pl.pallas_call(last_kernel, out_shape=jax.ShapeDtypeStruct((rows, heads *...  2.48 us
    pallas_call x1, Pallas kernels, near(): pl.pallas_call(first_kernel, out_shape=(state, state, state), in_specs=[V...  2 us
  transfers between devices with their start and end apart: 5, of which 2 were waited for; matrix products, arithmetic and copies ran while one was open for 0% of the time, Pallas kernels for 4%

profile of v1, /device:TPU:974, one launch (start us, length us, event | category | flops | bytes accessed | tf_op | source)
XLA Modules:
  0.0 51.5 jit_solution(12663226678060213098)
XLA Ops:
  1.9 0.0 copy-start.5
  2.0 0.7 %copy-done.5 = f32[256]{0:T(256)S(1)} copy-done((f32[256]{0:T(256)S(1)}, f32[256]{0:T(256)}, u32[]{:S(2)}) %copy-start.5) | copy-done | bytes 1048
  2.6 0.0 copy-start
  2.6 0.9 %copy-done = f32[2,144,128]{2,1,0:T(8,128)S(1)} copy-done((f32[2,144,128]{2,1,0:T(8,128)S(1)}, f32[2,144,128]{2,1,0:T(8,128)}, u32[]{:S(2)}) %copy-start) | copy-done | bytes 147480
  3.5 0.8 %copy-done.3 = bf16[128,256]{1,0:T(8,128)(2,1)S(1)} copy-done((bf16[128,256]{1,0:T(8,128)(2,1)S(1)}, bf16[128,256]{1,0:T(8,128)(2,1)}, u32[]{:S(2)}) %copy-start.3) | copy-done | bytes 65560
  4.4 0.8 %copy-done.4 = bf16[128,256]{1,0:T(8,128)(2,1)S(1)} copy-done((bf16[128,256]{1,0:T(8,128)(2,1)S(1)}, bf16[128,256]{1,0:T(8,128)(2,1)}, u32[]{:S(2)}) %copy-start.4) | copy-done | bytes 65560
  5.2 0.2 pack.1.own
  5.4 2.8 %collective-permute-start.2 = (bf16[272,256]{1,0:T(8,128)(2,1)S(1)}, bf16[272,256]{1,0:T(8,128)(2,1)S(1)}, u32[]{:S(2)}, u32[]{:S(2)}) collective-permute-start(bf16[272,256]{1,0:T(8,128)(2,1)S(1)} %pack.1.own), channel_id=1, source_target_pairs={{0,1},{1,2},{2,3},{3,4},{4,5},{5,6},{6,7},{7,8},{8,9},{9,10},{10,1... | collective-permute-start | bytes 417800 | tf_op jit(solution)/shard_map/ppermute | solution.py:184
  8.3 4.3 %collective-permute-start.3 = (bf16[272,256]{1,0:T(8,128)(2,1)S(1)}, bf16[272,256]{1,0:T(8,128)(2,1)S(1)}, u32[]{:S(2)}, u32[]{:S(2)}) collective-permute-start(bf16[272,256]{1,0:T(8,128)(2,1)S(1)} %pack.1.own), channel_id=1, source_target_pairs={{0,2},{1,3},{2,4},{3,5},{4,6},{5,7},{6,8},{7,9},{8,10},{9,11},{10,... | collective-permute-start | bytes 417800 | tf_op jit(solution)/shard_map/ppermute | solution.py:184
  12.6 13.1 %collective-permute-start.4 = (bf16[272,256]{1,0:T(8,128)(2,1)S(1)}, bf16[272,256]{1,0:T(8,128)(2,1)S(1)}, u32[]{:S(2)}, u32[]{:S(2)}) collective-permute-start(bf16[272,256]{1,0:T(8,128)(2,1)S(1)} %pack.1.own), channel_id=1, source_target_pairs={{0,3},{1,4},{2,5},{3,6},{4,7},{5,8},{6,9},{7,10},{8,11},{9,12},{10... | collective-permute-start | bytes 417800 | tf_op jit(solution)/shard_map/ppermute | solution.py:184
  25.8 0.0 copy-done.1
  25.8 0.0 copy-start.2
  25.8 1.0 %copy-done.2 = bf16[128,1536]{1,0:T(8,128)(2,1)S(1)} copy-done((bf16[128,1536]{1,0:T(8,128)(2,1)S(1)}, bf16[128,1536]{1,0:T(8,128)(2,1)}, u32[]{:S(2)}) %copy-start.2) | copy-done | bytes 393240
  26.8 0.2 turn_queries.1
  27.0 21.9 %conditional.1 = ((f32[1536,128]{1,0:T(8,128)S(1)}, f32[1536,128]{1,0:T(8,128)S(1)}, f32[1536,128]{1,0:T(8,128)S(1)})) conditional(s32[]{:T(128)} %bitcast.1, () %tuple.12, (bf16[272,256]{1,0:T(8,128)(2,1)S(1)}, bf16[272,256]{1,0:T(8,128)(2,1)S(1)}, bf16[1536,128]{1,0:T(8,128)(2,1)S(1)}) %tuple.13), branch_computations={%region_0.0_spmd, %region_1.0_spmd} | conditional | flops 403210240 | bytes 5228312 | solution.py:218
  27.0 3.0 %collective-permute-start = (bf16[272,256]{1,0:T(8,128)(2,1)S(1)}, bf16[272,256]{1,0:T(8,128)(2,1)S(1)}, u32[]{:S(2)}, u32[]{:S(2)}) collective-permute-start(bf16[272,256]{1,0:T(8,128)(2,1)S(1)} %get-tuple-element.12), channel_id=1, source_target_pairs={{1,0},{2,1},{3,2},{4,3},{5,4},{6,5},{7,6},{8,7},{9,8},{10,9},{11,1... | collective-permute-start | bytes 417800 | tf_op jit(solution)/shard_map/cond/branch_1_fun/ppermute | solution.py:194
  30.1 6.0 %collective-permute-done.a1 = bf16[272,256]{1,0:T(8,128)(2,1)S(1)} collective-permute-done((bf16[272,256]{1,0:T(8,128)(2,1)S(1)}, bf16[272,256]{1,0:T(8,128)(2,1)S(1)}, u32[]{:S(2)}, u32[]{:S(2)}) %collective-permute-start) | collective-permute-done | bytes 139296 | tf_op jit(solution)/shard_map/cond/branch_1_fun/ppermute | solution.py:194
  36.1 1.9 %collective-permute-start.1 = (bf16[544,256]{1,0:T(8,128)(2,1)S(1)}, bf16[544,256]{1,0:T(8,128)(2,1)S(1)}, u32[]{:S(2)}, u32[]{:S(2)}) collective-permute-start(bf16[544,256]{1,0:T(8,128)(2,1)S(1)} %pad_maximum_fusion), channel_id=1, source_target_pairs={{2,0},{3,1},{4,2},{5,3},{6,4},{7,5},{8,6},{9,7},{10,8},{11,9},{12,... | collective-permute-start | bytes 835592 | tf_op jit(solution)/shard_map/cond/branch_1_fun/ppermute | solution.py:194
  38.0 8.9 %collective-permute-done.1.a23 = bf16[544,256]{1,0:T(8,128)(2,1)S(1)} collective-permute-done((bf16[544,256]{1,0:T(8,128)(2,1)S(1)}, bf16[544,256]{1,0:T(8,128)(2,1)S(1)}, u32[]{:S(2)}, u32[]{:S(2)}) %collective-permute-start.1) | collective-permute-done | bytes 278560 | tf_op jit(solution)/shard_map/cond/branch_1_fun/ppermute | solution.py:194
  46.9 2.0 %own_and_ahead.1 = (f32[1536,128]{1,0:T(8,128)S(1)}, f32[1536,128]{1,0:T(8,128)S(1)}, f32[1536,128]{1,0:T(8,128)S(1)}) custom-call(bf16[272,256]{1,0:T(8,128)(2,1)S(1)} %get-tuple-element.11.own, bf16[272,256]{1,0:T(8,128)(2,1)S(1)} %collective-permute-done.a1, bf16[544,256]{1,0:T(8,128)(2,1)S(1)} %collective-permute-done.1.a23, ...), custom_call_target="tpu_custom_call" | custom-call | flops 402653184 | bytes 3000000 | tf_op jit(solution)/shard_map/cond/branch_1_fun/own_and_ahead/pallas_call | solution.py:200
  48.9 0.0 collective-permute-done.2.b1
  49.0 0.0 collective-permute-done.3.b2
  49.0 0.0 collective-permute-done.4.b3
  49.0 2.5 %back.1 = bf16[128,1536]{1,0:T(8,128)(2,1)} custom-call(bf16[272,256]{1,0:T(8,128)(2,1)S(1)} %pack.1.own, bf16[272,256]{1,0:T(8,128)(2,1)S(1)} %collective-permute-done.2.b1, bf16[272,256]{1,0:T(8,128)(2,1)S(1)} %collective-permute-done.3.b2, bf16[272,256]{1,0:T(8,128)(2,1)S(1)} %collective-permute-done.4.b3, bf16[1536,128]{1,0:T(8,128)(2,1)S(1)} %get-tuple-element.19.rq, ...), custom_call_target="tpu_custom_call" | custom-call | flops 301989888 | bytes 3000000 | tf_op jit(solution)/shard_map/back/pallas_call | solution.py:219
  (4 shorter events, 0.0 us)
Async XLA Ops:
  1.9 0.7 %copy-start.5 = (f32[256]{0:T(256)S(1)}, f32[256]{0:T(256)}, u32[]{:S(2)}) copy-start(f32[256]{0:T(256)} %param.13) | copy-start | bytes 3076
  2.6 0.9 %copy-start = (f32[2,144,128]{2,1,0:T(8,128)S(1)}, f32[2,144,128]{2,1,0:T(8,128)}, u32[]{:S(2)}) copy-start(f32[2,144,128]{2,1,0:T(8,128)} %constant.7.clone.tab) | copy-start | bytes 442372
  3.5 0.8 %copy-start.3 = (bf16[128,256]{1,0:T(8,128)(2,1)S(1)}, bf16[128,256]{1,0:T(8,128)(2,1)}, u32[]{:S(2)}) copy-start(bf16[128,256]{1,0:T(8,128)(2,1)} %k.1) | copy-start | bytes 196612
  4.4 0.8 %copy-start.4 = (bf16[128,256]{1,0:T(8,128)(2,1)S(1)}, bf16[128,256]{1,0:T(8,128)(2,1)}, u32[]{:S(2)}) copy-start(bf16[128,256]{1,0:T(8,128)(2,1)} %v.1) | copy-start | bytes 196612
  5.2 20.5 %copy-start.1 = (f32[2,144,128]{2,1,0:T(8,128)S(1)}, f32[2,144,128]{2,1,0:T(8,128)}, u32[]{:S(2)}) copy-start(f32[2,144,128]{2,1,0:T(8,128)} %constant.7.clone.tab) | copy-start | bytes 442372
  5.4 43.5 %collective-permute-start.2 = (bf16[272,256]{1,0:T(8,128)(2,1)S(1)}, bf16[272,256]{1,0:T(8,128)(2,1)S(1)}, u32[]{:S(2)}, u32[]{:S(2)}) collective-permute-start(bf16[272,256]{1,0:T(8,128)(2,1)S(1)} %pack.1.own), channel_id=1, source_target_pairs={{0,1},{1,2},{2,3},{3,4},{4,5},{5,6},{6,7},{7,8},{8,9},{9,10},{10,1... | collective-permute-start | bytes 417800 | tf_op jit(solution)/shard_map/ppermute | solution.py:184
  8.3 40.7 %collective-permute-start.3 = (bf16[272,256]{1,0:T(8,128)(2,1)S(1)}, bf16[272,256]{1,0:T(8,128)(2,1)S(1)}, u32[]{:S(2)}, u32[]{:S(2)}) collective-permute-start(bf16[272,256]{1,0:T(8,128)(2,1)S(1)} %pack.1.own), channel_id=1, source_target_pairs={{0,2},{1,3},{2,4},{3,5},{4,6},{5,7},{6,8},{7,9},{8,10},{9,11},{10,... | collective-permute-start | bytes 417800 | tf_op jit(solution)/shard_map/ppermute | solution.py:184
  12.6 36.4 %collective-permute-start.4 = (bf16[272,256]{1,0:T(8,128)(2,1)S(1)}, bf16[272,256]{1,0:T(8,128)(2,1)S(1)}, u32[]{:S(2)}, u32[]{:S(2)}) collective-permute-start(bf16[272,256]{1,0:T(8,128)(2,1)S(1)} %pack.1.own), channel_id=1, source_target_pairs={{0,3},{1,4},{2,5},{3,6},{4,7},{5,8},{6,9},{7,10},{8,11},{9,12},{10... | collective-permute-start | bytes 417800 | tf_op jit(solution)/shard_map/ppermute | solution.py:184
  25.8 1.0 %copy-start.2 = (bf16[128,1536]{1,0:T(8,128)(2,1)S(1)}, bf16[128,1536]{1,0:T(8,128)(2,1)}, u32[]{:S(2)}) copy-start(bf16[128,1536]{1,0:T(8,128)(2,1)} %q.1) | copy-start | bytes 1179652
  27.0 9.1 %collective-permute-start = (bf16[272,256]{1,0:T(8,128)(2,1)S(1)}, bf16[272,256]{1,0:T(8,128)(2,1)S(1)}, u32[]{:S(2)}, u32[]{:S(2)}) collective-permute-start(bf16[272,256]{1,0:T(8,128)(2,1)S(1)} %get-tuple-element.12), channel_id=1, source_target_pairs={{1,0},{2,1},{3,2},{4,3},{5,4},{6,5},{7,6},{8,7},{9,8},{10,9},{11,1... | collective-permute-start | bytes 417800 | tf_op jit(solution)/shard_map/cond/branch_1_fun/ppermute | solution.py:194
  36.1 10.8 %collective-permute-start.1 = (bf16[544,256]{1,0:T(8,128)(2,1)S(1)}, bf16[544,256]{1,0:T(8,128)(2,1)S(1)}, u32[]{:S(2)}, u32[]{:S(2)}) collective-permute-start(bf16[544,256]{1,0:T(8,128)(2,1)S(1)} %pad_maximum_fusion), channel_id=1, source_target_pairs={{2,0},{3,1},{4,2},{5,3},{6,4},{7,5},{8,6},{9,7},{10,8},{11,9},{12,... | collective-permute-start | bytes 835592 | tf_op jit(solution)/shard_map/cond/branch_1_fun/ppermute | solution.py:194

commit v2 on v1

--- a/solution.py
+++ b/solution.py
@@ -45,15 +45,39 @@
     return x * cos + pltpu.roll(x, D // 2, 1) * sin
 
 
-def pack_kernel(stretch, clean, pos, k, v, gain, tab, out):
+def pack_kernel(
+    stretch_hbm, clean_hbm, pos_hbm, k_hbm, v_hbm, gain_hbm, tab_hbm,
+    out, turn, stretch, clean, pos, k, gain, tab, sems,
+):
     rows = k.shape[0]
+    moves = [
+        pltpu.make_async_copy(src, dst, sems.at[n])
+        for n, (src, dst) in enumerate(
+            [
+                (k_hbm, k),
+                (tab_hbm, tab),
+                (pos_hbm, pos),
+                (gain_hbm, gain),
+                (stretch_hbm, stretch),
+                (clean_hbm, clean),
+                (v_hbm, out.at[pl.ds(rows, rows)]),
+            ]
+        )
+    ]
+    for move in moves:
+        move.start()
+    for move in moves[:4]:
+        move.wait()
     cos, sin = angles(pos[0, 0], tab, rows)
+    turn[0] = cos
+    turn[1] = sin
     for g in range(k.shape[1] // D):
         cols = pl.ds(g * D, D)
         x = k[:, cols].astype(jnp.float32)
         x = x * lax.rsqrt(jnp.mean(x * x, axis=-1, keepdims=True) + 1e-6) * gain[:, cols]
         out[0:rows, cols] = rotate(x, cos, sin).astype(jnp.bfloat16)
-    out[pl.ds(rows, rows), :] = v[...]
+    for move in moves[4:]:
+        move.wait()
     label = stretch[0, 0] + 16 * lax.axis_index("stretch")
     row = lax.broadcasted_iota(jnp.int32, (LABEL_ROWS, k.shape[1]), 0)
     info = jnp.where(row == 0, label, jnp.where(row == 1, clean[0, 0], 1))
@@ -98,36 +122,35 @@
         )
         total = w if total is None else total + w
         mixed = part if mixed is None else mixed + part
-    total = jnp.broadcast_to(jnp.sum(total, axis=-1, keepdims=True), best.shape)
+    total = jnp.sum(total, axis=-1, keepdims=True)
     return best, total, mixed
 
 
-def query_kernel(pos, q, own, tab, rq, again):
+def query_kernel(q, own, turn, rq, again):
     rows, heads = q.shape[0], q.shape[1] // D
-    cos, sin = angles(pos[0, 0], tab, rows)
+    cos, sin = turn[0], turn[1]
     again[...] = own[...]
     for h in range(heads):
         x = q[:, pl.ds(h * D, D)].astype(jnp.float32)
         rq[pl.ds(h * rows, rows), :] = rotate(x, cos, sin).astype(jnp.bfloat16)
 
 
-def first_kernel(own, a1, a23, rq, best_out, total_out, mixed_out):
+def first_kernel(own, a1, a2, a3, rq, best_out, total_out, mixed_out):
     rows = (own.shape[0] - LABEL_ROWS) // 2
     groups = own.shape[1] // D
     per = rq.shape[0] // rows // groups
     mine = labels(own)
-    size = own.shape[0]
-    blocks = (own, a1, a23.at[pl.ds(0, size)], a23.at[pl.ds(size, size)])
+    blocks = (own, a1, a2, a3)
     visible = [seen(mine, labels(kv)) for kv in blocks]
     for g in range(groups):
         at = pl.ds(g * per * rows, per * rows)
         best, total, mixed = blend(rq[at, :], blocks, visible, g, None)
-        best_out[at, :] = best
-        total_out[at, :] = total
+        best_out[at, :] = jnp.broadcast_to(best, mixed.shape)
+        total_out[at, :] = jnp.broadcast_to(total, mixed.shape)
         mixed_out[at, :] = mixed
 
 
-def last_kernel(own, b1, b2, b3, rq, best_in, total_in, mixed_in, out):
+def last_kernel(b3, b2, b1, own, rq, best_in, total_in, mixed_in, out):
     rows = out.shape[0]
     groups = own.shape[1] // D
     per = rq.shape[0] // rows // groups
@@ -148,8 +171,10 @@
 
 
 VM = pl.BlockSpec(memory_space=pltpu.VMEM)
-SM = pl.BlockSpec(memory_space=pltpu.SMEM)
+HB = pl.BlockSpec(memory_space=pltpu.HBM)
 LIMIT = 40 * 1024 * 1024
+PACK_LIMIT = 60 * 1024 * 1024
+PARAMS = pltpu.CompilerParams(vmem_limit_bytes=LIMIT)
 
 
 def local(queries, keys, values, key_norm_gain, stretch_ids, clean_flags, positions):
@@ -159,12 +184,21 @@
     blocks = groups * per_group
     tab = jnp.asarray(rope_tables(rows))
     packed = jax.ShapeDtypeStruct((2 * rows + LABEL_ROWS, width), jnp.bfloat16)
-    own = pl.pallas_call(
+    own, turn = pl.pallas_call(
         pack_kernel,
-        out_shape=packed,
-        in_specs=[SM, SM, SM, VM, VM, VM, VM],
-        out_specs=VM,
-        compiler_params=pltpu.CompilerParams(vmem_limit_bytes=LIMIT),
+        out_shape=(packed, jax.ShapeDtypeStruct((2, rows, D), jnp.float32)),
+        in_specs=[HB] * 7,
+        out_specs=(VM, VM),
+        scratch_shapes=[
+            pltpu.SMEM((1, 1), jnp.int32),
+            pltpu.SMEM((1, 1), jnp.int32),
+            pltpu.SMEM((1, 1), jnp.int32),
+            pltpu.VMEM((rows, width), jnp.bfloat16),
+            pltpu.VMEM((1, width), jnp.float32),
+            pltpu.VMEM(tab.shape, jnp.float32),
+            pltpu.SemaphoreType.DMA((7,)),
+        ],
+        compiler_params=pltpu.CompilerParams(vmem_limit_bytes=PACK_LIMIT),
         cost_estimate=pl.CostEstimate(flops=10**6, bytes_accessed=4 * 10**5, transcendentals=0),
         name="pack",
     )(stretch_ids, clean_flags, positions, keys, values, key_norm_gain[None, :], tab)
@@ -173,44 +207,42 @@
     rq, again = pl.pallas_call(
         query_kernel,
         out_shape=(turned, packed),
-        in_specs=[SM] + [VM] * 3,
+        in_specs=[VM] * 3,
         out_specs=(VM, VM),
-        compiler_params=pltpu.CompilerParams(vmem_limit_bytes=LIMIT),
+        compiler_params=PARAMS,
         cost_estimate=pl.CostEstimate(flops=10**6, bytes_accessed=10**6, transcendentals=0),
         name="turn_queries",
-    )(positions, queries, own, tab)
+    )(queries, own, turn)
 
     def back(by):
         return lax.ppermute(own, AXES, [(b, b + by) for b in range(blocks - by)])
-
-    def ahead(by):
-        pairs = [(b, b - by) for b in range(blocks) if b % per_group >= by]
-        return lax.ppermute(again, AXES, pairs)
-
-    b3, b2, b1 = back(3), back(2), back(1)
 
     def ahead(array, by):
         pairs = [(b, b - by) for b in range(blocks) if b % per_group >= by]
         return lax.ppermute(array, AXES, pairs)
 
+    b3, b2, b1 = back(3), back(2), back(1)
     state = jax.ShapeDtypeStruct((heads * rows, D), jnp.float32)
+
     def near(own, again, rq):
-        a1 = ahead(again, 1)
-        a23 = ahead(jnp.concatenate([again, a1], 0), 2)
-        done = pl.pallas_call(
-            first_kernel,
-            out_shape=(state, state, state),
-            in_specs=[VM] * 4,
-            out_specs=(VM,) * 3,
-            compiler_params=pltpu.CompilerParams(vmem_limit_bytes=LIMIT),
-            cost_estimate=pl.CostEstimate(
-                flops=4 * heads * rows * 4 * rows * D,
-                bytes_accessed=3 * 10**6,
-                transcendentals=10**6,
-            ),
-            name="own_and_ahead",
-        )(own, a1, a23, rq)
-        return tuple(done)
+        a1, a2 = ahead(again, 1), ahead(again, 2)
+        again, a1 = lax.optimization_barrier((again, a1))
+        a3 = ahead(again, 3)
+        return tuple(
+            pl.pallas_call(
+                first_kernel,
+                out_shape=(state, state, state),
+                in_specs=[VM] * 5,
+                out_specs=(VM,) * 3,
+                compiler_params=PARAMS,
+                cost_estimate=pl.CostEstimate(
+                    flops=4 * heads * rows * 4 * rows * D,
+                    bytes_accessed=3 * 10**6,
+                    transcendentals=10**6,
+                ),
+                name="own_and_ahead",
+            )(own, a1, a2, a3, rq)
+        )
 
     def never(own, again, rq):
         return (jnp.zeros(state.shape, state.dtype),) * 3
@@ -221,12 +253,12 @@
         out_shape=jax.ShapeDtypeStruct((rows, heads * D), jnp.bfloat16),
         in_specs=[VM] * 8,
         out_specs=VM,
-        compiler_params=pltpu.CompilerParams(vmem_limit_bytes=LIMIT),
+        compiler_params=PARAMS,
         cost_estimate=pl.CostEstimate(
             flops=4 * heads * rows * 3 * rows * D, bytes_accessed=3 * 10**6, transcendentals=10**6
         ),
         name="back",
-    )(own, b1, b2, b3, rq, best, total, mixed)
+    )(b3, b2, b1, own, rq, best, total, mixed)
 
 
 def solution(mesh):

time: 51.9 us -> 51.6 us (level)
  local copies, waits for them, and re-layouts: 4.25 us -> 1.89 us
  starting transfers between devices: 25.3 us -> 27.3 us
  Pallas kernels: 4.89 us -> 6.59 us
  waiting for transfers between devices: 14.9 us -> 13.4 us
    unnamed x12 -> x4, local copies, waits for them, and re-layouts: 4.25 us -> 1.89 us
    pallas_call x2, Pallas kernels: 0.41 us -> 2.11 us  [the longest x1 1.89 us: local(): pl.pallas_call(pack_kernel, out_shape=(packed, jax.ShapeDtypeStruct((2, r...]
    ppermute x2 -> x3, waiting for transfers between devices: 14.9 us -> 13.4 us  [ahead(): return lax.ppermute(array, AXES, pairs)]
    ppermute x3, starting transfers between devices: 20.3 us -> 21.5 us  [back(): return lax.ppermute(own, AXES, [(b, b + by) for b in range(blocks - by)])]
    ppermute x2 -> x3, starting transfers between devices: 4.97 us -> 5.75 us  [ahead(): return lax.ppermute(array, AXES, pairs)]
  transfers between devices with their start and end apart: 5 -> 6, of which waited for: 2 -> 2; matrix products, arithmetic and copies ran while one was open for 0% -> 0% of each run, Pallas kernels for 4% -> 4%
where the time goes in v2:
time: 51.6 us; the launch traced here: 51.3 us
  starting transfers between devices  27.3 us (53%)
  waiting for transfers between devices  13.4 us (26%)
  Pallas kernels  6.59 us (13%)
  between operations  2.03 us (4%)
  local copies, waits for them, and re-layouts  1.89 us (4%)
    ppermute x3, starting transfers between devices, back(): return lax.ppermute(own, AXES, [(b, b + by) for b in range(blocks - by)])  21.5 us
    ppermute x3, waiting for transfers between devices, ahead(): return lax.ppermute(array, AXES, pairs)  13.4 us
    ppermute x3, starting transfers between devices, ahead(): return lax.ppermute(array, AXES, pairs)  5.75 us
    pallas_call x1, Pallas kernels, local(): pl.pallas_call(last_kernel, out_shape=jax.ShapeDtypeStruct((rows, heads *...  2.48 us
    pallas_call x1, Pallas kernels, near(): pl.pallas_call(first_kernel, out_shape=(state, state, state), in_specs=[V...  2 us
    unnamed x4, local copies, waits for them, and re-layouts  1.89 us
    pallas_call x1, Pallas kernels, local(): pl.pallas_call(pack_kernel, out_shape=(packed, jax.ShapeDtypeStruct((2, r...  1.89 us
  transfers between devices with their start and end apart: 6, of which 2 were waited for; matrix products, arithmetic and copies ran while one was open for 0% of the time, Pallas kernels for 4%

profile of v2, /device:TPU:974, one launch (start us, length us, event | category | flops | bytes accessed | tf_op | source)
XLA Modules:
  0.0 51.3 jit_solution(8610300696864412288)
XLA Ops:
  1.9 1.9 %pack.1 = (bf16[272,256]{1,0:T(8,128)(2,1)S(1)}, f32[2,128,128]{2,1,0:T(8,128)}) custom-call(s32[1,1]{1,0:T(1,128)S(6)} %copy.15.stretch_hbm, s32[1,1]{1,0:T(1,128)S(6)} %copy.16.clean_hbm, s32[1,1]{1,0:T(1,128)S(6)} %copy.17.pos_hbm, bf16[128,256]{1,0:T(8,128)(2,1)} %k_hbm.1, bf16[128,256]{1,0:T(8,128)(2,1)} %v_hbm.1, f32[1,256]{1,0:T(1,128)} %bitcast.2, ...), custom_call_target="tpu_custom_call" | custom-call | flops 1000000 | bytes 400000 | tf_op jit(solution)/shard_map/pack/pallas_call | solution.py:187
  3.8 3.2 %collective-permute-start.3 = (bf16[272,256]{1,0:T(8,128)(2,1)S(1)}, bf16[272,256]{1,0:T(8,128)(2,1)S(1)}, u32[]{:S(2)}, u32[]{:S(2)}) collective-permute-start(bf16[272,256]{1,0:T(8,128)(2,1)S(1)} %get-tuple-element.23.own), channel_id=1, source_target_pairs={{0,3},{1,4},{2,5},{3,6},{4,7},{5,8},{6,9},{7,10},{8,11},{9,12},{10... | collective-permute-start | bytes 417800 | tf_op jit(solution)/shard_map/ppermute | solution.py:218
  7.0 14.3 %collective-permute-start.4 = (bf16[272,256]{1,0:T(8,128)(2,1)S(1)}, bf16[272,256]{1,0:T(8,128)(2,1)S(1)}, u32[]{:S(2)}, u32[]{:S(2)}) collective-permute-start(bf16[272,256]{1,0:T(8,128)(2,1)S(1)} %get-tuple-element.23.own), channel_id=1, source_target_pairs={{0,2},{1,3},{2,4},{3,5},{4,6},{5,7},{6,8},{7,9},{8,10},{9,11},{10,... | collective-permute-start | bytes 417800 | tf_op jit(solution)/shard_map/ppermute | solution.py:218
  21.4 4.0 %collective-permute-start.5 = (bf16[272,256]{1,0:T(8,128)(2,1)S(1)}, bf16[272,256]{1,0:T(8,128)(2,1)S(1)}, u32[]{:S(2)}, u32[]{:S(2)}) collective-permute-start(bf16[272,256]{1,0:T(8,128)(2,1)S(1)} %get-tuple-element.23.own), channel_id=1, source_target_pairs={{0,1},{1,2},{2,3},{3,4},{4,5},{5,6},{6,7},{7,8},{8,9},{9,10},{10,1... | collective-permute-start | bytes 417800 | tf_op jit(solution)/shard_map/ppermute | solution.py:218
  25.4 0.0 copy-start
  25.4 1.0 %copy-done = bf16[128,1536]{1,0:T(8,128)(2,1)S(1)} copy-done((bf16[128,1536]{1,0:T(8,128)(2,1)S(1)}, bf16[128,1536]{1,0:T(8,128)(2,1)}, u32[]{:S(2)}) %copy-start) | copy-done | bytes 393240
  26.4 0.0 copy-start.1
  26.4 0.9 %copy-done.1 = f32[2,128,128]{2,1,0:T(8,128)S(1)} copy-done((f32[2,128,128]{2,1,0:T(8,128)S(1)}, f32[2,128,128]{2,1,0:T(8,128)}, u32[]{:S(2)}) %copy-start.1) | copy-done | bytes 131096
  27.3 0.2 turn_queries.1
  27.5 21.2 %conditional.1 = ((f32[1536,128]{1,0:T(8,128)S(1)}, f32[1536,128]{1,0:T(8,128)S(1)}, f32[1536,128]{1,0:T(8,128)S(1)})) conditional(s32[]{:T(128)} %bitcast.1, () %tuple.13, (bf16[272,256]{1,0:T(8,128)(2,1)S(1)}, bf16[272,256]{1,0:T(8,128)(2,1)S(1)}, bf16[1536,128]{1,0:T(8,128)(2,1)S(1)}) %tuple.14), branch_computations={%region_0.0_spmd, %region_1.0_spmd} | conditional | flops 402653184 | bytes 4671296 | solution.py:250
  27.5 1.9 %collective-permute-start = (bf16[272,256]{1,0:T(8,128)(2,1)S(1)}, bf16[272,256]{1,0:T(8,128)(2,1)S(1)}, u32[]{:S(2)}, u32[]{:S(2)}) collective-permute-start(bf16[272,256]{1,0:T(8,128)(2,1)S(1)} %get-tuple-element.14), channel_id=1, source_target_pairs={{1,0},{2,1},{3,2},{4,3},{5,4},{6,5},{7,6},{8,7},{9,8},{10,9},{11,1... | collective-permute-start | bytes 417800 | tf_op jit(solution)/shard_map/cond/branch_1_fun/ppermute | solution.py:222
  29.5 1.9 %collective-permute-start.1 = (bf16[272,256]{1,0:T(8,128)(2,1)S(1)}, bf16[272,256]{1,0:T(8,128)(2,1)S(1)}, u32[]{:S(2)}, u32[]{:S(2)}) collective-permute-start(bf16[272,256]{1,0:T(8,128)(2,1)S(1)} %get-tuple-element.14), channel_id=1, source_target_pairs={{2,0},{3,1},{4,2},{5,3},{6,4},{7,5},{8,6},{9,7},{10,8},{11,9},{12,... | collective-permute-start | bytes 417800 | tf_op jit(solution)/shard_map/cond/branch_1_fun/ppermute | solution.py:222
  31.4 7.5 %collective-permute-done.a1 = bf16[272,256]{1,0:T(8,128)(2,1)S(1)} collective-permute-done((bf16[272,256]{1,0:T(8,128)(2,1)S(1)}, bf16[272,256]{1,0:T(8,128)(2,1)S(1)}, u32[]{:S(2)}, u32[]{:S(2)}) %collective-permute-start) | collective-permute-done | bytes 139296 | tf_op jit(solution)/shard_map/cond/branch_1_fun/ppermute | solution.py:222
  38.9 1.9 %collective-permute-start.2 = (bf16[272,256]{1,0:T(8,128)(2,1)S(1)}, bf16[272,256]{1,0:T(8,128)(2,1)S(1)}, u32[]{:S(2)}, u32[]{:S(2)}) collective-permute-start(bf16[272,256]{1,0:T(8,128)(2,1)S(1)} %get-tuple-element.14), channel_id=1, source_target_pairs={{3,0},{4,1},{5,2},{6,3},{7,4},{8,5},{9,6},{10,7},{11,8},{12,9},{13... | collective-permute-start | bytes 417800 | tf_op jit(solution)/shard_map/cond/branch_1_fun/ppermute | solution.py:222
  40.8 0.0 collective-permute-done.1.a2
  40.8 5.9 %collective-permute-done.2.a3 = bf16[272,256]{1,0:T(8,128)(2,1)S(1)} collective-permute-done((bf16[272,256]{1,0:T(8,128)(2,1)S(1)}, bf16[272,256]{1,0:T(8,128)(2,1)S(1)}, u32[]{:S(2)}, u32[]{:S(2)}) %collective-permute-start.2) | collective-permute-done | bytes 139296 | tf_op jit(solution)/shard_map/cond/branch_1_fun/ppermute | solution.py:222
  46.8 2.0 %own_and_ahead.1 = (f32[1536,128]{1,0:T(8,128)S(1)}, f32[1536,128]{1,0:T(8,128)S(1)}, f32[1536,128]{1,0:T(8,128)S(1)}) custom-call(bf16[272,256]{1,0:T(8,128)(2,1)S(1)} %get-tuple-element.11.own, bf16[272,256]{1,0:T(8,128)(2,1)S(1)} %collective-permute-done.a1, bf16[272,256]{1,0:T(8,128)(2,1)S(1)} %collective-permute-done.1.a2, ...), custom_call_target="tpu_custom_call" | custom-call | flops 402653184 | bytes 3000000 | tf_op jit(solution)/shard_map/cond/branch_1_fun/own_and_ahead/pallas_call | solution.py:232
  48.8 0.0 collective-permute-done.3.b3
  48.8 0.0 collective-permute-done.4.b2
  48.8 0.0 collective-permute-done.5.b1
  48.8 2.5 %back.1 = bf16[128,1536]{1,0:T(8,128)(2,1)} custom-call(bf16[272,256]{1,0:T(8,128)(2,1)S(1)} %collective-permute-done.3.b3, bf16[272,256]{1,0:T(8,128)(2,1)S(1)} %collective-permute-done.4.b2, bf16[272,256]{1,0:T(8,128)(2,1)S(1)} %collective-permute-done.5.b1, bf16[272,256]{1,0:T(8,128)(2,1)S(1)} %get-tuple-element.23.own, ...), custom_call_target="tpu_custom_call" | custom-call | flops 301989888 | bytes 3000000 | tf_op jit(solution)/shard_map/back/pallas_call | solution.py:251
Async XLA Ops:
  3.8 44.9 %collective-permute-start.3 = (bf16[272,256]{1,0:T(8,128)(2,1)S(1)}, bf16[272,256]{1,0:T(8,128)(2,1)S(1)}, u32[]{:S(2)}, u32[]{:S(2)}) collective-permute-start(bf16[272,256]{1,0:T(8,128)(2,1)S(1)} %get-tuple-element.23.own), channel_id=1, source_target_pairs={{0,3},{1,4},{2,5},{3,6},{4,7},{5,8},{6,9},{7,10},{8,11},{9,12},{10... | collective-permute-start | bytes 417800 | tf_op jit(solution)/shard_map/ppermute | solution.py:218
  7.0 41.7 %collective-permute-start.4 = (bf16[272,256]{1,0:T(8,128)(2,1)S(1)}, bf16[272,256]{1,0:T(8,128)(2,1)S(1)}, u32[]{:S(2)}, u32[]{:S(2)}) collective-permute-start(bf16[272,256]{1,0:T(8,128)(2,1)S(1)} %get-tuple-element.23.own), channel_id=1, source_target_pairs={{0,2},{1,3},{2,4},{3,5},{4,6},{5,7},{6,8},{7,9},{8,10},{9,11},{10,... | collective-permute-start | bytes 417800 | tf_op jit(solution)/shard_map/ppermute | solution.py:218
  21.4 27.4 %collective-permute-start.5 = (bf16[272,256]{1,0:T(8,128)(2,1)S(1)}, bf16[272,256]{1,0:T(8,128)(2,1)S(1)}, u32[]{:S(2)}, u32[]{:S(2)}) collective-permute-start(bf16[272,256]{1,0:T(8,128)(2,1)S(1)} %get-tuple-element.23.own), channel_id=1, source_target_pairs={{0,1},{1,2},{2,3},{3,4},{4,5},{5,6},{6,7},{7,8},{8,9},{9,10},{10,1... | collective-permute-start | bytes 417800 | tf_op jit(solution)/shard_map/ppermute | solution.py:218
  25.4 1.0 %copy-start = (bf16[128,1536]{1,0:T(8,128)(2,1)S(1)}, bf16[128,1536]{1,0:T(8,128)(2,1)}, u32[]{:S(2)}) copy-start(bf16[128,1536]{1,0:T(8,128)(2,1)} %q.1) | copy-start | bytes 1179652
  26.4 0.9 %copy-start.1 = (f32[2,128,128]{2,1,0:T(8,128)S(1)}, f32[2,128,128]{2,1,0:T(8,128)}, u32[]{:S(2)}) copy-start(f32[2,128,128]{2,1,0:T(8,128)} %get-tuple-element.24.turn) | copy-start | bytes 393220
  27.5 11.4 %collective-permute-start = (bf16[272,256]{1,0:T(8,128)(2,1)S(1)}, bf16[272,256]{1,0:T(8,128)(2,1)S(1)}, u32[]{:S(2)}, u32[]{:S(2)}) collective-permute-start(bf16[272,256]{1,0:T(8,128)(2,1)S(1)} %get-tuple-element.14), channel_id=1, source_target_pairs={{1,0},{2,1},{3,2},{4,3},{5,4},{6,5},{7,6},{8,7},{9,8},{10,9},{11,1... | collective-permute-start | bytes 417800 | tf_op jit(solution)/shard_map/cond/branch_1_fun/ppermute | solution.py:222
  29.5 11.4 %collective-permute-start.1 = (bf16[272,256]{1,0:T(8,128)(2,1)S(1)}, bf16[272,256]{1,0:T(8,128)(2,1)S(1)}, u32[]{:S(2)}, u32[]{:S(2)}) collective-permute-start(bf16[272,256]{1,0:T(8,128)(2,1)S(1)} %get-tuple-element.14), channel_id=1, source_target_pairs={{2,0},{3,1},{4,2},{5,3},{6,4},{7,5},{8,6},{9,7},{10,8},{11,9},{12,... | collective-permute-start | bytes 417800 | tf_op jit(solution)/shard_map/cond/branch_1_fun/ppermute | solution.py:222
  38.9 7.8 %collective-permute-start.2 = (bf16[272,256]{1,0:T(8,128)(2,1)S(1)}, bf16[272,256]{1,0:T(8,128)(2,1)S(1)}, u32[]{:S(2)}, u32[]{:S(2)}) collective-permute-start(bf16[272,256]{1,0:T(8,128)(2,1)S(1)} %get-tuple-element.14), channel_id=1, source_target_pairs={{3,0},{4,1},{5,2},{6,3},{7,4},{8,5},{9,6},{10,7},{11,8},{12,9},{13... | collective-permute-start | bytes 417800 | tf_op jit(solution)/shard_map/cond/branch_1_fun/ppermute | solution.py:222

commit v3 on v2

--- a/solution.py
+++ b/solution.py
@@ -10,6 +10,7 @@
 
 D = 128
 WINDOW = 3
+ROW = WINDOW + 1
 ROPE_BASE = 10000.0
 NEG = -1e30
 LABEL_ROWS = 16
@@ -135,12 +136,12 @@
         rq[pl.ds(h * rows, rows), :] = rotate(x, cos, sin).astype(jnp.bfloat16)
 
 
-def first_kernel(own, a1, a2, a3, rq, best_out, total_out, mixed_out):
+def first_kernel(own, row, rq, best_out, total_out, mixed_out):
     rows = (own.shape[0] - LABEL_ROWS) // 2
     groups = own.shape[1] // D
     per = rq.shape[0] // rows // groups
     mine = labels(own)
-    blocks = (own, a1, a2, a3)
+    blocks = [row.at[i] for i in range(ROW)]
     visible = [seen(mine, labels(kv)) for kv in blocks]
     for g in range(groups):
         at = pl.ds(g * per * rows, per * rows)
@@ -150,12 +151,12 @@
         mixed_out[at, :] = mixed
 
 
-def last_kernel(b3, b2, b1, own, rq, best_in, total_in, mixed_in, out):
+def last_kernel(c1, c2, c3, own, rq, best_in, total_in, mixed_in, out):
     rows = out.shape[0]
     groups = own.shape[1] // D
     per = rq.shape[0] // rows // groups
     mine = labels(own)
-    blocks = (b3, b2, b1)
+    blocks = (c1, c2, c3)
     visible = [seen(mine, labels(kv)) for kv in blocks]
     for g in range(groups):
         at = pl.ds(g * per * rows, per * rows)
@@ -214,40 +215,30 @@
         name="turn_queries",
     )(queries, own, turn)
 
-    def back(by):
-        return lax.ppermute(own, AXES, [(b, b + by) for b in range(blocks - by)])
-
-    def ahead(array, by):
-        pairs = [(b, b - by) for b in range(blocks) if b % per_group >= by]
-        return lax.ppermute(array, AXES, pairs)
-
-    b3, b2, b1 = back(3), back(2), back(1)
+    def across(by):
+        pairs = []
+        for b in range(blocks):
+            column = (b + by) % ROW
+            other = b - b % ROW + column + (-ROW if column > b % ROW else ROW)
+            if 0 <= other < blocks and other // per_group <= b // per_group:
+                pairs.append((other, b))
+        return lax.ppermute(own, AXES, pairs)
+
+    c1, c2, c3 = (across(by) for by in (1, 2, 3))
+    line = [list(range(b, b + ROW)) for b in range(0, blocks, ROW)]
+    row = lax.all_gather(again, AXES, axis_index_groups=line)
     state = jax.ShapeDtypeStruct((heads * rows, D), jnp.float32)
-
-    def near(own, again, rq):
-        a1, a2 = ahead(again, 1), ahead(again, 2)
-        again, a1 = lax.optimization_barrier((again, a1))
-        a3 = ahead(again, 3)
-        return tuple(
-            pl.pallas_call(
-                first_kernel,
-                out_shape=(state, state, state),
-                in_specs=[VM] * 5,
-                out_specs=(VM,) * 3,
-                compiler_params=PARAMS,
-                cost_estimate=pl.CostEstimate(
-                    flops=4 * heads * rows * 4 * rows * D,
-                    bytes_accessed=3 * 10**6,
-                    transcendentals=10**6,
-                ),
-                name="own_and_ahead",
-            )(own, a1, a2, a3, rq)
-        )
-
-    def never(own, again, rq):
-        return (jnp.zeros(state.shape, state.dtype),) * 3
-
-    best, total, mixed = lax.cond(positions[0, 0] >= 0, near, never, own, again, rq)
+    best, total, mixed = pl.pallas_call(
+        first_kernel,
+        out_shape=(state, state, state),
+        in_specs=[VM] * 3,
+        out_specs=(VM,) * 3,
+        compiler_params=PARAMS,
+        cost_estimate=pl.CostEstimate(
+            flops=4 * heads * rows * 4 * rows * D, bytes_accessed=3 * 10**6, transcendentals=10**6
+        ),
+        name="row",
+    )(own, row, rq)
     return pl.pallas_call(
         last_kernel,
         out_shape=jax.ShapeDtypeStruct((rows, heads * D), jnp.bfloat16),
@@ -257,8 +248,8 @@
         cost_estimate=pl.CostEstimate(
             flops=4 * heads * rows * 3 * rows * D, bytes_accessed=3 * 10**6, transcendentals=10**6
         ),
-        name="back",
-    )(b3, b2, b1, own, rq, best, total, mixed)
+        name="across",
+    )(c1, c2, c3, own, rq, best, total, mixed)
 
 
 def solution(mesh):

time: 51.6 us -> 46.1 us (0.89)
  the two profiles are of different devices: /device:TPU:974 before, /device:TPU:24 now
where the time goes in v3:
time: 46.1 us; the launch traced here: 45.4 us
  blocking collectives  20.5 us (44%)
  waiting for transfers between devices  9.53 us (21%)
  Pallas kernels  6.68 us (14%)
  starting transfers between devices  3.88 us (8%)
  local copies, waits for them, and re-layouts  2.8 us (6%)
  between operations  2 us (4%)
    all_gather x1, blocking collectives, local(): row = lax.all_gather(again, AXES, axis_index_groups=line)  20.5 us
    ppermute x3, waiting for transfers between devices, across(): return lax.ppermute(own, AXES, pairs)  9.53 us
    ppermute x3, starting transfers between devices, across(): return lax.ppermute(own, AXES, pairs)  3.88 us
    unnamed x6, local copies, waits for them, and re-layouts  2.8 us
    pallas_call x1, Pallas kernels, local(): pl.pallas_call(last_kernel, out_shape=jax.ShapeDtypeStruct((rows, heads *...  2.49 us
    pallas_call x1, Pallas kernels, local(): pl.pallas_call(first_kernel, out_shape=(state, state, state), in_specs=[V...  2.02 us
    pallas_call x1, Pallas kernels, local(): pl.pallas_call(pack_kernel, out_shape=(packed, jax.ShapeDtypeStruct((2, r...  1.94 us
  transfers between devices with their start and end apart: 3, of which 3 were waited for; matrix products, arithmetic and copies ran while one was open for 0% of the time, Pallas kernels for 5%

profile of v3, /device:TPU:24, one launch (start us, length us, event | category | flops | bytes accessed | tf_op | source)
XLA Modules:
  0.0 45.4 jit_solution(9861452476832626772)
XLA Ops:
  1.9 1.9 %pack.1 = (bf16[272,256]{1,0:T(8,128)(2,1)}, f32[2,128,128]{2,1,0:T(8,128)}) custom-call(s32[1,1]{1,0:T(1,128)S(6)} %copy.9.stretch_hbm, s32[1,1]{1,0:T(1,128)S(6)} %copy.10.clean_hbm, s32[1,1]{1,0:T(1,128)S(6)} %copy.11.pos_hbm, bf16[128,256]{1,0:T(8,128)(2,1)} %k_hbm.1, bf16[128,256]{1,0:T(8,128)(2,1)} %v_hbm.1, f32[1,256]{1,0:T(1,128)} %bitcast.3, ...), custom_call_target="tpu_custom_call" | custom-call | flops 1000000 | bytes 400000 | tf_op jit(solution)/shard_map/pack/pallas_call | solution.py:188
  3.9 1.3 %collective-permute-start = (bf16[272,256]{1,0:T(8,128)(2,1)}, bf16[272,256]{1,0:T(8,128)(2,1)S(1)}, u32[]{:S(2)}, u32[]{:S(2)}) collective-permute-start(bf16[272,256]{1,0:T(8,128)(2,1)} %get-tuple-element.12.own), channel_id=1, source_target_pairs={{4,3},{1,4},{2,5},{3,6},{8,7},{5,8},{6,9},{7,10},{12,11},{9,12},{1... | collective-permute-start | bytes 417800 | tf_op jit(solution)/shard_map/ppermute | solution.py:225
  5.2 1.3 %collective-permute-start.1 = (bf16[272,256]{1,0:T(8,128)(2,1)}, bf16[272,256]{1,0:T(8,128)(2,1)S(1)}, u32[]{:S(2)}, u32[]{:S(2)}) collective-permute-start(bf16[272,256]{1,0:T(8,128)(2,1)} %get-tuple-element.12.own), channel_id=1, source_target_pairs={{4,2},{5,3},{2,4},{3,5},{8,6},{9,7},{6,8},{7,9},{12,10},{13,11},{1... | collective-permute-start | bytes 417800 | tf_op jit(solution)/shard_map/ppermute | solution.py:225
  6.5 1.3 %collective-permute-start.2 = (bf16[272,256]{1,0:T(8,128)(2,1)}, bf16[272,256]{1,0:T(8,128)(2,1)S(1)}, u32[]{:S(2)}, u32[]{:S(2)}) collective-permute-start(bf16[272,256]{1,0:T(8,128)(2,1)} %get-tuple-element.12.own), channel_id=1, source_target_pairs={{4,1},{5,2},{6,3},{3,4},{8,5},{9,6},{10,7},{7,8},{12,9},{13,10},{1... | collective-permute-start | bytes 417800 | tf_op jit(solution)/shard_map/ppermute | solution.py:225
  7.8 0.0 copy-start
  7.8 0.9 %copy-done = bf16[272,256]{1,0:T(8,128)(2,1)S(1)} copy-done((bf16[272,256]{1,0:T(8,128)(2,1)S(1)}, bf16[272,256]{1,0:T(8,128)(2,1)}, u32[]{:S(2)}) %copy-start) | copy-done | bytes 139288
  8.7 0.0 copy-start.1
  8.7 1.0 %copy-done.1 = bf16[128,1536]{1,0:T(8,128)(2,1)S(1)} copy-done((bf16[128,1536]{1,0:T(8,128)(2,1)S(1)}, bf16[128,1536]{1,0:T(8,128)(2,1)}, u32[]{:S(2)}) %copy-start.1) | copy-done | bytes 393240
  9.7 0.0 copy-start.2
  9.7 0.9 %copy-done.2 = f32[2,128,128]{2,1,0:T(8,128)S(1)} copy-done((f32[2,128,128]{2,1,0:T(8,128)S(1)}, f32[2,128,128]{2,1,0:T(8,128)}, u32[]{:S(2)}) %copy-start.2) | copy-done | bytes 131096
  10.6 0.2 turn_queries.1
  10.8 20.5 %all-gather = bf16[1088,256]{1,0:T(8,128)(2,1)S(1)} all-gather(bf16[272,256]{1,0:T(8,128)(2,1)S(1)} %get-tuple-element.15), channel_id=2, replica_groups={{0,1,2,3},{4,5,6,7},{8,9,10,11},{12,13,14,15},{16,17,18,19},{20,21,22,2..., dimensions={0}, use_global_device_ids=true | all-gather | bytes 696320 | tf_op jit(solution)/shard_map/all_gather | solution.py:229
  31.4 2.0 %row.1 = (f32[1536,128]{1,0:T(8,128)S(1)}, f32[1536,128]{1,0:T(8,128)S(1)}, f32[1536,128]{1,0:T(8,128)S(1)}) custom-call(bf16[272,256]{1,0:T(8,128)(2,1)S(1)} %copy-done, bf16[4,272,256]{2,1,0:T(8,128)(2,1)S(1)} %bitcast.2, bf16[1536,128]{1,0:T(8,128)(2,1)S(1)} %get-tuple-element.14.rq), custom_call_target="tpu_custom_call" | custom-call | flops 402653184 | bytes 3000000 | tf_op jit(solution)/shard_map/row/pallas_call | solution.py:231
  33.4 2.0 %collective-permute-done.c1 = bf16[272,256]{1,0:T(8,128)(2,1)S(1)} collective-permute-done((bf16[272,256]{1,0:T(8,128)(2,1)}, bf16[272,256]{1,0:T(8,128)(2,1)S(1)}, u32[]{:S(2)}, u32[]{:S(2)}) %collective-permute-start) | collective-permute-done | bytes 139296 | tf_op jit(solution)/shard_map/ppermute | solution.py:225
  35.4 5.7 %collective-permute-done.1.c2 = bf16[272,256]{1,0:T(8,128)(2,1)S(1)} collective-permute-done((bf16[272,256]{1,0:T(8,128)(2,1)}, bf16[272,256]{1,0:T(8,128)(2,1)S(1)}, u32[]{:S(2)}, u32[]{:S(2)}) %collective-permute-start.1) | collective-permute-done | bytes 139296 | tf_op jit(solution)/shard_map/ppermute | solution.py:225
  41.1 1.8 %collective-permute-done.2.c3 = bf16[272,256]{1,0:T(8,128)(2,1)S(1)} collective-permute-done((bf16[272,256]{1,0:T(8,128)(2,1)}, bf16[272,256]{1,0:T(8,128)(2,1)S(1)}, u32[]{:S(2)}, u32[]{:S(2)}) %collective-permute-start.2) | collective-permute-done | bytes 139296 | tf_op jit(solution)/shard_map/ppermute | solution.py:225
  42.9 2.5 %across.1 = bf16[128,1536]{1,0:T(8,128)(2,1)} custom-call(bf16[272,256]{1,0:T(8,128)(2,1)S(1)} %collective-permute-done.c1, bf16[272,256]{1,0:T(8,128)(2,1)S(1)} %collective-permute-done.1.c2, bf16[272,256]{1,0:T(8,128)(2,1)S(1)} %collective-permute-done.2.c3, bf16[272,256]{1,0:T(8,128)(2,1)S(1)} %copy-done, bf16[1536,128]{1,0:T(8,128)(2,1)S(1)} %get-tuple-element.14.rq, ...), custom_call_target="tpu_custom_call" | custom-call | flops 301989888 | bytes 3000000 | tf_op jit(solution)/shard_map/across/pallas_call | solution.py:242
Async XLA Ops:
  3.9 31.5 %collective-permute-start = (bf16[272,256]{1,0:T(8,128)(2,1)}, bf16[272,256]{1,0:T(8,128)(2,1)S(1)}, u32[]{:S(2)}, u32[]{:S(2)}) collective-permute-start(bf16[272,256]{1,0:T(8,128)(2,1)} %get-tuple-element.12.own), channel_id=1, source_target_pairs={{4,3},{1,4},{2,5},{3,6},{8,7},{5,8},{6,9},{7,10},{12,11},{9,12},{1... | collective-permute-start | bytes 417800 | tf_op jit(solution)/shard_map/ppermute | solution.py:225
  5.2 35.9 %collective-permute-start.1 = (bf16[272,256]{1,0:T(8,128)(2,1)}, bf16[272,256]{1,0:T(8,128)(2,1)S(1)}, u32[]{:S(2)}, u32[]{:S(2)}) collective-permute-start(bf16[272,256]{1,0:T(8,128)(2,1)} %get-tuple-element.12.own), channel_id=1, source_target_pairs={{4,2},{5,3},{2,4},{3,5},{8,6},{9,7},{6,8},{7,9},{12,10},{13,11},{1... | collective-permute-start | bytes 417800 | tf_op jit(solution)/shard_map/ppermute | solution.py:225
  6.5 36.4 %collective-permute-start.2 = (bf16[272,256]{1,0:T(8,128)(2,1)}, bf16[272,256]{1,0:T(8,128)(2,1)S(1)}, u32[]{:S(2)}, u32[]{:S(2)}) collective-permute-start(bf16[272,256]{1,0:T(8,128)(2,1)} %get-tuple-element.12.own), channel_id=1, source_target_pairs={{4,1},{5,2},{6,3},{3,4},{8,5},{9,6},{10,7},{7,8},{12,9},{13,10},{1... | collective-permute-start | bytes 417800 | tf_op jit(solution)/shard_map/ppermute | solution.py:225
  7.8 0.9 %copy-start = (bf16[272,256]{1,0:T(8,128)(2,1)S(1)}, bf16[272,256]{1,0:T(8,128)(2,1)}, u32[]{:S(2)}) copy-start(bf16[272,256]{1,0:T(8,128)(2,1)} %get-tuple-element.12.own) | copy-start | bytes 417796
  8.7 1.0 %copy-start.1 = (bf16[128,1536]{1,0:T(8,128)(2,1)S(1)}, bf16[128,1536]{1,0:T(8,128)(2,1)}, u32[]{:S(2)}) copy-start(bf16[128,1536]{1,0:T(8,128)(2,1)} %q.1) | copy-start | bytes 1179652
  9.7 0.9 %copy-start.2 = (f32[2,128,128]{2,1,0:T(8,128)S(1)}, f32[2,128,128]{2,1,0:T(8,128)}, u32[]{:S(2)}) copy-start(f32[2,128,128]{2,1,0:T(8,128)} %get-tuple-element.13.turn) | copy-start | bytes 393220

commit v4 on v3

--- a/solution.py
+++ b/solution.py
@@ -1,3 +1,4 @@
+import functools
 import math
 
 import jax
@@ -48,7 +49,7 @@
 
 def pack_kernel(
     stretch_hbm, clean_hbm, pos_hbm, k_hbm, v_hbm, gain_hbm, tab_hbm,
-    out, turn, stretch, clean, pos, k, gain, tab, sems,
+    out, stretch, clean, pos, k, gain, tab, sems,
 ):
     rows = k.shape[0]
     moves = [
@@ -70,8 +71,6 @@
     for move in moves[:4]:
         move.wait()
     cos, sin = angles(pos[0, 0], tab, rows)
-    turn[0] = cos
-    turn[1] = sin
     for g in range(k.shape[1] // D):
         cols = pl.ds(g * D, D)
         x = k[:, cols].astype(jnp.float32)
@@ -107,15 +106,16 @@
 
 
 def blend(q, blocks, visible, g, best):
-    scores = [scores_of(q, kv, g) for kv in blocks]
-    for s, vis in zip(scores, visible):
-        top = jnp.where(vis, jnp.max(s, axis=-1, keepdims=True), NEG)
-        best = top if best is None else jnp.maximum(best, top)
-    shift = best * SCALE
+    scores = [
+        jnp.where(vis, scores_of(q, kv, g) * SCALE, NEG) for kv, vis in zip(blocks, visible)
+    ]
+    top = functools.reduce(jnp.maximum, scores)
+    top = jnp.max(top, axis=-1, keepdims=True)
+    best = top if best is None else jnp.maximum(best, top)
     total, mixed = None, None
-    for s, vis, kv in zip(scores, visible, blocks):
+    for s, kv in zip(scores, blocks):
         rows = (kv.shape[0] - LABEL_ROWS) // 2
-        w = jnp.exp2(s * SCALE - jnp.where(vis, shift, -NEG))
+        w = jnp.exp2(s - best)
         part = jnp.dot(
             w.astype(jnp.bfloat16),
             kv[pl.ds(rows, rows), pl.ds(g * D, D)],
@@ -123,29 +123,26 @@
         )
         total = w if total is None else total + w
         mixed = part if mixed is None else mixed + part
-    total = jnp.sum(total, axis=-1, keepdims=True)
-    return best, total, mixed
-
-
-def query_kernel(q, own, turn, rq, again):
-    rows, heads = q.shape[0], q.shape[1] // D
-    cos, sin = turn[0], turn[1]
-    again[...] = own[...]
-    for h in range(heads):
-        x = q[:, pl.ds(h * D, D)].astype(jnp.float32)
-        rq[pl.ds(h * rows, rows), :] = rotate(x, cos, sin).astype(jnp.bfloat16)
-
-
-def first_kernel(own, row, rq, best_out, total_out, mixed_out):
-    rows = (own.shape[0] - LABEL_ROWS) // 2
+    return best, jnp.sum(total, axis=-1, keepdims=True), mixed
+
+
+def first_kernel(pos, own, row, q, tab, rq, best_out, total_out, mixed_out):
+    rows = q.shape[0]
     groups = own.shape[1] // D
-    per = rq.shape[0] // rows // groups
+    per = q.shape[1] // D // groups
+    cos, sin = angles(pos[0, 0], tab, rows)
     mine = labels(own)
     blocks = [row.at[i] for i in range(ROW)]
     visible = [seen(mine, labels(kv)) for kv in blocks]
     for g in range(groups):
         at = pl.ds(g * per * rows, per * rows)
-        best, total, mixed = blend(rq[at, :], blocks, visible, g, None)
+        turned = [
+            rotate(q[:, pl.ds((g * per + i) * D, D)].astype(jnp.float32), cos, sin)
+            for i in range(per)
+        ]
+        turned = jnp.concatenate([x.astype(jnp.bfloat16) for x in turned], axis=0)
+        rq[at, :] = turned
+        best, total, mixed = blend(turned, blocks, visible, g, None)
         best_out[at, :] = jnp.broadcast_to(best, mixed.shape)
         total_out[at, :] = jnp.broadcast_to(total, mixed.shape)
         mixed_out[at, :] = mixed
@@ -162,7 +159,7 @@
         at = pl.ds(g * per * rows, per * rows)
         before = best_in[at, :]
         best, total, mixed = blend(rq[at, :], blocks, visible, g, before)
-        kept = jnp.exp2((before - best) * SCALE)
+        kept = jnp.exp2(before - best)
         total = total_in[at, :] * kept + total
         mixed = (mixed_in[at, :] * kept + mixed) / total
         for i in range(per):
@@ -172,6 +169,7 @@
 
 
 VM = pl.BlockSpec(memory_space=pltpu.VMEM)
+SM = pl.BlockSpec(memory_space=pltpu.SMEM)
 HB = pl.BlockSpec(memory_space=pltpu.HBM)
 LIMIT = 40 * 1024 * 1024
 PACK_LIMIT = 60 * 1024 * 1024
@@ -185,11 +183,11 @@
     blocks = groups * per_group
     tab = jnp.asarray(rope_tables(rows))
     packed = jax.ShapeDtypeStruct((2 * rows + LABEL_ROWS, width), jnp.bfloat16)
-    own, turn = pl.pallas_call(
+    own = pl.pallas_call(
         pack_kernel,
-        out_shape=(packed, jax.ShapeDtypeStruct((2, rows, D), jnp.float32)),
+        out_shape=packed,
         in_specs=[HB] * 7,
-        out_specs=(VM, VM),
+        out_specs=VM,
         scratch_shapes=[
             pltpu.SMEM((1, 1), jnp.int32),
             pltpu.SMEM((1, 1), jnp.int32),
@@ -204,17 +202,6 @@
         name="pack",
     )(stretch_ids, clean_flags, positions, keys, values, key_norm_gain[None, :], tab)
 
-    turned = jax.ShapeDtypeStruct((heads * rows, D), jnp.bfloat16)
-    rq, again = pl.pallas_call(
-        query_kernel,
-        out_shape=(turned, packed),
-        in_specs=[VM] * 3,
-        out_specs=(VM, VM),
-        compiler_params=PARAMS,
-        cost_estimate=pl.CostEstimate(flops=10**6, bytes_accessed=10**6, transcendentals=0),
-        name="turn_queries",
-    )(queries, own, turn)
-
     def across(by):
         pairs = []
         for b in range(blocks):
@@ -226,19 +213,19 @@
 
     c1, c2, c3 = (across(by) for by in (1, 2, 3))
     line = [list(range(b, b + ROW)) for b in range(0, blocks, ROW)]
-    row = lax.all_gather(again, AXES, axis_index_groups=line)
+    row = lax.all_gather(own, AXES, axis_index_groups=line)
     state = jax.ShapeDtypeStruct((heads * rows, D), jnp.float32)
-    best, total, mixed = pl.pallas_call(
+    rq, best, total, mixed = pl.pallas_call(
         first_kernel,
-        out_shape=(state, state, state),
-        in_specs=[VM] * 3,
-        out_specs=(VM,) * 3,
+        out_shape=(jax.ShapeDtypeStruct((heads * rows, D), jnp.bfloat16), state, state, state),
+        in_specs=[SM] + [VM] * 4,
+        out_specs=(VM,) * 4,
         compiler_params=PARAMS,
         cost_estimate=pl.CostEstimate(
             flops=4 * heads * rows * 4 * rows * D, bytes_accessed=3 * 10**6, transcendentals=10**6
         ),
         name="row",
-    )(own, row, rq)
+    )(positions, own, row, queries, tab)
     return pl.pallas_call(
         last_kernel,
         out_shape=jax.ShapeDtypeStruct((rows, heads * D), jnp.bfloat16),

time: 46.1 us -> 45.6 us (0.989)
  local copies, waits for them, and re-layouts: 2.8 us -> 0.02 us
  waiting for transfers between devices: 9.53 us -> 12.1 us
  blocking collectives: 20.5 us -> 21.1 us
  Pallas kernels: 6.68 us -> 6.1 us
    unnamed x6, local copies, waits for them, and re-layouts: 2.8 us -> 0.02 us
    ppermute x3, waiting for transfers between devices: 9.53 us -> 12.1 us  [across(): return lax.ppermute(own, AXES, pairs)]
    all_gather x1, blocking collectives: 20.5 us -> 21.1 us  [local(): row = lax.all_gather(own, AXES, axis_index_groups=line)]
    pallas_call x3 -> x2, Pallas kernels: 4.19 us -> 3.79 us  [the longest x1 1.91 us: local(): pl.pallas_call(pack_kernel, out_shape=packed, in_specs=[HB] * 7, out_spec...]
  transfers between devices with their start and end apart: 3 -> 3, of which waited for: 3 -> 3; matrix products, arithmetic and copies ran while one was open for 0% -> 0% of each run, Pallas kernels for 5% -> 4%
where the time goes in v4:
time: 45.6 us; the launch traced here: 45.4 us
  blocking collectives  21.1 us (46%)
  waiting for transfers between devices  12.1 us (27%)
  Pallas kernels  6.1 us (13%)
  starting transfers between devices  4.01 us (9%)
  between operations  2.01 us (4%)
    all_gather x1, blocking collectives, local(): row = lax.all_gather(own, AXES, axis_index_groups=line)  21.1 us
    ppermute x3, waiting for transfers between devices, across(): return lax.ppermute(own, AXES, pairs)  12.1 us
    ppermute x3, starting transfers between devices, across(): return lax.ppermute(own, AXES, pairs)  4.01 us
    pallas_call x1, Pallas kernels, local(): pl.pallas_call(last_kernel, out_shape=jax.ShapeDtypeStruct((rows, heads *...  2.31 us
    pallas_call x1, Pallas kernels, local(): pl.pallas_call(pack_kernel, out_shape=packed, in_specs=[HB] * 7, out_spec...  1.91 us
    pallas_call x1, Pallas kernels, local(): pl.pallas_call(first_kernel, out_shape=(jax.ShapeDtypeStruct((heads * row...  1.88 us
  transfers between devices with their start and end apart: 3, of which 3 were waited for; matrix products, arithmetic and copies ran while one was open for 0% of the time, Pallas kernels for 4%

profile of v4, /device:TPU:24, one launch (start us, length us, event | category | flops | bytes accessed | tf_op | source)
XLA Modules:
  0.0 45.4 jit_solution(16769352611691189285)
XLA Ops:
  1.9 1.9 %pack.1.own = bf16[272,256]{1,0:T(8,128)(2,1)} custom-call(s32[1,1]{1,0:T(1,128)S(6)} %copy.9.stretch_hbm, s32[1,1]{1,0:T(1,128)S(6)} %copy.10.clean_hbm, s32[1,1]{1,0:T(1,128)S(6)} %copy.11.pos_hbm.pos, bf16[128,256]{1,0:T(8,128)(2,1)} %k_hbm.1, bf16[128,256]{1,0:T(8,128)(2,1)} %v_hbm.1, f32[1,256]{1,0:T(1,128)} %bitcast.3, ...), custom_call_target="tpu_custom_call" | custom-call | flops 1000000 | bytes 400000 | tf_op jit(solution)/shard_map/pack/pallas_call | solution.py:186
  3.9 0.0 copy-start
  3.9 0.0 copy-start.1
  3.9 0.0 copy-start.2
  3.9 1.4 %collective-permute-start = (bf16[272,256]{1,0:T(8,128)(2,1)}, bf16[272,256]{1,0:T(8,128)(2,1)S(1)}, u32[]{:S(2)}, u32[]{:S(2)}) collective-permute-start(bf16[272,256]{1,0:T(8,128)(2,1)} %pack.1.own), channel_id=1, source_target_pairs={{4,3},{1,4},{2,5},{3,6},{8,7},{5,8},{6,9},{7,10},{12,11},{9,12},{1... | collective-permute-start | bytes 417800 | tf_op jit(solution)/shard_map/ppermute | solution.py:212
  5.3 1.3 %collective-permute-start.1 = (bf16[272,256]{1,0:T(8,128)(2,1)}, bf16[272,256]{1,0:T(8,128)(2,1)S(1)}, u32[]{:S(2)}, u32[]{:S(2)}) collective-permute-start(bf16[272,256]{1,0:T(8,128)(2,1)} %pack.1.own), channel_id=1, source_target_pairs={{4,2},{5,3},{2,4},{3,5},{8,6},{9,7},{6,8},{7,9},{12,10},{13,11},{1... | collective-permute-start | bytes 417800 | tf_op jit(solution)/shard_map/ppermute | solution.py:212
  6.6 1.3 %collective-permute-start.2 = (bf16[272,256]{1,0:T(8,128)(2,1)}, bf16[272,256]{1,0:T(8,128)(2,1)S(1)}, u32[]{:S(2)}, u32[]{:S(2)}) collective-permute-start(bf16[272,256]{1,0:T(8,128)(2,1)} %pack.1.own), channel_id=1, source_target_pairs={{4,1},{5,2},{6,3},{3,4},{8,5},{9,6},{10,7},{7,8},{12,9},{13,10},{1... | collective-permute-start | bytes 417800 | tf_op jit(solution)/shard_map/ppermute | solution.py:212
  7.9 21.1 %all-gather = bf16[1088,256]{1,0:T(8,128)(2,1)S(1)} all-gather(bf16[272,256]{1,0:T(8,128)(2,1)} %pack.1.own), channel_id=2, replica_groups={{0,1,2,3},{4,5,6,7},{8,9,10,11},{12,13,14,15},{16,17,18,19},{20,21,22,2..., dimensions={0}, use_global_device_ids=true | all-gather | bytes 696320 | tf_op jit(solution)/shard_map/all_gather | solution.py:216
  29.1 0.0 copy-done
  29.1 0.0 copy-done.1
  29.1 0.0 copy-done.2
  29.1 1.9 %row.1 = (bf16[1536,128]{1,0:T(8,128)(2,1)S(1)}, f32[1536,128]{1,0:T(8,128)S(1)}, f32[1536,128]{1,0:T(8,128)S(1)}, f32[1536,128]{1,0:T(8,128)S(1)}) custom-call(s32[1,1]{1,0:T(1,128)S(6)} %copy.11.pos_hbm.pos, bf16[272,256]{1,0:T(8,128)(2,1)S(1)} %copy-done, bf16[4,272,256]{2,1,0:T(8,128)(2,1)S(1)} %bitcast.2, bf16[128,1536]{1,0:T(8,128)(2,1)S(1)} %copy-done.2, ...), custom_call_target="tpu_custom_call" | custom-call | flops 402653184 | bytes 3000000 | tf_op jit(solution)/shard_map/row/pallas_call | solution.py:218
  31.0 4.6 %collective-permute-done.c1 = bf16[272,256]{1,0:T(8,128)(2,1)S(1)} collective-permute-done((bf16[272,256]{1,0:T(8,128)(2,1)}, bf16[272,256]{1,0:T(8,128)(2,1)S(1)}, u32[]{:S(2)}, u32[]{:S(2)}) %collective-permute-start) | collective-permute-done | bytes 139296 | tf_op jit(solution)/shard_map/ppermute | solution.py:212
  35.6 5.7 %collective-permute-done.1.c2 = bf16[272,256]{1,0:T(8,128)(2,1)S(1)} collective-permute-done((bf16[272,256]{1,0:T(8,128)(2,1)}, bf16[272,256]{1,0:T(8,128)(2,1)S(1)}, u32[]{:S(2)}, u32[]{:S(2)}) %collective-permute-start.1) | collective-permute-done | bytes 139296 | tf_op jit(solution)/shard_map/ppermute | solution.py:212
  41.2 1.8 %collective-permute-done.2.c3 = bf16[272,256]{1,0:T(8,128)(2,1)S(1)} collective-permute-done((bf16[272,256]{1,0:T(8,128)(2,1)}, bf16[272,256]{1,0:T(8,128)(2,1)S(1)}, u32[]{:S(2)}, u32[]{:S(2)}) %collective-permute-start.2) | collective-permute-done | bytes 139296 | tf_op jit(solution)/shard_map/ppermute | solution.py:212
  43.1 2.3 %across.1 = bf16[128,1536]{1,0:T(8,128)(2,1)} custom-call(bf16[272,256]{1,0:T(8,128)(2,1)S(1)} %collective-permute-done.c1, bf16[272,256]{1,0:T(8,128)(2,1)S(1)} %collective-permute-done.1.c2, bf16[272,256]{1,0:T(8,128)(2,1)S(1)} %collective-permute-done.2.c3, bf16[272,256]{1,0:T(8,128)(2,1)S(1)} %copy-done, bf16[1536,128]{1,0:T(8,128)(2,1)S(1)} %get-tuple-element.9.rq, ...), custom_call_target="tpu_custom_call" | custom-call | flops 301989888 | bytes 3000000 | tf_op jit(solution)/shard_map/across/pallas_call | solution.py:229
Async XLA Ops:
  3.9 25.2 %copy-start = (bf16[272,256]{1,0:T(8,128)(2,1)S(1)}, bf16[272,256]{1,0:T(8,128)(2,1)}, u32[]{:S(2)}) copy-start(bf16[272,256]{1,0:T(8,128)(2,1)} %pack.1.own) | copy-start | bytes 417796
  3.9 25.2 %copy-start.1 = (f32[2,144,128]{2,1,0:T(8,128)S(1)}, f32[2,144,128]{2,1,0:T(8,128)}, u32[]{:S(2)}) copy-start(f32[2,144,128]{2,1,0:T(8,128)} %constant.2.clone.tab_hbm.tab) | copy-start | bytes 442372
  3.9 25.2 %copy-start.2 = (bf16[128,1536]{1,0:T(8,128)(2,1)S(1)}, bf16[128,1536]{1,0:T(8,128)(2,1)}, u32[]{:S(2)}) copy-start(bf16[128,1536]{1,0:T(8,128)(2,1)} %q.1) | copy-start | bytes 1179652
  3.9 31.7 %collective-permute-start = (bf16[272,256]{1,0:T(8,128)(2,1)}, bf16[272,256]{1,0:T(8,128)(2,1)S(1)}, u32[]{:S(2)}, u32[]{:S(2)}) collective-permute-start(bf16[272,256]{1,0:T(8,128)(2,1)} %pack.1.own), channel_id=1, source_target_pairs={{4,3},{1,4},{2,5},{3,6},{8,7},{5,8},{6,9},{7,10},{12,11},{9,12},{1... | collective-permute-start | bytes 417800 | tf_op jit(solution)/shard_map/ppermute | solution.py:212
  5.3 35.9 %collective-permute-start.1 = (bf16[272,256]{1,0:T(8,128)(2,1)}, bf16[272,256]{1,0:T(8,128)(2,1)S(1)}, u32[]{:S(2)}, u32[]{:S(2)}) collective-permute-start(bf16[272,256]{1,0:T(8,128)(2,1)} %pack.1.own), channel_id=1, source_target_pairs={{4,2},{5,3},{2,4},{3,5},{8,6},{9,7},{6,8},{7,9},{12,10},{13,11},{1... | collective-permute-start | bytes 417800 | tf_op jit(solution)/shard_map/ppermute | solution.py:212
  6.6 36.4 %collective-permute-start.2 = (bf16[272,256]{1,0:T(8,128)(2,1)}, bf16[272,256]{1,0:T(8,128)(2,1)S(1)}, u32[]{:S(2)}, u32[]{:S(2)}) collective-permute-start(bf16[272,256]{1,0:T(8,128)(2,1)} %pack.1.own), channel_id=1, source_target_pairs={{4,1},{5,2},{6,3},{3,4},{8,5},{9,6},{10,7},{7,8},{12,9},{13,10},{1... | collective-permute-start | bytes 417800 | tf_op jit(solution)/shard_map/ppermute | solution.py:212

commit v5 on v4

--- a/solution.py
+++ b/solution.py
@@ -12,9 +12,10 @@
 D = 128
 WINDOW = 3
 ROW = WINDOW + 1
+CHUNK = 2
 ROPE_BASE = 10000.0
 NEG = -1e30
-LABEL_ROWS = 16
+LABEL_ROWS = 8
 AXES = ("stretch", "blk")
 SCALE = math.log2(math.e) / math.sqrt(D)
 
@@ -48,8 +49,8 @@
 
 
 def pack_kernel(
-    stretch_hbm, clean_hbm, pos_hbm, k_hbm, v_hbm, gain_hbm, tab_hbm,
-    out, stretch, clean, pos, k, gain, tab, sems,
+    stretch, clean, pos, k_hbm, v_hbm, gain_hbm, tab_hbm,
+    out, k, gain, tab, sems,
 ):
     rows = k.shape[0]
     moves = [
@@ -58,17 +59,14 @@
             [
                 (k_hbm, k),
                 (tab_hbm, tab),
-                (pos_hbm, pos),
                 (gain_hbm, gain),
-                (stretch_hbm, stretch),
-                (clean_hbm, clean),
                 (v_hbm, out.at[pl.ds(rows, rows)]),
             ]
         )
     ]
     for move in moves:
         move.start()
-    for move in moves[:4]:
+    for move in moves[:3]:
         move.wait()
     cos, sin = angles(pos[0, 0], tab, rows)
     for g in range(k.shape[1] // D):
@@ -76,7 +74,7 @@
         x = k[:, cols].astype(jnp.float32)
         x = x * lax.rsqrt(jnp.mean(x * x, axis=-1, keepdims=True) + 1e-6) * gain[:, cols]
         out[0:rows, cols] = rotate(x, cos, sin).astype(jnp.bfloat16)
-    for move in moves[4:]:
+    for move in moves[3:]:
         move.wait()
     label = stretch[0, 0] + 16 * lax.axis_index("stretch")
     row = lax.broadcasted_iota(jnp.int32, (LABEL_ROWS, k.shape[1]), 0)
@@ -97,75 +95,81 @@
     return (there > 0.5) & (earlier | same)
 
 
-def scores_of(q, kv, g):
-    rows = (kv.shape[0] - LABEL_ROWS) // 2
-    keys = kv[0:rows, pl.ds(g * D, D)]
+def cross(a, b, over_a, over_b):
     return lax.dot_general(
-        q, keys, (((1,), (1,)), ((), ())), preferred_element_type=jnp.float32
+        a, b, (((over_a,), (over_b,)), ((), ())), preferred_element_type=jnp.float32
     )
 
 
-def blend(q, blocks, visible, g, best):
-    scores = [
-        jnp.where(vis, scores_of(q, kv, g) * SCALE, NEG) for kv, vis in zip(blocks, visible)
-    ]
+def blend(q, blocks, bias, g, best):
+    cols = pl.ds(g * D, D)
+    scores = []
+    for kv, hidden in zip(blocks, bias):
+        rows = (kv.shape[0] - LABEL_ROWS) // 2
+        scores.append(cross(kv[0:rows, cols], q, 1, 1) * SCALE + hidden)
     top = functools.reduce(jnp.maximum, scores)
-    top = jnp.max(top, axis=-1, keepdims=True)
+    top = jnp.max(top, axis=0, keepdims=True)
     best = top if best is None else jnp.maximum(best, top)
     total, mixed = None, None
     for s, kv in zip(scores, blocks):
         rows = (kv.shape[0] - LABEL_ROWS) // 2
         w = jnp.exp2(s - best)
-        part = jnp.dot(
-            w.astype(jnp.bfloat16),
-            kv[pl.ds(rows, rows), pl.ds(g * D, D)],
-            preferred_element_type=jnp.float32,
-        )
+        part = cross(kv[pl.ds(rows, rows), cols], w.astype(jnp.bfloat16), 0, 0)
         total = w if total is None else total + w
         mixed = part if mixed is None else mixed + part
-    return best, jnp.sum(total, axis=-1, keepdims=True), mixed
-
-
-def first_kernel(pos, own, row, q, tab, rq, best_out, total_out, mixed_out):
+    return best, jnp.sum(total, axis=0, keepdims=True), mixed
+
+
+def hidden_by(mine, blocks):
+    bias = [jnp.where(seen(mine, labels(kv)), 0.0, NEG) for kv in blocks]
+    return [jnp.concatenate([b] * CHUNK, axis=1) for b in bias]
+
+
+def first_kernel(pos, own, row, q, tab, rq, stat_out, mixed_out):
     rows = q.shape[0]
     groups = own.shape[1] // D
     per = q.shape[1] // D // groups
     cos, sin = angles(pos[0, 0], tab, rows)
-    mine = labels(own)
     blocks = [row.at[i] for i in range(ROW)]
-    visible = [seen(mine, labels(kv)) for kv in blocks]
-    for g in range(groups):
-        at = pl.ds(g * per * rows, per * rows)
+    bias = hidden_by(labels(own), blocks)
+    for head in range(0, groups * per, CHUNK):
         turned = [
-            rotate(q[:, pl.ds((g * per + i) * D, D)].astype(jnp.float32), cos, sin)
-            for i in range(per)
+            rotate(q[:, pl.ds((head + i) * D, D)].astype(jnp.float32), cos, sin)
+            for i in range(CHUNK)
         ]
         turned = jnp.concatenate([x.astype(jnp.bfloat16) for x in turned], axis=0)
-        rq[at, :] = turned
-        best, total, mixed = blend(turned, blocks, visible, g, None)
-        best_out[at, :] = jnp.broadcast_to(best, mixed.shape)
-        total_out[at, :] = jnp.broadcast_to(total, mixed.shape)
-        mixed_out[at, :] = mixed
-
-
-def last_kernel(c1, c2, c3, own, rq, best_in, total_in, mixed_in, out):
+        rq[pl.ds(head * rows, CHUNK * rows), :] = turned
+        best, total, mixed = blend(turned, blocks, bias, head // per, None)
+        cols = pl.ds(head * rows, CHUNK * rows)
+        stat_out[0:1, cols] = best
+        stat_out[1:2, cols] = total
+        mixed_out[:, cols] = mixed
+
+
+def last_kernel(c1, c2, c3, own, rq, stat, mixed_in, out_hbm, out, sems):
     rows = out.shape[0]
     groups = own.shape[1] // D
     per = rq.shape[0] // rows // groups
-    mine = labels(own)
     blocks = (c1, c2, c3)
-    visible = [seen(mine, labels(kv)) for kv in blocks]
-    for g in range(groups):
-        at = pl.ds(g * per * rows, per * rows)
-        before = best_in[at, :]
-        best, total, mixed = blend(rq[at, :], blocks, visible, g, before)
+    bias = hidden_by(labels(own), blocks)
+    moves = []
+    for head in range(0, groups * per, CHUNK):
+        at = pl.ds(head * rows, CHUNK * rows)
+        before = stat[0:1, at]
+        best, total, mixed = blend(rq[at, :], blocks, bias, head // per, before)
         kept = jnp.exp2(before - best)
-        total = total_in[at, :] * kept + total
-        mixed = (mixed_in[at, :] * kept + mixed) / total
-        for i in range(per):
-            out[:, pl.ds((g * per + i) * D, D)] = mixed[i * rows : (i + 1) * rows].astype(
-                jnp.bfloat16
-            )
+        share = 1.0 / (stat[1:2, at] * kept + total)
+        mixed = mixed_in[:, at] * (kept * share) + mixed * share
+        for i in range(CHUNK):
+            one = mixed[:, i * rows : (i + 1) * rows]
+            out[:, pl.ds((head + i) * D, D)] = one.T.astype(jnp.bfloat16)
+        cols = pl.ds(head * D, CHUNK * D)
+        moves.append(
+            pltpu.make_async_copy(out.at[:, cols], out_hbm.at[:, cols], sems.at[head // CHUNK])
+        )
+        moves[-1].start()
+    for move in moves:
+        move.wait()
 
 
 VM = pl.BlockSpec(memory_space=pltpu.VMEM)
@@ -186,16 +190,13 @@
     own = pl.pallas_call(
         pack_kernel,
         out_shape=packed,
-        in_specs=[HB] * 7,
+        in_specs=[SM] * 3 + [HB] * 4,
         out_specs=VM,
         scratch_shapes=[
-            pltpu.SMEM((1, 1), jnp.int32),
-            pltpu.SMEM((1, 1), jnp.int32),
-            pltpu.SMEM((1, 1), jnp.int32),
             pltpu.VMEM((rows, width), jnp.bfloat16),
             pltpu.VMEM((1, width), jnp.float32),
             pltpu.VMEM(tab.shape, jnp.float32),
-            pltpu.SemaphoreType.DMA((7,)),
+            pltpu.SemaphoreType.DMA((4,)),
         ],
         compiler_params=pltpu.CompilerParams(vmem_limit_bytes=PACK_LIMIT),
         cost_estimate=pl.CostEstimate(flops=10**6, bytes_accessed=4 * 10**5, transcendentals=0),
@@ -214,12 +215,15 @@
     c1, c2, c3 = (across(by) for by in (1, 2, 3))
     line = [list(range(b, b + ROW)) for b in range(0, blocks, ROW)]
     row = lax.all_gather(own, AXES, axis_index_groups=line)
-    state = jax.ShapeDtypeStruct((heads * rows, D), jnp.float32)
-    rq, best, total, mixed = pl.pallas_call(
+    rq, stat, mixed = pl.pallas_call(
         first_kernel,
-        out_shape=(jax.ShapeDtypeStruct((heads * rows, D), jnp.bfloat16), state, state, state),
+        out_shape=(
+            jax.ShapeDtypeStruct((heads * rows, D), jnp.bfloat16),
+            jax.ShapeDtypeStruct((8, heads * rows), jnp.float32),
+            jax.ShapeDtypeStruct((D, heads * rows), jnp.float32),
+        ),
         in_specs=[SM] + [VM] * 4,
-        out_specs=(VM,) * 4,
+        out_specs=(VM,) * 3,
         compiler_params=PARAMS,
         cost_estimate=pl.CostEstimate(
             flops=4 * heads * rows * 4 * rows * D, bytes_accessed=3 * 10**6, transcendentals=10**6
@@ -229,14 +233,18 @@
     return pl.pallas_call(
         last_kernel,
         out_shape=jax.ShapeDtypeStruct((rows, heads * D), jnp.bfloat16),
-        in_specs=[VM] * 8,
-        out_specs=VM,
+        in_specs=[VM] * 7,
+        out_specs=HB,
+        scratch_shapes=[
+            pltpu.VMEM((rows, heads * D), jnp.bfloat16),
+            pltpu.SemaphoreType.DMA((heads // CHUNK,)),
+        ],
         compiler_params=PARAMS,
         cost_estimate=pl.CostEstimate(
             flops=4 * heads * rows * 3 * rows * D, bytes_accessed=3 * 10**6, transcendentals=10**6
         ),
         name="across",
-    )(c1, c2, c3, own, rq, best, total, mixed)
+    )(c1, c2, c3, own, rq, stat, mixed)
 
 
 def solution(mesh):

time: 45.6 us -> 44.9 us (0.985)
  Pallas kernels: 6.1 us -> 5.39 us
where the time goes in v5:
time: 44.9 us; the launch traced here: 44.7 us
  blocking collectives  20.9 us (47%)
  waiting for transfers between devices  12.4 us (28%)
  Pallas kernels  5.39 us (12%)
  starting transfers between devices  4.01 us (9%)
  between operations  2.01 us (4%)
    all_gather x1, blocking collectives, local(): row = lax.all_gather(own, AXES, axis_index_groups=line)  20.9 us
    ppermute x3, waiting for transfers between devices, across(): return lax.ppermute(own, AXES, pairs)  12.4 us
    ppermute x3, starting transfers between devices, across(): return lax.ppermute(own, AXES, pairs)  4.01 us
    pallas_call x1, Pallas kernels, local(): pl.pallas_call(last_kernel, out_shape=jax.ShapeDtypeStruct((rows, heads *...  1.95 us
    pallas_call x1, Pallas kernels, local(): pl.pallas_call(pack_kernel, out_shape=packed, in_specs=[SM] * 3 + [HB] *...  1.85 us
    pallas_call x1, Pallas kernels, local(): pl.pallas_call(first_kernel, out_shape=(jax.ShapeDtypeStruct((heads * row...  1.59 us
  transfers between devices with their start and end apart: 3, of which 3 were waited for; matrix products, arithmetic and copies ran while one was open for 0% of the time, Pallas kernels for 4%

profile of v5, /device:TPU:24, one launch (start us, length us, event | category | flops | bytes accessed | tf_op | source)
XLA Modules:
  0.0 44.7 jit_solution(7560706550579609688)
XLA Ops:
  1.9 1.8 %pack.1.own = bf16[264,256]{1,0:T(8,128)(2,1)} custom-call(s32[1,1]{1,0:T(1,128)S(6)} %copy.9.stretch, s32[1,1]{1,0:T(1,128)S(6)} %copy.10.clean, s32[1,1]{1,0:T(1,128)S(6)} %copy.11.pos, bf16[128,256]{1,0:T(8,128)(2,1)} %k_hbm.1, bf16[128,256]{1,0:T(8,128)(2,1)} %v_hbm.1, f32[1,256]{1,0:T(1,128)} %bitcast.3, f32[2,144,128]{2,1,0:T(8,128)} %constant.2.clone.tab_hbm.tab), custom_call_target="tpu_custom_call" | custom-call | flops 1000000 | bytes 400000 | tf_op jit(solution)/shard_map/pack/pallas_call | solution.py:190
  3.8 0.0 copy-start
  3.8 0.0 copy-start.1
  3.8 0.0 copy-start.2
  3.8 1.4 %collective-permute-start = (bf16[264,256]{1,0:T(8,128)(2,1)}, bf16[264,256]{1,0:T(8,128)(2,1)S(1)}, u32[]{:S(2)}, u32[]{:S(2)}) collective-permute-start(bf16[264,256]{1,0:T(8,128)(2,1)} %pack.1.own), channel_id=1, source_target_pairs={{4,3},{1,4},{2,5},{3,6},{8,7},{5,8},{6,9},{7,10},{12,11},{9,12},{1... | collective-permute-start | bytes 405512 | tf_op jit(solution)/shard_map/ppermute | solution.py:213
  5.3 1.3 %collective-permute-start.1 = (bf16[264,256]{1,0:T(8,128)(2,1)}, bf16[264,256]{1,0:T(8,128)(2,1)S(1)}, u32[]{:S(2)}, u32[]{:S(2)}) collective-permute-start(bf16[264,256]{1,0:T(8,128)(2,1)} %pack.1.own), channel_id=1, source_target_pairs={{4,2},{5,3},{2,4},{3,5},{8,6},{9,7},{6,8},{7,9},{12,10},{13,11},{1... | collective-permute-start | bytes 405512 | tf_op jit(solution)/shard_map/ppermute | solution.py:213
  6.6 1.3 %collective-permute-start.2 = (bf16[264,256]{1,0:T(8,128)(2,1)}, bf16[264,256]{1,0:T(8,128)(2,1)S(1)}, u32[]{:S(2)}, u32[]{:S(2)}) collective-permute-start(bf16[264,256]{1,0:T(8,128)(2,1)} %pack.1.own), channel_id=1, source_target_pairs={{4,1},{5,2},{6,3},{3,4},{8,5},{9,6},{10,7},{7,8},{12,9},{13,10},{1... | collective-permute-start | bytes 405512 | tf_op jit(solution)/shard_map/ppermute | solution.py:213
  7.9 20.9 %all-gather = bf16[1056,256]{1,0:T(8,128)(2,1)S(1)} all-gather(bf16[264,256]{1,0:T(8,128)(2,1)} %pack.1.own), channel_id=2, replica_groups={{0,1,2,3},{4,5,6,7},{8,9,10,11},{12,13,14,15},{16,17,18,19},{20,21,22,2..., dimensions={0}, use_global_device_ids=true | all-gather | bytes 675840 | tf_op jit(solution)/shard_map/all_gather | solution.py:217
  28.7 0.0 copy-done
  28.7 0.0 copy-done.1
  28.8 0.0 copy-done.2
  28.8 1.6 %row.1 = (bf16[1536,128]{1,0:T(8,128)(2,1)S(1)}, f32[8,1536]{1,0:T(8,128)S(1)}, f32[128,1536]{1,0:T(8,128)S(1)}) custom-call(s32[1,1]{1,0:T(1,128)S(6)} %copy.11.pos, bf16[264,256]{1,0:T(8,128)(2,1)S(1)} %copy-done, bf16[4,264,256]{2,1,0:T(8,128)(2,1)S(1)} %bitcast.2, bf16[128,1536]{1,0:T(8,128)(2,1)S(1)} %copy-done.2, f32[2,144,128]{2,1,0:T(8,128)S(1)} %copy-done.1), custom_call_target="tpu_custom_call" | custom-call | flops 402653184 | bytes 3000000 | tf_op jit(solution)/shard_map/row/pallas_call | solution.py:218
  30.4 5.1 %collective-permute-done.c1 = bf16[264,256]{1,0:T(8,128)(2,1)S(1)} collective-permute-done((bf16[264,256]{1,0:T(8,128)(2,1)}, bf16[264,256]{1,0:T(8,128)(2,1)S(1)}, u32[]{:S(2)}, u32[]{:S(2)}) %collective-permute-start) | collective-permute-done | bytes 135200 | tf_op jit(solution)/shard_map/ppermute | solution.py:213
  35.4 5.6 %collective-permute-done.1.c2 = bf16[264,256]{1,0:T(8,128)(2,1)S(1)} collective-permute-done((bf16[264,256]{1,0:T(8,128)(2,1)}, bf16[264,256]{1,0:T(8,128)(2,1)S(1)}, u32[]{:S(2)}, u32[]{:S(2)}) %collective-permute-start.1) | collective-permute-done | bytes 135200 | tf_op jit(solution)/shard_map/ppermute | solution.py:213
  41.0 1.7 %collective-permute-done.2.c3 = bf16[264,256]{1,0:T(8,128)(2,1)S(1)} collective-permute-done((bf16[264,256]{1,0:T(8,128)(2,1)}, bf16[264,256]{1,0:T(8,128)(2,1)S(1)}, u32[]{:S(2)}, u32[]{:S(2)}) %collective-permute-start.2) | collective-permute-done | bytes 135200 | tf_op jit(solution)/shard_map/ppermute | solution.py:213
  42.7 2.0 %across.1 = bf16[128,1536]{1,0:T(8,128)(2,1)} custom-call(bf16[264,256]{1,0:T(8,128)(2,1)S(1)} %collective-permute-done.c1, bf16[264,256]{1,0:T(8,128)(2,1)S(1)} %collective-permute-done.1.c2, bf16[264,256]{1,0:T(8,128)(2,1)S(1)} %collective-permute-done.2.c3, bf16[264,256]{1,0:T(8,128)(2,1)S(1)} %copy-done, bf16[1536,128]{1,0:T(8,128)(2,1)S(1)} %get-tuple-element.8.rq, ...), custom_call_target="tpu_custom_call" | custom-call | flops 301989888 | bytes 3000000 | tf_op jit(solution)/shard_map/across/pallas_call | solution.py:233
Async XLA Ops:
  3.8 24.9 %copy-start = (bf16[264,256]{1,0:T(8,128)(2,1)S(1)}, bf16[264,256]{1,0:T(8,128)(2,1)}, u32[]{:S(2)}) copy-start(bf16[264,256]{1,0:T(8,128)(2,1)} %pack.1.own) | copy-start | bytes 405508
  3.8 24.9 %copy-start.1 = (f32[2,144,128]{2,1,0:T(8,128)S(1)}, f32[2,144,128]{2,1,0:T(8,128)}, u32[]{:S(2)}) copy-start(f32[2,144,128]{2,1,0:T(8,128)} %constant.2.clone.tab_hbm.tab) | copy-start | bytes 442372
  3.8 24.9 %copy-start.2 = (bf16[128,1536]{1,0:T(8,128)(2,1)S(1)}, bf16[128,1536]{1,0:T(8,128)(2,1)}, u32[]{:S(2)}) copy-start(bf16[128,1536]{1,0:T(8,128)(2,1)} %q.1) | copy-start | bytes 1179652
  3.8 31.6 %collective-permute-start = (bf16[264,256]{1,0:T(8,128)(2,1)}, bf16[264,256]{1,0:T(8,128)(2,1)S(1)}, u32[]{:S(2)}, u32[]{:S(2)}) collective-permute-start(bf16[264,256]{1,0:T(8,128)(2,1)} %pack.1.own), channel_id=1, source_target_pairs={{4,3},{1,4},{2,5},{3,6},{8,7},{5,8},{6,9},{7,10},{12,11},{9,12},{1... | collective-permute-start | bytes 405512 | tf_op jit(solution)/shard_map/ppermute | solution.py:213
  5.3 35.7 %collective-permute-start.1 = (bf16[264,256]{1,0:T(8,128)(2,1)}, bf16[264,256]{1,0:T(8,128)(2,1)S(1)}, u32[]{:S(2)}, u32[]{:S(2)}) collective-permute-start(bf16[264,256]{1,0:T(8,128)(2,1)} %pack.1.own), channel_id=1, source_target_pairs={{4,2},{5,3},{2,4},{3,5},{8,6},{9,7},{6,8},{7,9},{12,10},{13,11},{1... | collective-permute-start | bytes 405512 | tf_op jit(solution)/shard_map/ppermute | solution.py:213
  6.6 36.2 %collective-permute-start.2 = (bf16[264,256]{1,0:T(8,128)(2,1)}, bf16[264,256]{1,0:T(8,128)(2,1)S(1)}, u32[]{:S(2)}, u32[]{:S(2)}) collective-permute-start(bf16[264,256]{1,0:T(8,128)(2,1)} %pack.1.own), channel_id=1, source_target_pairs={{4,1},{5,2},{6,3},{3,4},{8,5},{9,6},{10,7},{7,8},{12,9},{13,10},{1... | collective-permute-start | bytes 405512 | tf_op jit(solution)/shard_map/ppermute | solution.py:213

commit v6 on v5

--- a/solution.py
+++ b/solution.py
@@ -146,11 +146,11 @@
         mixed_out[:, cols] = mixed
 
 
-def last_kernel(c1, c2, c3, own, rq, stat, mixed_in, out_hbm, out, sems):
+def last_kernel(c2, c3, c1, own, rq, stat, mixed_in, out_hbm, out, sems):
     rows = out.shape[0]
     groups = own.shape[1] // D
     per = rq.shape[0] // rows // groups
-    blocks = (c1, c2, c3)
+    blocks = (c2, c3, c1)
     bias = hidden_by(labels(own), blocks)
     moves = []
     for head in range(0, groups * per, CHUNK):
@@ -244,7 +244,7 @@
             flops=4 * heads * rows * 3 * rows * D, bytes_accessed=3 * 10**6, transcendentals=10**6
         ),
         name="across",
-    )(c1, c2, c3, own, rq, stat, mixed)
+    )(c2, c3, c1, own, rq, stat, mixed)
 
 
 def solution(mesh):

time: 44.9 us -> 45.2 us (level)
  no operation moved by 1% of the time
where the time goes in v6:
time: 45.2 us; the launch traced here: 44.7 us
  blocking collectives  21.1 us (47%)
  waiting for transfers between devices  12.2 us (27%)
  Pallas kernels  5.39 us (12%)
  starting transfers between devices  4.01 us (9%)
  between operations  2.01 us (4%)
    all_gather x1, blocking collectives, local(): row = lax.all_gather(own, AXES, axis_index_groups=line)  21.1 us
    ppermute x3, waiting for transfers between devices, across(): return lax.ppermute(own, AXES, pairs)  12.2 us
    ppermute x3, starting transfers between devices, across(): return lax.ppermute(own, AXES, pairs)  4.01 us
    pallas_call x1, Pallas kernels, local(): pl.pallas_call(last_kernel, out_shape=jax.ShapeDtypeStruct((rows, heads *...  1.95 us
    pallas_call x1, Pallas kernels, local(): pl.pallas_call(pack_kernel, out_shape=packed, in_specs=[SM] * 3 + [HB] *...  1.85 us
    pallas_call x1, Pallas kernels, local(): pl.pallas_call(first_kernel, out_shape=(jax.ShapeDtypeStruct((heads * row...  1.59 us
  transfers between devices with their start and end apart: 3, of which 3 were waited for; matrix products, arithmetic and copies ran while one was open for 0% of the time, Pallas kernels for 4%

profile of v6, /device:TPU:24, one launch (start us, length us, event | category | flops | bytes accessed | tf_op | source)
XLA Modules:
  0.0 44.7 jit_solution(10745573891433001123)
XLA Ops:
  1.9 1.8 %pack.1.own = bf16[264,256]{1,0:T(8,128)(2,1)} custom-call(s32[1,1]{1,0:T(1,128)S(6)} %copy.9.stretch, s32[1,1]{1,0:T(1,128)S(6)} %copy.10.clean, s32[1,1]{1,0:T(1,128)S(6)} %copy.11.pos, bf16[128,256]{1,0:T(8,128)(2,1)} %k_hbm.1, bf16[128,256]{1,0:T(8,128)(2,1)} %v_hbm.1, f32[1,256]{1,0:T(1,128)} %bitcast.3, f32[2,144,128]{2,1,0:T(8,128)} %constant.2.clone.tab_hbm.tab), custom_call_target="tpu_custom_call" | custom-call | flops 1000000 | bytes 400000 | tf_op jit(solution)/shard_map/pack/pallas_call | solution.py:190
  3.8 0.0 copy-start
  3.8 0.0 copy-start.1
  3.8 0.0 copy-start.2
  3.8 1.4 %collective-permute-start = (bf16[264,256]{1,0:T(8,128)(2,1)}, bf16[264,256]{1,0:T(8,128)(2,1)S(1)}, u32[]{:S(2)}, u32[]{:S(2)}) collective-permute-start(bf16[264,256]{1,0:T(8,128)(2,1)} %pack.1.own), channel_id=1, source_target_pairs={{4,2},{5,3},{2,4},{3,5},{8,6},{9,7},{6,8},{7,9},{12,10},{13,11},{1... | collective-permute-start | bytes 405512 | tf_op jit(solution)/shard_map/ppermute | solution.py:213
  5.3 1.3 %collective-permute-start.1 = (bf16[264,256]{1,0:T(8,128)(2,1)}, bf16[264,256]{1,0:T(8,128)(2,1)S(1)}, u32[]{:S(2)}, u32[]{:S(2)}) collective-permute-start(bf16[264,256]{1,0:T(8,128)(2,1)} %pack.1.own), channel_id=1, source_target_pairs={{4,1},{5,2},{6,3},{3,4},{8,5},{9,6},{10,7},{7,8},{12,9},{13,10},{1... | collective-permute-start | bytes 405512 | tf_op jit(solution)/shard_map/ppermute | solution.py:213
  6.6 1.3 %collective-permute-start.2 = (bf16[264,256]{1,0:T(8,128)(2,1)}, bf16[264,256]{1,0:T(8,128)(2,1)S(1)}, u32[]{:S(2)}, u32[]{:S(2)}) collective-permute-start(bf16[264,256]{1,0:T(8,128)(2,1)} %pack.1.own), channel_id=1, source_target_pairs={{4,3},{1,4},{2,5},{3,6},{8,7},{5,8},{6,9},{7,10},{12,11},{9,12},{1... | collective-permute-start | bytes 405512 | tf_op jit(solution)/shard_map/ppermute | solution.py:213
  7.9 21.1 %all-gather = bf16[1056,256]{1,0:T(8,128)(2,1)S(1)} all-gather(bf16[264,256]{1,0:T(8,128)(2,1)} %pack.1.own), channel_id=2, replica_groups={{0,1,2,3},{4,5,6,7},{8,9,10,11},{12,13,14,15},{16,17,18,19},{20,21,22,2..., dimensions={0}, use_global_device_ids=true | all-gather | bytes 675840 | tf_op jit(solution)/shard_map/all_gather | solution.py:217
  28.9 0.0 copy-done
  28.9 0.0 copy-done.1
  28.9 0.0 copy-done.2
  29.0 1.6 %row.1 = (bf16[1536,128]{1,0:T(8,128)(2,1)S(1)}, f32[8,1536]{1,0:T(8,128)S(1)}, f32[128,1536]{1,0:T(8,128)S(1)}) custom-call(s32[1,1]{1,0:T(1,128)S(6)} %copy.11.pos, bf16[264,256]{1,0:T(8,128)(2,1)S(1)} %copy-done, bf16[4,264,256]{2,1,0:T(8,128)(2,1)S(1)} %bitcast.2, bf16[128,1536]{1,0:T(8,128)(2,1)S(1)} %copy-done.2, f32[2,144,128]{2,1,0:T(8,128)S(1)} %copy-done.1), custom_call_target="tpu_custom_call" | custom-call | flops 402653184 | bytes 3000000 | tf_op jit(solution)/shard_map/row/pallas_call | solution.py:218
  30.5 6.3 %collective-permute-done.c2 = bf16[264,256]{1,0:T(8,128)(2,1)S(1)} collective-permute-done((bf16[264,256]{1,0:T(8,128)(2,1)}, bf16[264,256]{1,0:T(8,128)(2,1)S(1)}, u32[]{:S(2)}, u32[]{:S(2)}) %collective-permute-start) | collective-permute-done | bytes 135200 | tf_op jit(solution)/shard_map/ppermute | solution.py:213
  36.9 3.1 %collective-permute-done.1.c3 = bf16[264,256]{1,0:T(8,128)(2,1)S(1)} collective-permute-done((bf16[264,256]{1,0:T(8,128)(2,1)}, bf16[264,256]{1,0:T(8,128)(2,1)S(1)}, u32[]{:S(2)}, u32[]{:S(2)}) %collective-permute-start.1) | collective-permute-done | bytes 135200 | tf_op jit(solution)/shard_map/ppermute | solution.py:213
  40.0 2.8 %collective-permute-done.2.c1 = bf16[264,256]{1,0:T(8,128)(2,1)S(1)} collective-permute-done((bf16[264,256]{1,0:T(8,128)(2,1)}, bf16[264,256]{1,0:T(8,128)(2,1)S(1)}, u32[]{:S(2)}, u32[]{:S(2)}) %collective-permute-start.2) | collective-permute-done | bytes 135200 | tf_op jit(solution)/shard_map/ppermute | solution.py:213
  42.7 2.0 %across.1 = bf16[128,1536]{1,0:T(8,128)(2,1)} custom-call(bf16[264,256]{1,0:T(8,128)(2,1)S(1)} %collective-permute-done.c2, bf16[264,256]{1,0:T(8,128)(2,1)S(1)} %collective-permute-done.1.c3, bf16[264,256]{1,0:T(8,128)(2,1)S(1)} %collective-permute-done.2.c1, bf16[264,256]{1,0:T(8,128)(2,1)S(1)} %copy-done, bf16[1536,128]{1,0:T(8,128)(2,1)S(1)} %get-tuple-element.8.rq, ...), custom_call_target="tpu_custom_call" | custom-call | flops 301989888 | bytes 3000000 | tf_op jit(solution)/shard_map/across/pallas_call | solution.py:233
Async XLA Ops:
  3.8 25.1 %copy-start = (bf16[264,256]{1,0:T(8,128)(2,1)S(1)}, bf16[264,256]{1,0:T(8,128)(2,1)}, u32[]{:S(2)}) copy-start(bf16[264,256]{1,0:T(8,128)(2,1)} %pack.1.own) | copy-start | bytes 405508
  3.8 25.1 %copy-start.1 = (f32[2,144,128]{2,1,0:T(8,128)S(1)}, f32[2,144,128]{2,1,0:T(8,128)}, u32[]{:S(2)}) copy-start(f32[2,144,128]{2,1,0:T(8,128)} %constant.2.clone.tab_hbm.tab) | copy-start | bytes 442372
  3.8 25.1 %copy-start.2 = (bf16[128,1536]{1,0:T(8,128)(2,1)S(1)}, bf16[128,1536]{1,0:T(8,128)(2,1)}, u32[]{:S(2)}) copy-start(bf16[128,1536]{1,0:T(8,128)(2,1)} %q.1) | copy-start | bytes 1179652
  3.8 33.0 %collective-permute-start = (bf16[264,256]{1,0:T(8,128)(2,1)}, bf16[264,256]{1,0:T(8,128)(2,1)S(1)}, u32[]{:S(2)}, u32[]{:S(2)}) collective-permute-start(bf16[264,256]{1,0:T(8,128)(2,1)} %pack.1.own), channel_id=1, source_target_pairs={{4,2},{5,3},{2,4},{3,5},{8,6},{9,7},{6,8},{7,9},{12,10},{13,11},{1... | collective-permute-start | bytes 405512 | tf_op jit(solution)/shard_map/ppermute | solution.py:213
  5.3 34.7 %collective-permute-start.1 = (bf16[264,256]{1,0:T(8,128)(2,1)}, bf16[264,256]{1,0:T(8,128)(2,1)S(1)}, u32[]{:S(2)}, u32[]{:S(2)}) collective-permute-start(bf16[264,256]{1,0:T(8,128)(2,1)} %pack.1.own), channel_id=1, source_target_pairs={{4,1},{5,2},{6,3},{3,4},{8,5},{9,6},{10,7},{7,8},{12,9},{13,10},{1... | collective-permute-start | bytes 405512 | tf_op jit(solution)/shard_map/ppermute | solution.py:213
  6.6 36.2 %collective-permute-start.2 = (bf16[264,256]{1,0:T(8,128)(2,1)}, bf16[264,256]{1,0:T(8,128)(2,1)S(1)}, u32[]{:S(2)}, u32[]{:S(2)}) collective-permute-start(bf16[264,256]{1,0:T(8,128)(2,1)} %pack.1.own), channel_id=1, source_target_pairs={{4,3},{1,4},{2,5},{3,6},{8,7},{5,8},{6,9},{7,10},{12,11},{9,12},{1... | collective-permute-start | bytes 405512 | tf_op jit(solution)/shard_map/ppermute | solution.py:213

commit v7 on v5

--- a/solution.py
+++ b/solution.py
@@ -12,6 +12,7 @@
 D = 128
 WINDOW = 3
 ROW = WINDOW + 1
+SOURCES = ((2, 0, 3, 1), (1, 3, 0, 2), (3, 2, 1, 0))
 CHUNK = 2
 ROPE_BASE = 10000.0
 NEG = -1e30
@@ -203,16 +204,16 @@
         name="pack",
     )(stretch_ids, clean_flags, positions, keys, values, key_norm_gain[None, :], tab)
 
-    def across(by):
+    def across(sources):
         pairs = []
         for b in range(blocks):
-            column = (b + by) % ROW
+            column = sources[b % ROW]
             other = b - b % ROW + column + (-ROW if column > b % ROW else ROW)
             if 0 <= other < blocks and other // per_group <= b // per_group:
                 pairs.append((other, b))
         return lax.ppermute(own, AXES, pairs)
 
-    c1, c2, c3 = (across(by) for by in (1, 2, 3))
+    c1, c2, c3 = (across(sources) for sources in SOURCES)
     line = [list(range(b, b + ROW)) for b in range(0, blocks, ROW)]
     row = lax.all_gather(own, AXES, axis_index_groups=line)
     rq, stat, mixed = pl.pallas_call(

time: 44.9 us -> 44.9 us (level)
  waiting for transfers between devices: 12.4 us -> 11.9 us
    ppermute x3, waiting for transfers between devices: 12.4 us -> 11.9 us  [across(): return lax.ppermute(own, AXES, pairs)]
where the time goes in v7:
time: 44.9 us; the launch traced here: 44.6 us
  blocking collectives  21.3 us (47%)
  waiting for transfers between devices  11.9 us (27%)
  Pallas kernels  5.39 us (12%)
  starting transfers between devices  4.01 us (9%)
  between operations  2.01 us (4%)
    all_gather x1, blocking collectives, local(): row = lax.all_gather(own, AXES, axis_index_groups=line)  21.3 us
    ppermute x3, waiting for transfers between devices, across(): return lax.ppermute(own, AXES, pairs)  11.9 us
    ppermute x3, starting transfers between devices, across(): return lax.ppermute(own, AXES, pairs)  4.01 us
    pallas_call x1, Pallas kernels, local(): pl.pallas_call(last_kernel, out_shape=jax.ShapeDtypeStruct((rows, heads *...  1.95 us
    pallas_call x1, Pallas kernels, local(): pl.pallas_call(pack_kernel, out_shape=packed, in_specs=[SM] * 3 + [HB] *...  1.85 us
    pallas_call x1, Pallas kernels, local(): pl.pallas_call(first_kernel, out_shape=(jax.ShapeDtypeStruct((heads * row...  1.59 us
  transfers between devices with their start and end apart: 3, of which 3 were waited for; matrix products, arithmetic and copies ran while one was open for 0% of the time, Pallas kernels for 4%

profile of v7, /device:TPU:24, one launch (start us, length us, event | category | flops | bytes accessed | tf_op | source)
XLA Modules:
  0.0 44.6 jit_solution(15025372769077258672)
XLA Ops:
  1.9 1.8 %pack.1.own = bf16[264,256]{1,0:T(8,128)(2,1)} custom-call(s32[1,1]{1,0:T(1,128)S(6)} %copy.9.stretch, s32[1,1]{1,0:T(1,128)S(6)} %copy.10.clean, s32[1,1]{1,0:T(1,128)S(6)} %copy.11.pos, bf16[128,256]{1,0:T(8,128)(2,1)} %k_hbm.1, bf16[128,256]{1,0:T(8,128)(2,1)} %v_hbm.1, f32[1,256]{1,0:T(1,128)} %bitcast.3, f32[2,144,128]{2,1,0:T(8,128)} %constant.2.clone.tab_hbm.tab), custom_call_target="tpu_custom_call" | custom-call | flops 1000000 | bytes 400000 | tf_op jit(solution)/shard_map/pack/pallas_call | solution.py:191
  3.8 0.0 copy-start
  3.8 0.0 copy-start.1
  3.8 0.0 copy-start.2
  3.8 1.4 %collective-permute-start = (bf16[264,256]{1,0:T(8,128)(2,1)}, bf16[264,256]{1,0:T(8,128)(2,1)S(1)}, u32[]{:S(2)}, u32[]{:S(2)}) collective-permute-start(bf16[264,256]{1,0:T(8,128)(2,1)} %pack.1.own), channel_id=1, source_target_pairs={{4,1},{5,3},{2,4},{8,5},{3,6},{9,7},{6,8},{12,9},{7,10},{13,11},{1... | collective-permute-start | bytes 405512 | tf_op jit(solution)/shard_map/ppermute | solution.py:214
  5.3 1.3 %collective-permute-start.1 = (bf16[264,256]{1,0:T(8,128)(2,1)}, bf16[264,256]{1,0:T(8,128)(2,1)S(1)}, u32[]{:S(2)}, u32[]{:S(2)}) collective-permute-start(bf16[264,256]{1,0:T(8,128)(2,1)} %pack.1.own), channel_id=1, source_target_pairs={{4,2},{6,3},{1,4},{3,5},{8,6},{10,7},{5,8},{7,9},{12,10},{14,11},{... | collective-permute-start | bytes 405512 | tf_op jit(solution)/shard_map/ppermute | solution.py:214
  6.6 1.3 %collective-permute-start.2 = (bf16[264,256]{1,0:T(8,128)(2,1)}, bf16[264,256]{1,0:T(8,128)(2,1)S(1)}, u32[]{:S(2)}, u32[]{:S(2)}) collective-permute-start(bf16[264,256]{1,0:T(8,128)(2,1)} %pack.1.own), channel_id=1, source_target_pairs={{5,2},{4,3},{3,4},{2,5},{9,6},{8,7},{7,8},{6,9},{13,10},{12,11},{1... | collective-permute-start | bytes 405512 | tf_op jit(solution)/shard_map/ppermute | solution.py:214
  7.9 21.3 %all-gather = bf16[1056,256]{1,0:T(8,128)(2,1)S(1)} all-gather(bf16[264,256]{1,0:T(8,128)(2,1)} %pack.1.own), channel_id=2, replica_groups={{0,1,2,3},{4,5,6,7},{8,9,10,11},{12,13,14,15},{16,17,18,19},{20,21,22,2..., dimensions={0}, use_global_device_ids=true | all-gather | bytes 675840 | tf_op jit(solution)/shard_map/all_gather | solution.py:218
  29.2 0.0 copy-done
  29.2 0.0 copy-done.1
  29.2 0.0 copy-done.2
  29.2 1.6 %row.1 = (bf16[1536,128]{1,0:T(8,128)(2,1)S(1)}, f32[8,1536]{1,0:T(8,128)S(1)}, f32[128,1536]{1,0:T(8,128)S(1)}) custom-call(s32[1,1]{1,0:T(1,128)S(6)} %copy.11.pos, bf16[264,256]{1,0:T(8,128)(2,1)S(1)} %copy-done, bf16[4,264,256]{2,1,0:T(8,128)(2,1)S(1)} %bitcast.2, bf16[128,1536]{1,0:T(8,128)(2,1)S(1)} %copy-done.2, f32[2,144,128]{2,1,0:T(8,128)S(1)} %copy-done.1), custom_call_target="tpu_custom_call" | custom-call | flops 402653184 | bytes 3000000 | tf_op jit(solution)/shard_map/row/pallas_call | solution.py:219
  30.8 6.7 %collective-permute-done.c1 = bf16[264,256]{1,0:T(8,128)(2,1)S(1)} collective-permute-done((bf16[264,256]{1,0:T(8,128)(2,1)}, bf16[264,256]{1,0:T(8,128)(2,1)S(1)}, u32[]{:S(2)}, u32[]{:S(2)}) %collective-permute-start) | collective-permute-done | bytes 135200 | tf_op jit(solution)/shard_map/ppermute | solution.py:214
  37.5 3.4 %collective-permute-done.1.c2 = bf16[264,256]{1,0:T(8,128)(2,1)S(1)} collective-permute-done((bf16[264,256]{1,0:T(8,128)(2,1)}, bf16[264,256]{1,0:T(8,128)(2,1)S(1)}, u32[]{:S(2)}, u32[]{:S(2)}) %collective-permute-start.1) | collective-permute-done | bytes 135200 | tf_op jit(solution)/shard_map/ppermute | solution.py:214
  40.9 1.8 %collective-permute-done.2.c3 = bf16[264,256]{1,0:T(8,128)(2,1)S(1)} collective-permute-done((bf16[264,256]{1,0:T(8,128)(2,1)}, bf16[264,256]{1,0:T(8,128)(2,1)S(1)}, u32[]{:S(2)}, u32[]{:S(2)}) %collective-permute-start.2) | collective-permute-done | bytes 135200 | tf_op jit(solution)/shard_map/ppermute | solution.py:214
  42.7 2.0 %across.1 = bf16[128,1536]{1,0:T(8,128)(2,1)} custom-call(bf16[264,256]{1,0:T(8,128)(2,1)S(1)} %collective-permute-done.c1, bf16[264,256]{1,0:T(8,128)(2,1)S(1)} %collective-permute-done.1.c2, bf16[264,256]{1,0:T(8,128)(2,1)S(1)} %collective-permute-done.2.c3, bf16[264,256]{1,0:T(8,128)(2,1)S(1)} %copy-done, bf16[1536,128]{1,0:T(8,128)(2,1)S(1)} %get-tuple-element.8.rq, ...), custom_call_target="tpu_custom_call" | custom-call | flops 301989888 | bytes 3000000 | tf_op jit(solution)/shard_map/across/pallas_call | solution.py:234
Async XLA Ops:
  3.8 25.4 %copy-start = (bf16[264,256]{1,0:T(8,128)(2,1)S(1)}, bf16[264,256]{1,0:T(8,128)(2,1)}, u32[]{:S(2)}) copy-start(bf16[264,256]{1,0:T(8,128)(2,1)} %pack.1.own) | copy-start | bytes 405508
  3.8 25.4 %copy-start.1 = (f32[2,144,128]{2,1,0:T(8,128)S(1)}, f32[2,144,128]{2,1,0:T(8,128)}, u32[]{:S(2)}) copy-start(f32[2,144,128]{2,1,0:T(8,128)} %constant.2.clone.tab_hbm.tab) | copy-start | bytes 442372
  3.8 25.4 %copy-start.2 = (bf16[128,1536]{1,0:T(8,128)(2,1)S(1)}, bf16[128,1536]{1,0:T(8,128)(2,1)}, u32[]{:S(2)}) copy-start(bf16[128,1536]{1,0:T(8,128)(2,1)} %q.1) | copy-start | bytes 1179652
  3.8 33.7 %collective-permute-start = (bf16[264,256]{1,0:T(8,128)(2,1)}, bf16[264,256]{1,0:T(8,128)(2,1)S(1)}, u32[]{:S(2)}, u32[]{:S(2)}) collective-permute-start(bf16[264,256]{1,0:T(8,128)(2,1)} %pack.1.own), channel_id=1, source_target_pairs={{4,1},{5,3},{2,4},{8,5},{3,6},{9,7},{6,8},{12,9},{7,10},{13,11},{1... | collective-permute-start | bytes 405512 | tf_op jit(solution)/shard_map/ppermute | solution.py:214
  5.3 35.6 %collective-permute-start.1 = (bf16[264,256]{1,0:T(8,128)(2,1)}, bf16[264,256]{1,0:T(8,128)(2,1)S(1)}, u32[]{:S(2)}, u32[]{:S(2)}) collective-permute-start(bf16[264,256]{1,0:T(8,128)(2,1)} %pack.1.own), channel_id=1, source_target_pairs={{4,2},{6,3},{1,4},{3,5},{8,6},{10,7},{5,8},{7,9},{12,10},{14,11},{... | collective-permute-start | bytes 405512 | tf_op jit(solution)/shard_map/ppermute | solution.py:214
  6.6 36.1 %collective-permute-start.2 = (bf16[264,256]{1,0:T(8,128)(2,1)}, bf16[264,256]{1,0:T(8,128)(2,1)S(1)}, u32[]{:S(2)}, u32[]{:S(2)}) collective-permute-start(bf16[264,256]{1,0:T(8,128)(2,1)} %pack.1.own), channel_id=1, source_target_pairs={{5,2},{4,3},{3,4},{2,5},{9,6},{8,7},{7,8},{6,9},{13,10},{12,11},{1... | collective-permute-start | bytes 405512 | tf_op jit(solution)/shard_map/ppermute | solution.py:214

commit v8 on v7

--- a/solution.py
+++ b/solution.py
@@ -147,11 +147,27 @@
         mixed_out[:, cols] = mixed
 
 
-def last_kernel(c1, c2, c3, own, rq, stat, mixed_in, out_hbm, out, sems):
+def middle_kernel(c1, c2, own, rq, stat, mixed_in, stat_out, mixed_out):
+    groups = own.shape[1] // D
+    rows = mixed_in.shape[0]
+    per = rq.shape[0] // rows // groups
+    blocks = (c1, c2)
+    bias = hidden_by(labels(own), blocks)
+    for head in range(0, groups * per, CHUNK):
+        at = pl.ds(head * rows, CHUNK * rows)
+        before = stat[0:1, at]
+        best, total, mixed = blend(rq[at, :], blocks, bias, head // per, before)
+        kept = jnp.exp2(before - best)
+        stat_out[0:1, at] = best
+        stat_out[1:2, at] = stat[1:2, at] * kept + total
+        mixed_out[:, at] = mixed_in[:, at] * kept + mixed
+
+
+def last_kernel(c3, own, rq, stat, mixed_in, out_hbm, out, sems):
     rows = out.shape[0]
     groups = own.shape[1] // D
     per = rq.shape[0] // rows // groups
-    blocks = (c1, c2, c3)
+    blocks = (c3,)
     bias = hidden_by(labels(own), blocks)
     moves = []
     for head in range(0, groups * per, CHUNK):
@@ -231,10 +247,24 @@
         ),
         name="row",
     )(positions, own, row, queries, tab)
+    stat, mixed = pl.pallas_call(
+        middle_kernel,
+        out_shape=(
+            jax.ShapeDtypeStruct((8, heads * rows), jnp.float32),
+            jax.ShapeDtypeStruct((D, heads * rows), jnp.float32),
+        ),
+        in_specs=[VM] * 6,
+        out_specs=(VM,) * 2,
+        compiler_params=PARAMS,
+        cost_estimate=pl.CostEstimate(
+            flops=4 * heads * rows * 2 * rows * D, bytes_accessed=2 * 10**6, transcendentals=10**6
+        ),
+        name="across_two",
+    )(c1, c2, own, rq, stat, mixed)
     return pl.pallas_call(
         last_kernel,
         out_shape=jax.ShapeDtypeStruct((rows, heads * D), jnp.bfloat16),
-        in_specs=[VM] * 7,
+        in_specs=[VM] * 5,
         out_specs=HB,
         scratch_shapes=[
             pltpu.VMEM((rows, heads * D), jnp.bfloat16),
@@ -244,8 +274,8 @@
         cost_estimate=pl.CostEstimate(
             flops=4 * heads * rows * 3 * rows * D, bytes_accessed=3 * 10**6, transcendentals=10**6
         ),
-        name="across",
-    )(c1, c2, c3, own, rq, stat, mixed)
+        name="across_one",
+    )(c3, own, rq, stat, mixed)
 
 
 def solution(mesh):

time: 44.9 us -> 44.4 us (0.989)
  waiting for transfers between devices: 11.9 us -> 11.1 us
    ppermute x3, waiting for transfers between devices: 11.9 us -> 11.1 us  [across(): return lax.ppermute(own, AXES, pairs)]
    pallas_call x0 -> x1, Pallas kernels: none -> 0.85 us  [local(): pl.pallas_call(middle_kernel, out_shape=(jax.ShapeDtypeStruct((8, heads *...]
    pallas_call x1, Pallas kernels: 1.95 us -> 1.5 us  [local(): pl.pallas_call(last_kernel, out_shape=jax.ShapeDtypeStruct((rows, heads *...]
  transfers between devices with their start and end apart: 3 -> 3, of which waited for: 3 -> 3; matrix products, arithmetic and copies ran while one was open for 0% -> 0% of each run, Pallas kernels for 4% -> 6%
where the time goes in v8:
time: 44.4 us; the launch traced here: 44.2 us
  blocking collectives  21.3 us (48%)
  waiting for transfers between devices  11.1 us (25%)
  Pallas kernels  5.78 us (13%)
  starting transfers between devices  4.01 us (9%)
  between operations  2.02 us (5%)
    all_gather x1, blocking collectives, local(): row = lax.all_gather(own, AXES, axis_index_groups=line)  21.3 us
    ppermute x3, waiting for transfers between devices, across(): return lax.ppermute(own, AXES, pairs)  11.1 us
    ppermute x3, starting transfers between devices, across(): return lax.ppermute(own, AXES, pairs)  4.01 us
    pallas_call x1, Pallas kernels, local(): pl.pallas_call(pack_kernel, out_shape=packed, in_specs=[SM] * 3 + [HB] *...  1.85 us
    pallas_call x1, Pallas kernels, local(): pl.pallas_call(first_kernel, out_shape=(jax.ShapeDtypeStruct((heads * row...  1.58 us
    pallas_call x1, Pallas kernels, local(): pl.pallas_call(last_kernel, out_shape=jax.ShapeDtypeStruct((rows, heads *...  1.5 us
  transfers between devices with their start and end apart: 3, of which 3 were waited for; matrix products, arithmetic and copies ran while one was open for 0% of the time, Pallas kernels for 6%

profile of v8, /device:TPU:24, one launch (start us, length us, event | category | flops | bytes accessed | tf_op | source)
XLA Modules:
  0.0 44.2 jit_solution(16721743031677333544)
XLA Ops:
  1.9 1.8 %pack.1.own = bf16[264,256]{1,0:T(8,128)(2,1)} custom-call(s32[1,1]{1,0:T(1,128)S(6)} %copy.9.stretch, s32[1,1]{1,0:T(1,128)S(6)} %copy.10.clean, s32[1,1]{1,0:T(1,128)S(6)} %copy.11.pos, bf16[128,256]{1,0:T(8,128)(2,1)} %k_hbm.1, bf16[128,256]{1,0:T(8,128)(2,1)} %v_hbm.1, f32[1,256]{1,0:T(1,128)} %bitcast.3, f32[2,144,128]{2,1,0:T(8,128)} %constant.2.clone.tab_hbm.tab), custom_call_target="tpu_custom_call" | custom-call | flops 1000000 | bytes 400000 | tf_op jit(solution)/shard_map/pack/pallas_call | solution.py:207
  3.8 0.0 copy-start
  3.8 0.0 copy-start.1
  3.8 0.0 copy-start.2
  3.8 1.4 %collective-permute-start.1 = (bf16[264,256]{1,0:T(8,128)(2,1)}, bf16[264,256]{1,0:T(8,128)(2,1)S(1)}, u32[]{:S(2)}, u32[]{:S(2)}) collective-permute-start(bf16[264,256]{1,0:T(8,128)(2,1)} %pack.1.own), channel_id=1, source_target_pairs={{4,1},{5,3},{2,4},{8,5},{3,6},{9,7},{6,8},{12,9},{7,10},{13,11},{1... | collective-permute-start | bytes 405512 | tf_op jit(solution)/shard_map/ppermute | solution.py:230
  5.3 1.3 %collective-permute-start.2 = (bf16[264,256]{1,0:T(8,128)(2,1)}, bf16[264,256]{1,0:T(8,128)(2,1)S(1)}, u32[]{:S(2)}, u32[]{:S(2)}) collective-permute-start(bf16[264,256]{1,0:T(8,128)(2,1)} %pack.1.own), channel_id=1, source_target_pairs={{4,2},{6,3},{1,4},{3,5},{8,6},{10,7},{5,8},{7,9},{12,10},{14,11},{... | collective-permute-start | bytes 405512 | tf_op jit(solution)/shard_map/ppermute | solution.py:230
  6.6 1.3 %collective-permute-start = (bf16[264,256]{1,0:T(8,128)(2,1)}, bf16[264,256]{1,0:T(8,128)(2,1)S(1)}, u32[]{:S(2)}, u32[]{:S(2)}) collective-permute-start(bf16[264,256]{1,0:T(8,128)(2,1)} %pack.1.own), channel_id=1, source_target_pairs={{5,2},{4,3},{3,4},{2,5},{9,6},{8,7},{7,8},{6,9},{13,10},{12,11},{1... | collective-permute-start | bytes 405512 | tf_op jit(solution)/shard_map/ppermute | solution.py:230
  7.9 21.3 %all-gather = bf16[1056,256]{1,0:T(8,128)(2,1)S(1)} all-gather(bf16[264,256]{1,0:T(8,128)(2,1)} %pack.1.own), channel_id=2, replica_groups={{0,1,2,3},{4,5,6,7},{8,9,10,11},{12,13,14,15},{16,17,18,19},{20,21,22,2..., dimensions={0}, use_global_device_ids=true | all-gather | bytes 675840 | tf_op jit(solution)/shard_map/all_gather | solution.py:234
  29.2 0.0 copy-done
  29.2 0.0 copy-done.1
  29.2 0.0 copy-done.2
  29.2 1.6 %row.1 = (bf16[1536,128]{1,0:T(8,128)(2,1)S(1)}, f32[8,1536]{1,0:T(8,128)S(1)}, f32[128,1536]{1,0:T(8,128)S(1)}) custom-call(s32[1,1]{1,0:T(1,128)S(6)} %copy.11.pos, bf16[264,256]{1,0:T(8,128)(2,1)S(1)} %copy-done, bf16[4,264,256]{2,1,0:T(8,128)(2,1)S(1)} %bitcast.2, bf16[128,1536]{1,0:T(8,128)(2,1)S(1)} %copy-done.2, f32[2,144,128]{2,1,0:T(8,128)S(1)} %copy-done.1), custom_call_target="tpu_custom_call" | custom-call | flops 402653184 | bytes 3000000 | tf_op jit(solution)/shard_map/row/pallas_call | solution.py:235
  30.8 6.7 %collective-permute-done.1.c1 = bf16[264,256]{1,0:T(8,128)(2,1)S(1)} collective-permute-done((bf16[264,256]{1,0:T(8,128)(2,1)}, bf16[264,256]{1,0:T(8,128)(2,1)S(1)}, u32[]{:S(2)}, u32[]{:S(2)}) %collective-permute-start.1) | collective-permute-done | bytes 135200 | tf_op jit(solution)/shard_map/ppermute | solution.py:230
  37.5 3.4 %collective-permute-done.2.c2 = bf16[264,256]{1,0:T(8,128)(2,1)S(1)} collective-permute-done((bf16[264,256]{1,0:T(8,128)(2,1)}, bf16[264,256]{1,0:T(8,128)(2,1)S(1)}, u32[]{:S(2)}, u32[]{:S(2)}) %collective-permute-start.2) | collective-permute-done | bytes 135200 | tf_op jit(solution)/shard_map/ppermute | solution.py:230
  40.9 0.8 %across_two.1 = (f32[8,1536]{1,0:T(8,128)S(1)}, f32[128,1536]{1,0:T(8,128)S(1)}) custom-call(bf16[264,256]{1,0:T(8,128)(2,1)S(1)} %collective-permute-done.1.c1, bf16[264,256]{1,0:T(8,128)(2,1)S(1)} %collective-permute-done.2.c2, bf16[264,256]{1,0:T(8,128)(2,1)S(1)} %copy-done, bf16[1536,128]{1,0:T(8,128)(2,1)S(1)} %get-tuple-element.10.rq, ...), custom_call_target="tpu_custom_call" | custom-call | flops 201326592 | bytes 2000000 | tf_op jit(solution)/shard_map/across_two/pallas_call | solution.py:250
  41.8 0.9 %collective-permute-done.c3 = bf16[264,256]{1,0:T(8,128)(2,1)S(1)} collective-permute-done((bf16[264,256]{1,0:T(8,128)(2,1)}, bf16[264,256]{1,0:T(8,128)(2,1)S(1)}, u32[]{:S(2)}, u32[]{:S(2)}) %collective-permute-start) | collective-permute-done | bytes 135200 | tf_op jit(solution)/shard_map/ppermute | solution.py:230
  42.7 1.5 %across_one.1 = bf16[128,1536]{1,0:T(8,128)(2,1)} custom-call(bf16[264,256]{1,0:T(8,128)(2,1)S(1)} %collective-permute-done.c3, bf16[264,256]{1,0:T(8,128)(2,1)S(1)} %copy-done, bf16[1536,128]{1,0:T(8,128)(2,1)S(1)} %get-tuple-element.10.rq, f32[8,1536]{1,0:T(8,128)S(1)} %get-tuple-element.13.stat, f32[128,1536]{1,0:T(8,128)S(1)} %get-tuple-element.14.mixed_in), custom_call_target="tpu_custom_call" | custom-call | flops 301989888 | bytes 3000000 | tf_op jit(solution)/shard_map/across_one/pallas_call | solution.py:264
Async XLA Ops:
  3.8 25.4 %copy-start = (bf16[264,256]{1,0:T(8,128)(2,1)S(1)}, bf16[264,256]{1,0:T(8,128)(2,1)}, u32[]{:S(2)}) copy-start(bf16[264,256]{1,0:T(8,128)(2,1)} %pack.1.own) | copy-start | bytes 405508
  3.8 25.4 %copy-start.1 = (f32[2,144,128]{2,1,0:T(8,128)S(1)}, f32[2,144,128]{2,1,0:T(8,128)}, u32[]{:S(2)}) copy-start(f32[2,144,128]{2,1,0:T(8,128)} %constant.2.clone.tab_hbm.tab) | copy-start | bytes 442372
  3.8 25.4 %copy-start.2 = (bf16[128,1536]{1,0:T(8,128)(2,1)S(1)}, bf16[128,1536]{1,0:T(8,128)(2,1)}, u32[]{:S(2)}) copy-start(bf16[128,1536]{1,0:T(8,128)(2,1)} %q.1) | copy-start | bytes 1179652
  3.8 33.7 %collective-permute-start.1 = (bf16[264,256]{1,0:T(8,128)(2,1)}, bf16[264,256]{1,0:T(8,128)(2,1)S(1)}, u32[]{:S(2)}, u32[]{:S(2)}) collective-permute-start(bf16[264,256]{1,0:T(8,128)(2,1)} %pack.1.own), channel_id=1, source_target_pairs={{4,1},{5,3},{2,4},{8,5},{3,6},{9,7},{6,8},{12,9},{7,10},{13,11},{1... | collective-permute-start | bytes 405512 | tf_op jit(solution)/shard_map/ppermute | solution.py:230
  5.3 35.6 %collective-permute-start.2 = (bf16[264,256]{1,0:T(8,128)(2,1)}, bf16[264,256]{1,0:T(8,128)(2,1)S(1)}, u32[]{:S(2)}, u32[]{:S(2)}) collective-permute-start(bf16[264,256]{1,0:T(8,128)(2,1)} %pack.1.own), channel_id=1, source_target_pairs={{4,2},{6,3},{1,4},{3,5},{8,6},{10,7},{5,8},{7,9},{12,10},{14,11},{... | collective-permute-start | bytes 405512 | tf_op jit(solution)/shard_map/ppermute | solution.py:230
  6.6 36.1 %collective-permute-start = (bf16[264,256]{1,0:T(8,128)(2,1)}, bf16[264,256]{1,0:T(8,128)(2,1)S(1)}, u32[]{:S(2)}, u32[]{:S(2)}) collective-permute-start(bf16[264,256]{1,0:T(8,128)(2,1)} %pack.1.own), channel_id=1, source_target_pairs={{5,2},{4,3},{3,4},{2,5},{9,6},{8,7},{7,8},{6,9},{13,10},{12,11},{1... | collective-permute-start | bytes 405512 | tf_op jit(solution)/shard_map/ppermute | solution.py:230

commit v9 on v8

--- a/solution.py
+++ b/solution.py
@@ -12,7 +12,7 @@
 D = 128
 WINDOW = 3
 ROW = WINDOW + 1
-SOURCES = ((2, 0, 3, 1), (1, 3, 0, 2), (3, 2, 1, 0))
+SOURCES = ((1, 3, 0, 2), (2, 0, 3, 1), (3, 2, 1, 0))
 CHUNK = 2
 ROPE_BASE = 10000.0
 NEG = -1e30

time: 44.4 us -> 44.7 us (level)
  transfers between devices with their start and end apart: 3 -> 3, of which waited for: 3 -> 2; matrix products, arithmetic and copies ran while one was open for 0% -> 0% of each run, Pallas kernels for 6% -> 5%
where the time goes in v9:
time: 44.7 us; the launch traced here: 44.4 us
  blocking collectives  21.5 us (48%)
  waiting for transfers between devices  11.1 us (25%)
  Pallas kernels  5.79 us (13%)
  starting transfers between devices  4.01 us (9%)
  between operations  2.03 us (5%)
    all_gather x1, blocking collectives, local(): row = lax.all_gather(own, AXES, axis_index_groups=line)  21.5 us
    ppermute x3, waiting for transfers between devices, across(): return lax.ppermute(own, AXES, pairs)  11.1 us
    ppermute x3, starting transfers between devices, across(): return lax.ppermute(own, AXES, pairs)  4.01 us
    pallas_call x1, Pallas kernels, local(): pl.pallas_call(pack_kernel, out_shape=packed, in_specs=[SM] * 3 + [HB] *...  1.85 us
    pallas_call x1, Pallas kernels, local(): pl.pallas_call(first_kernel, out_shape=(jax.ShapeDtypeStruct((heads * row...  1.58 us
    pallas_call x1, Pallas kernels, local(): pl.pallas_call(last_kernel, out_shape=jax.ShapeDtypeStruct((rows, heads *...  1.51 us
  transfers between devices with their start and end apart: 3, of which 2 were waited for; matrix products, arithmetic and copies ran while one was open for 0% of the time, Pallas kernels for 5%

profile of v9, /device:TPU:24, one launch (start us, length us, event | category | flops | bytes accessed | tf_op | source)
XLA Modules:
  0.0 44.4 jit_solution(6912212358117204167)
XLA Ops:
  1.9 1.8 %pack.1.own = bf16[264,256]{1,0:T(8,128)(2,1)} custom-call(s32[1,1]{1,0:T(1,128)S(6)} %copy.9.stretch, s32[1,1]{1,0:T(1,128)S(6)} %copy.10.clean, s32[1,1]{1,0:T(1,128)S(6)} %copy.11.pos, bf16[128,256]{1,0:T(8,128)(2,1)} %k_hbm.1, bf16[128,256]{1,0:T(8,128)(2,1)} %v_hbm.1, f32[1,256]{1,0:T(1,128)} %bitcast.3, f32[2,144,128]{2,1,0:T(8,128)} %constant.2.clone.tab_hbm.tab), custom_call_target="tpu_custom_call" | custom-call | flops 1000000 | bytes 400000 | tf_op jit(solution)/shard_map/pack/pallas_call | solution.py:207
  3.8 0.0 copy-start
  3.8 0.0 copy-start.1
  3.8 0.0 copy-start.2
  3.8 1.4 %collective-permute-start.1 = (bf16[264,256]{1,0:T(8,128)(2,1)}, bf16[264,256]{1,0:T(8,128)(2,1)S(1)}, u32[]{:S(2)}, u32[]{:S(2)}) collective-permute-start(bf16[264,256]{1,0:T(8,128)(2,1)} %pack.1.own), channel_id=1, source_target_pairs={{4,2},{6,3},{1,4},{3,5},{8,6},{10,7},{5,8},{7,9},{12,10},{14,11},{... | collective-permute-start | bytes 405512 | tf_op jit(solution)/shard_map/ppermute | solution.py:230
  5.3 1.3 %collective-permute-start.2 = (bf16[264,256]{1,0:T(8,128)(2,1)}, bf16[264,256]{1,0:T(8,128)(2,1)S(1)}, u32[]{:S(2)}, u32[]{:S(2)}) collective-permute-start(bf16[264,256]{1,0:T(8,128)(2,1)} %pack.1.own), channel_id=1, source_target_pairs={{4,1},{5,3},{2,4},{8,5},{3,6},{9,7},{6,8},{12,9},{7,10},{13,11},{1... | collective-permute-start | bytes 405512 | tf_op jit(solution)/shard_map/ppermute | solution.py:230
  6.6 1.3 %collective-permute-start = (bf16[264,256]{1,0:T(8,128)(2,1)}, bf16[264,256]{1,0:T(8,128)(2,1)S(1)}, u32[]{:S(2)}, u32[]{:S(2)}) collective-permute-start(bf16[264,256]{1,0:T(8,128)(2,1)} %pack.1.own), channel_id=1, source_target_pairs={{5,2},{4,3},{3,4},{2,5},{9,6},{8,7},{7,8},{6,9},{13,10},{12,11},{1... | collective-permute-start | bytes 405512 | tf_op jit(solution)/shard_map/ppermute | solution.py:230
  7.9 21.5 %all-gather = bf16[1056,256]{1,0:T(8,128)(2,1)S(1)} all-gather(bf16[264,256]{1,0:T(8,128)(2,1)} %pack.1.own), channel_id=2, replica_groups={{0,1,2,3},{4,5,6,7},{8,9,10,11},{12,13,14,15},{16,17,18,19},{20,21,22,2..., dimensions={0}, use_global_device_ids=true | all-gather | bytes 675840 | tf_op jit(solution)/shard_map/all_gather | solution.py:234
  29.4 0.0 copy-done
  29.4 0.0 copy-done.1
  29.4 0.0 copy-done.2
  29.4 1.6 %row.1 = (bf16[1536,128]{1,0:T(8,128)(2,1)S(1)}, f32[8,1536]{1,0:T(8,128)S(1)}, f32[128,1536]{1,0:T(8,128)S(1)}) custom-call(s32[1,1]{1,0:T(1,128)S(6)} %copy.11.pos, bf16[264,256]{1,0:T(8,128)(2,1)S(1)} %copy-done, bf16[4,264,256]{2,1,0:T(8,128)(2,1)S(1)} %bitcast.2, bf16[128,1536]{1,0:T(8,128)(2,1)S(1)} %copy-done.2, f32[2,144,128]{2,1,0:T(8,128)S(1)} %copy-done.1), custom_call_target="tpu_custom_call" | custom-call | flops 402653184 | bytes 3000000 | tf_op jit(solution)/shard_map/row/pallas_call | solution.py:235
  31.0 4.4 %collective-permute-done.1.c1 = bf16[264,256]{1,0:T(8,128)(2,1)S(1)} collective-permute-done((bf16[264,256]{1,0:T(8,128)(2,1)}, bf16[264,256]{1,0:T(8,128)(2,1)S(1)}, u32[]{:S(2)}, u32[]{:S(2)}) %collective-permute-start.1) | collective-permute-done | bytes 135200 | tf_op jit(solution)/shard_map/ppermute | solution.py:230
  35.4 6.7 %collective-permute-done.2.c2 = bf16[264,256]{1,0:T(8,128)(2,1)S(1)} collective-permute-done((bf16[264,256]{1,0:T(8,128)(2,1)}, bf16[264,256]{1,0:T(8,128)(2,1)S(1)}, u32[]{:S(2)}, u32[]{:S(2)}) %collective-permute-start.2) | collective-permute-done | bytes 135200 | tf_op jit(solution)/shard_map/ppermute | solution.py:230
  42.1 0.8 %across_two.1 = (f32[8,1536]{1,0:T(8,128)S(1)}, f32[128,1536]{1,0:T(8,128)S(1)}) custom-call(bf16[264,256]{1,0:T(8,128)(2,1)S(1)} %collective-permute-done.1.c1, bf16[264,256]{1,0:T(8,128)(2,1)S(1)} %collective-permute-done.2.c2, bf16[264,256]{1,0:T(8,128)(2,1)S(1)} %copy-done, bf16[1536,128]{1,0:T(8,128)(2,1)S(1)} %get-tuple-element.10.rq, ...), custom_call_target="tpu_custom_call" | custom-call | flops 201326592 | bytes 2000000 | tf_op jit(solution)/shard_map/across_two/pallas_call | solution.py:250
  42.9 0.0 collective-permute-done.c3
  42.9 1.5 %across_one.1 = bf16[128,1536]{1,0:T(8,128)(2,1)} custom-call(bf16[264,256]{1,0:T(8,128)(2,1)S(1)} %collective-permute-done.c3, bf16[264,256]{1,0:T(8,128)(2,1)S(1)} %copy-done, bf16[1536,128]{1,0:T(8,128)(2,1)S(1)} %get-tuple-element.10.rq, f32[8,1536]{1,0:T(8,128)S(1)} %get-tuple-element.13.stat, f32[128,1536]{1,0:T(8,128)S(1)} %get-tuple-element.14.mixed_in), custom_call_target="tpu_custom_call" | custom-call | flops 301989888 | bytes 3000000 | tf_op jit(solution)/shard_map/across_one/pallas_call | solution.py:264
Async XLA Ops:
  3.8 25.6 %copy-start = (bf16[264,256]{1,0:T(8,128)(2,1)S(1)}, bf16[264,256]{1,0:T(8,128)(2,1)}, u32[]{:S(2)}) copy-start(bf16[264,256]{1,0:T(8,128)(2,1)} %pack.1.own) | copy-start | bytes 405508
  3.8 25.6 %copy-start.1 = (f32[2,144,128]{2,1,0:T(8,128)S(1)}, f32[2,144,128]{2,1,0:T(8,128)}, u32[]{:S(2)}) copy-start(f32[2,144,128]{2,1,0:T(8,128)} %constant.2.clone.tab_hbm.tab) | copy-start | bytes 442372
  3.8 25.6 %copy-start.2 = (bf16[128,1536]{1,0:T(8,128)(2,1)S(1)}, bf16[128,1536]{1,0:T(8,128)(2,1)}, u32[]{:S(2)}) copy-start(bf16[128,1536]{1,0:T(8,128)(2,1)} %q.1) | copy-start | bytes 1179652
  3.8 31.5 %collective-permute-start.1 = (bf16[264,256]{1,0:T(8,128)(2,1)}, bf16[264,256]{1,0:T(8,128)(2,1)S(1)}, u32[]{:S(2)}, u32[]{:S(2)}) collective-permute-start(bf16[264,256]{1,0:T(8,128)(2,1)} %pack.1.own), channel_id=1, source_target_pairs={{4,2},{6,3},{1,4},{3,5},{8,6},{10,7},{5,8},{7,9},{12,10},{14,11},{... | collective-permute-start | bytes 405512 | tf_op jit(solution)/shard_map/ppermute | solution.py:230
  5.3 36.8 %collective-permute-start.2 = (bf16[264,256]{1,0:T(8,128)(2,1)}, bf16[264,256]{1,0:T(8,128)(2,1)S(1)}, u32[]{:S(2)}, u32[]{:S(2)}) collective-permute-start(bf16[264,256]{1,0:T(8,128)(2,1)} %pack.1.own), channel_id=1, source_target_pairs={{4,1},{5,3},{2,4},{8,5},{3,6},{9,7},{6,8},{12,9},{7,10},{13,11},{1... | collective-permute-start | bytes 405512 | tf_op jit(solution)/shard_map/ppermute | solution.py:230
  6.6 36.4 %collective-permute-start = (bf16[264,256]{1,0:T(8,128)(2,1)}, bf16[264,256]{1,0:T(8,128)(2,1)S(1)}, u32[]{:S(2)}, u32[]{:S(2)}) collective-permute-start(bf16[264,256]{1,0:T(8,128)(2,1)} %pack.1.own), channel_id=1, source_target_pairs={{5,2},{4,3},{3,4},{2,5},{9,6},{8,7},{7,8},{6,9},{13,10},{12,11},{1... | collective-permute-start | bytes 405512 | tf_op jit(solution)/shard_map/ppermute | solution.py:230

commit v10 on v9

--- a/solution.py
+++ b/solution.py
@@ -147,11 +147,11 @@
         mixed_out[:, cols] = mixed
 
 
-def middle_kernel(c1, c2, own, rq, stat, mixed_in, stat_out, mixed_out):
+def middle_kernel(c1, own, rq, stat, mixed_in, stat_out, mixed_out):
     groups = own.shape[1] // D
     rows = mixed_in.shape[0]
     per = rq.shape[0] // rows // groups
-    blocks = (c1, c2)
+    blocks = (c1,)
     bias = hidden_by(labels(own), blocks)
     for head in range(0, groups * per, CHUNK):
         at = pl.ds(head * rows, CHUNK * rows)
@@ -163,11 +163,11 @@
         mixed_out[:, at] = mixed_in[:, at] * kept + mixed
 
 
-def last_kernel(c3, own, rq, stat, mixed_in, out_hbm, out, sems):
+def last_kernel(c2, c3, own, rq, stat, mixed_in, out_hbm, out, sems):
     rows = out.shape[0]
     groups = own.shape[1] // D
     per = rq.shape[0] // rows // groups
-    blocks = (c3,)
+    blocks = (c2, c3)
     bias = hidden_by(labels(own), blocks)
     moves = []
     for head in range(0, groups * per, CHUNK):
@@ -253,18 +253,18 @@
             jax.ShapeDtypeStruct((8, heads * rows), jnp.float32),
             jax.ShapeDtypeStruct((D, heads * rows), jnp.float32),
         ),
-        in_specs=[VM] * 6,
+        in_specs=[VM] * 5,
         out_specs=(VM,) * 2,
         compiler_params=PARAMS,
         cost_estimate=pl.CostEstimate(
-            flops=4 * heads * rows * 2 * rows * D, bytes_accessed=2 * 10**6, transcendentals=10**6
-        ),
-        name="across_two",
-    )(c1, c2, own, rq, stat, mixed)
+            flops=4 * heads * rows * rows * D, bytes_accessed=2 * 10**6, transcendentals=10**6
+        ),
+        name="across_first",
+    )(c1, own, rq, stat, mixed)
     return pl.pallas_call(
         last_kernel,
         out_shape=jax.ShapeDtypeStruct((rows, heads * D), jnp.bfloat16),
-        in_specs=[VM] * 5,
+        in_specs=[VM] * 6,
         out_specs=HB,
         scratch_shapes=[
             pltpu.VMEM((rows, heads * D), jnp.bfloat16),
@@ -272,10 +272,10 @@
         ],
         compiler_params=PARAMS,
         cost_estimate=pl.CostEstimate(
-            flops=4 * heads * rows * 3 * rows * D, bytes_accessed=3 * 10**6, transcendentals=10**6
-        ),
-        name="across_one",
-    )(c3, own, rq, stat, mixed)
+            flops=4 * heads * rows * 2 * rows * D, bytes_accessed=3 * 10**6, transcendentals=10**6
+        ),
+        name="across_rest",
+    )(c2, c3, own, rq, stat, mixed)
 
 
 def solution(mesh):

time: 44.7 us -> 44.8 us (level)
  transfers between devices with their start and end apart: 3 -> 3, of which waited for: 2 -> 3; matrix products, arithmetic and copies ran while one was open for 0% -> 0% of each run, Pallas kernels for 5% -> 5%
where the time goes in v10:
time: 44.8 us; the launch traced here: 44.6 us
  blocking collectives  21.5 us (48%)
  waiting for transfers between devices  11.1 us (25%)
  Pallas kernels  5.81 us (13%)
  starting transfers between devices  4.01 us (9%)
  between operations  2.02 us (5%)
    all_gather x1, blocking collectives, local(): row = lax.all_gather(own, AXES, axis_index_groups=line)  21.5 us
    ppermute x3, waiting for transfers between devices, across(): return lax.ppermute(own, AXES, pairs)  11.1 us
    ppermute x3, starting transfers between devices, across(): return lax.ppermute(own, AXES, pairs)  4.01 us
    pallas_call x1, Pallas kernels, local(): pl.pallas_call(pack_kernel, out_shape=packed, in_specs=[SM] * 3 + [HB] *...  1.85 us
    pallas_call x1, Pallas kernels, local(): pl.pallas_call(last_kernel, out_shape=jax.ShapeDtypeStruct((rows, heads *...  1.64 us
    pallas_call x1, Pallas kernels, local(): pl.pallas_call(first_kernel, out_shape=(jax.ShapeDtypeStruct((heads * row...  1.59 us
  transfers between devices with their start and end apart: 3, of which 3 were waited for; matrix products, arithmetic and copies ran while one was open for 0% of the time, Pallas kernels for 5%

profile of v10, /device:TPU:24, one launch (start us, length us, event | category | flops | bytes accessed | tf_op | source)
XLA Modules:
  0.0 44.6 jit_solution(5258679539746148980)
XLA Ops:
  1.9 1.8 %pack.1.own = bf16[264,256]{1,0:T(8,128)(2,1)} custom-call(s32[1,1]{1,0:T(1,128)S(6)} %copy.9.stretch, s32[1,1]{1,0:T(1,128)S(6)} %copy.10.clean, s32[1,1]{1,0:T(1,128)S(6)} %copy.11.pos, bf16[128,256]{1,0:T(8,128)(2,1)} %k_hbm.1, bf16[128,256]{1,0:T(8,128)(2,1)} %v_hbm.1, f32[1,256]{1,0:T(1,128)} %bitcast.3, f32[2,144,128]{2,1,0:T(8,128)} %constant.2.clone.tab_hbm.tab), custom_call_target="tpu_custom_call" | custom-call | flops 1000000 | bytes 400000 | tf_op jit(solution)/shard_map/pack/pallas_call | solution.py:207
  3.8 0.0 copy-start
  3.8 0.0 copy-start.1
  3.8 0.0 copy-start.2
  3.8 1.4 %collective-permute-start.2 = (bf16[264,256]{1,0:T(8,128)(2,1)}, bf16[264,256]{1,0:T(8,128)(2,1)S(1)}, u32[]{:S(2)}, u32[]{:S(2)}) collective-permute-start(bf16[264,256]{1,0:T(8,128)(2,1)} %pack.1.own), channel_id=1, source_target_pairs={{4,2},{6,3},{1,4},{3,5},{8,6},{10,7},{5,8},{7,9},{12,10},{14,11},{... | collective-permute-start | bytes 405512 | tf_op jit(solution)/shard_map/ppermute | solution.py:230
  5.3 1.3 %collective-permute-start = (bf16[264,256]{1,0:T(8,128)(2,1)}, bf16[264,256]{1,0:T(8,128)(2,1)S(1)}, u32[]{:S(2)}, u32[]{:S(2)}) collective-permute-start(bf16[264,256]{1,0:T(8,128)(2,1)} %pack.1.own), channel_id=1, source_target_pairs={{4,1},{5,3},{2,4},{8,5},{3,6},{9,7},{6,8},{12,9},{7,10},{13,11},{1... | collective-permute-start | bytes 405512 | tf_op jit(solution)/shard_map/ppermute | solution.py:230
  6.6 1.3 %collective-permute-start.1 = (bf16[264,256]{1,0:T(8,128)(2,1)}, bf16[264,256]{1,0:T(8,128)(2,1)S(1)}, u32[]{:S(2)}, u32[]{:S(2)}) collective-permute-start(bf16[264,256]{1,0:T(8,128)(2,1)} %pack.1.own), channel_id=1, source_target_pairs={{5,2},{4,3},{3,4},{2,5},{9,6},{8,7},{7,8},{6,9},{13,10},{12,11},{1... | collective-permute-start | bytes 405512 | tf_op jit(solution)/shard_map/ppermute | solution.py:230
  7.9 21.5 %all-gather = bf16[1056,256]{1,0:T(8,128)(2,1)S(1)} all-gather(bf16[264,256]{1,0:T(8,128)(2,1)} %pack.1.own), channel_id=2, replica_groups={{0,1,2,3},{4,5,6,7},{8,9,10,11},{12,13,14,15},{16,17,18,19},{20,21,22,2..., dimensions={0}, use_global_device_ids=true | all-gather | bytes 675840 | tf_op jit(solution)/shard_map/all_gather | solution.py:234
  29.4 0.0 copy-done
  29.4 0.0 copy-done.1
  29.4 0.0 copy-done.2
  29.4 1.6 %row.1 = (bf16[1536,128]{1,0:T(8,128)(2,1)S(1)}, f32[8,1536]{1,0:T(8,128)S(1)}, f32[128,1536]{1,0:T(8,128)S(1)}) custom-call(s32[1,1]{1,0:T(1,128)S(6)} %copy.11.pos, bf16[264,256]{1,0:T(8,128)(2,1)S(1)} %copy-done, bf16[4,264,256]{2,1,0:T(8,128)(2,1)S(1)} %bitcast.2, bf16[128,1536]{1,0:T(8,128)(2,1)S(1)} %copy-done.2, f32[2,144,128]{2,1,0:T(8,128)S(1)} %copy-done.1), custom_call_target="tpu_custom_call" | custom-call | flops 402653184 | bytes 3000000 | tf_op jit(solution)/shard_map/row/pallas_call | solution.py:235
  31.0 4.4 %collective-permute-done.2.c1 = bf16[264,256]{1,0:T(8,128)(2,1)S(1)} collective-permute-done((bf16[264,256]{1,0:T(8,128)(2,1)}, bf16[264,256]{1,0:T(8,128)(2,1)S(1)}, u32[]{:S(2)}, u32[]{:S(2)}) %collective-permute-start.2) | collective-permute-done | bytes 135200 | tf_op jit(solution)/shard_map/ppermute | solution.py:230
  35.4 0.7 %across_first.1 = (f32[8,1536]{1,0:T(8,128)S(1)}, f32[128,1536]{1,0:T(8,128)S(1)}) custom-call(bf16[264,256]{1,0:T(8,128)(2,1)S(1)} %collective-permute-done.2.c1, bf16[264,256]{1,0:T(8,128)(2,1)S(1)} %copy-done, bf16[1536,128]{1,0:T(8,128)(2,1)S(1)} %get-tuple-element.10.rq, f32[8,1536]{1,0:T(8,128)S(1)} %get-tuple-element.11.stat, ...), custom_call_target="tpu_custom_call" | custom-call | flops 100663296 | bytes 2000000 | tf_op jit(solution)/shard_map/across_first/pallas_call | solution.py:250
  36.1 6.0 %collective-permute-done.c2 = bf16[264,256]{1,0:T(8,128)(2,1)S(1)} collective-permute-done((bf16[264,256]{1,0:T(8,128)(2,1)}, bf16[264,256]{1,0:T(8,128)(2,1)S(1)}, u32[]{:S(2)}, u32[]{:S(2)}) %collective-permute-start) | collective-permute-done | bytes 135200 | tf_op jit(solution)/shard_map/ppermute | solution.py:230
  42.1 0.8 %collective-permute-done.1.c3 = bf16[264,256]{1,0:T(8,128)(2,1)S(1)} collective-permute-done((bf16[264,256]{1,0:T(8,128)(2,1)}, bf16[264,256]{1,0:T(8,128)(2,1)S(1)}, u32[]{:S(2)}, u32[]{:S(2)}) %collective-permute-start.1) | collective-permute-done | bytes 135200 | tf_op jit(solution)/shard_map/ppermute | solution.py:230
  42.9 1.6 %across_rest.1 = bf16[128,1536]{1,0:T(8,128)(2,1)} custom-call(bf16[264,256]{1,0:T(8,128)(2,1)S(1)} %collective-permute-done.c2, bf16[264,256]{1,0:T(8,128)(2,1)S(1)} %collective-permute-done.1.c3, bf16[264,256]{1,0:T(8,128)(2,1)S(1)} %copy-done, bf16[1536,128]{1,0:T(8,128)(2,1)S(1)} %get-tuple-element.10.rq, f32[8,1536]{1,0:T(8,128)S(1)} %get-tuple-element.13.stat, ...), custom_call_target="tpu_custom_call" | custom-call | flops 201326592 | bytes 3000000 | tf_op jit(solution)/shard_map/across_rest/pallas_call | solution.py:264
Async XLA Ops:
  3.8 25.6 %copy-start = (bf16[264,256]{1,0:T(8,128)(2,1)S(1)}, bf16[264,256]{1,0:T(8,128)(2,1)}, u32[]{:S(2)}) copy-start(bf16[264,256]{1,0:T(8,128)(2,1)} %pack.1.own) | copy-start | bytes 405508
  3.8 25.6 %copy-start.1 = (f32[2,144,128]{2,1,0:T(8,128)S(1)}, f32[2,144,128]{2,1,0:T(8,128)}, u32[]{:S(2)}) copy-start(f32[2,144,128]{2,1,0:T(8,128)} %constant.2.clone.tab_hbm.tab) | copy-start | bytes 442372
  3.8 25.6 %copy-start.2 = (bf16[128,1536]{1,0:T(8,128)(2,1)S(1)}, bf16[128,1536]{1,0:T(8,128)(2,1)}, u32[]{:S(2)}) copy-start(bf16[128,1536]{1,0:T(8,128)(2,1)} %q.1) | copy-start | bytes 1179652
  3.8 31.5 %collective-permute-start.2 = (bf16[264,256]{1,0:T(8,128)(2,1)}, bf16[264,256]{1,0:T(8,128)(2,1)S(1)}, u32[]{:S(2)}, u32[]{:S(2)}) collective-permute-start(bf16[264,256]{1,0:T(8,128)(2,1)} %pack.1.own), channel_id=1, source_target_pairs={{4,2},{6,3},{1,4},{3,5},{8,6},{10,7},{5,8},{7,9},{12,10},{14,11},{... | collective-permute-start | bytes 405512 | tf_op jit(solution)/shard_map/ppermute | solution.py:230
  5.3 36.8 %collective-permute-start = (bf16[264,256]{1,0:T(8,128)(2,1)}, bf16[264,256]{1,0:T(8,128)(2,1)S(1)}, u32[]{:S(2)}, u32[]{:S(2)}) collective-permute-start(bf16[264,256]{1,0:T(8,128)(2,1)} %pack.1.own), channel_id=1, source_target_pairs={{4,1},{5,3},{2,4},{8,5},{3,6},{9,7},{6,8},{12,9},{7,10},{13,11},{1... | collective-permute-start | bytes 405512 | tf_op jit(solution)/shard_map/ppermute | solution.py:230
  6.6 36.3 %collective-permute-start.1 = (bf16[264,256]{1,0:T(8,128)(2,1)}, bf16[264,256]{1,0:T(8,128)(2,1)S(1)}, u32[]{:S(2)}, u32[]{:S(2)}) collective-permute-start(bf16[264,256]{1,0:T(8,128)(2,1)} %pack.1.own), channel_id=1, source_target_pairs={{5,2},{4,3},{3,4},{2,5},{9,6},{8,7},{7,8},{6,9},{13,10},{12,11},{1... | collective-permute-start | bytes 405512 | tf_op jit(solution)/shard_map/ppermute | solution.py:230
